TPU v7x, 32 devices: a whole 2x2x4 slice. The times are simulated.
32 devices in a mesh: shard: 2 (over x), ctx: 8 (over z, core), tp: 2 (over y).
Axes of the slice: x: 2, y: 2, z: 4, core: 2. Of those that a mesh axis runs over, the one named last changes fastest.
Arguments:
- tokens: bfloat16 [4, 4096, 768], P('shard', 'ctx'), may hold values from -6 to 6
- cotangent: bfloat16 [4, 4096, 768], P('shard', 'ctx'), may hold values from -6 to 6
- segment_ids: int32 [4, 4096], P('shard'), may hold values from 0 to 3, never falling along the last dimension, each value on 1 to 1920 neighbouring positions
- w_qkv: float32 [3, 768, 768], P(None, 'shard', 'tp'), may hold values from -0.21875 to 0.21875
- w_out: float32 [768, 768], P('tp', 'shard'), may hold values from -0.21875 to 0.21875
- w_fc1: float32 [768, 3072], P('shard', 'tp'), may hold values from -0.21875 to 0.21875
- w_fc2: float32 [3072, 768], P('tp', 'shard'), may hold values from -0.109375 to 0.109375
- norm_gain: float32 [2, 768], P(None, 'shard'), may hold values from 0.1 to 1.9
- norm_bias: float32 [4, 768], P(None, 'shard'), may hold values from -3 to 3
- head_gain: float32 [768], P('tp'), may hold values from 0.1 to 1.9
- head_bias: float32 [3, 768], P(None, 'tp'), may hold values from -3 to 3
- ffn_gain: float32 [3072], P('tp'), may hold values from 0.1 to 1.9
- ffn_bias: float32 [2, 3072], P(None, 'tp'), may hold values from -3 to 3
Outputs:
- out: bfloat16 [4, 4096, 768], P('shard', 'ctx')
- grad_tokens: bfloat16 [4, 4096, 768], P('shard', 'ctx')
- grad_w_qkv: float32 [3, 768, 768], P(None, ('shard', 'ctx'), 'tp')
- grad_w_out: float32 [768, 768], P('tp', ('shard', 'ctx'))
- grad_w_fc1: float32 [768, 3072], P(('shard', 'ctx'), 'tp')
- grad_w_fc2: float32 [3072, 768], P('tp', ('shard', 'ctx'))
- grad_norm_gain: float32 [2, 768], P(None, ('shard', 'ctx'))
- grad_norm_bias: float32 [4, 768], P(None, ('shard', 'ctx'))
- grad_head_gain: float32 [768], P('tp')
- grad_head_bias: float32 [3, 768], P(None, 'tp')
- grad_ffn_gain: float32 [3072], P('tp')
- grad_ffn_bias: float32 [2, 3072], P(None, 'tp')
Inputs may be any that keep to these rules, and one draw needn't show every extreme that they name: `segment_ids`: along each sequence the document number never falls; every document holds 1 to 1920 tokens and some document holds exactly 1920.
All inputs are finite; a program needn't handle non-finite values.
Results may differ from a plain program's by a relative error of at most 0.014.
Values may be sent and summed in bfloat16 or wider, within the bound.
A program may use at most 192 MiB of HBM per device.

v0:
```python
import jax
import jax.numpy as jnp
from jax import lax
from jax.sharding import PartitionSpec as P

HEAD_DIM = 64


EPS = 1e-05
NEGATIVE = -1e30


def layer_norm(values, gain, shift):
    row_mean = jnp.mean(values, -1, keepdims=True)
    centred = values - row_mean
    variance = jnp.mean(centred * centred, -1, keepdims=True)
    return centred * lax.rsqrt(variance + EPS) * gain + shift


def split_norm(values, gain, shift):
    total_sum, total_square = lax.psum(
        (jnp.sum(values, -1, keepdims=True), jnp.sum(values * values, -1, keepdims=True)), "tp"
    )
    full_width = values.shape[-1] * lax.axis_size("tp")
    row_mean = total_sum / full_width
    variance = total_square / full_width - row_mean * row_mean
    inv_std = lax.rsqrt(variance + EPS)
    normed = (values - row_mean) * inv_std
    return (normed * gain + shift, normed, inv_std)


def split_norm_back(upstream, normed, inv_std, gain):
    grad_gain = jnp.sum(upstream * normed, 0)
    grad_shift = jnp.sum(upstream, 0)
    scaled = upstream * gain
    first_sum, second_sum = lax.psum(
        (jnp.sum(scaled, -1, keepdims=True), jnp.sum(scaled * normed, -1, keepdims=True)), "tp"
    )
    full_width = upstream.shape[-1] * lax.axis_size("tp")
    return (
        inv_std * (scaled - first_sum / full_width - normed * second_sum / full_width),
        grad_gain,
        grad_shift,
    )


def tensor_sum(partial_part):
    return lax.psum(partial_part.astype(jnp.bfloat16), "tp").astype(jnp.float32)


def tensor_grad(partial_part):
    return lax.psum(partial_part.astype(jnp.bfloat16), "tp").astype(jnp.float32)


def per_device(
    tokens,
    cotangent,
    segment_ids,
    w_qkv,
    w_out,
    w_fc1,
    w_fc2,
    norm_gain,
    norm_bias,
    head_gain,
    head_bias,
    ffn_gain,
    ffn_bias,
):
    seqs_here, local_len, model_width = tokens.shape
    rows_here = seqs_here * local_len
    seq_length = segment_ids.shape[1]
    ctx_rank = lax.axis_index("ctx")
    gathered = (
        lax.all_gather(w_qkv.astype(jnp.bfloat16), "shard", axis=1, tiled=True),
        lax.all_gather(w_out.astype(jnp.bfloat16), "shard", axis=1, tiled=True),
        lax.all_gather(w_fc1.astype(jnp.bfloat16), "shard", axis=0, tiled=True),
        lax.all_gather(w_fc2.astype(jnp.bfloat16), "shard", axis=1, tiled=True),
        lax.all_gather(norm_gain.astype(jnp.bfloat16), "shard", axis=1, tiled=True),
        lax.all_gather(norm_bias.astype(jnp.bfloat16), "shard", axis=1, tiled=True),
    )
    qkv_low, out_low, up_low, down_low, gain_low, bias_low = gathered
    gains = gain_low.astype(jnp.float32)
    biases = bias_low.astype(jnp.float32)
    inputs = tokens.astype(jnp.float32).reshape(rows_here, model_width)
    normed_in, pull_in = jax.vjp(layer_norm, inputs, gains[0], biases[0])
    normed_low = normed_in.astype(jnp.bfloat16)
    projected = jnp.einsum("rd,kde->kre", normed_low, qkv_low, preferred_element_type=jnp.float32)
    local_width = projected.shape[2]
    query_low = (projected[0] + head_bias[0]).astype(jnp.bfloat16)
    key_low = projected[1].astype(jnp.bfloat16)
    value_low = (projected[2] + head_bias[1]).astype(jnp.bfloat16)
    own_keys = key_low.reshape(seqs_here, local_len, local_width)
    own_values = value_low.reshape(seqs_here, local_len, local_width)
    keys_all, values_all = (
        lax.all_gather(own_keys, "ctx", axis=1, tiled=True),
        lax.all_gather(own_values, "ctx", axis=1, tiled=True),
    )
    queries = query_low.reshape(seqs_here, local_len, local_width)
    query_pos = ctx_rank * local_len + jnp.arange(local_len, dtype=jnp.int32)
    key_pos = jnp.arange(seq_length, dtype=jnp.int32)
    query_seg = lax.dynamic_slice_in_dim(segment_ids, ctx_rank * local_len, local_len, 1)
    allowed = (query_seg[:, :, None] == segment_ids[:, None, :]) & (
        key_pos[None, None, :] <= query_pos[None, :, None]
    )
    head_count = local_width // HEAD_DIM

    def columns(array, head_index):
        return lax.dynamic_slice_in_dim(array, head_index * HEAD_DIM, HEAD_DIM, 2)

    def scores(head_index):
        raw = (
            jnp.einsum(
                "sqd,skd->sqk",
                columns(queries, head_index),
                columns(keys_all, head_index),
                preferred_element_type=jnp.float32,
            )
            * 0.125
        )
        return jnp.where(allowed, raw, NEGATIVE)

    def forward_head(head_index):
        masked = scores(head_index)
        peak = jnp.max(masked, -1, keepdims=True)
        expo = jnp.exp(masked - peak)
        denom = jnp.sum(expo, -1, keepdims=True)
        probs = (expo / denom).astype(jnp.bfloat16)
        mixed = jnp.einsum(
            "sqk,skd->sqd",
            probs,
            columns(values_all, head_index),
            preferred_element_type=jnp.float32,
        )
        return (mixed, peak, denom)

    mixed_heads, peaks, denoms = lax.map(forward_head, jnp.arange(head_count))
    attended = mixed_heads.transpose(1, 2, 0, 3).reshape(rows_here, local_width)
    sub_out, sub_normed, sub_scale = split_norm(attended, head_gain, head_bias[2])
    sub_low = sub_out.astype(jnp.bfloat16)
    residual = (
        inputs
        + tensor_sum(jnp.dot(sub_low, out_low, preferred_element_type=jnp.float32))
        + biases[2]
    )
    ffn_in, pull_fin = jax.vjp(layer_norm, residual, gains[1], biases[1])
    ffn_low = ffn_in.astype(jnp.bfloat16)
    hidden = jnp.dot(ffn_low, up_low, preferred_element_type=jnp.float32) + ffn_bias[0]
    active, pull_gelu = jax.vjp(jax.nn.gelu, hidden)
    inner_out, inner_normed, inner_scale = split_norm(active, ffn_gain, ffn_bias[1])
    inner_low = inner_out.astype(jnp.bfloat16)
    result = (
        residual
        + tensor_sum(jnp.dot(inner_low, down_low, preferred_element_type=jnp.float32))
        + biases[3]
    )
    qkv_low, out_low, up_low, down_low = (
        lax.all_gather(w_qkv.astype(jnp.bfloat16), "shard", axis=1, tiled=True),
        lax.all_gather(w_out.astype(jnp.bfloat16), "shard", axis=1, tiled=True),
        lax.all_gather(w_fc1.astype(jnp.bfloat16), "shard", axis=0, tiled=True),
        lax.all_gather(w_fc2.astype(jnp.bfloat16), "shard", axis=1, tiled=True),
    )
    upstream = cotangent.astype(jnp.float32).reshape(rows_here, model_width)
    upstream_low = cotangent.reshape(rows_here, model_width)
    grad_fc2_bias = jnp.sum(upstream, 0)
    grad_down = jnp.einsum("rf,rd->fd", inner_low, upstream_low, preferred_element_type=jnp.float32)
    inner_grad = jnp.einsum("rd,fd->rf", upstream_low, down_low, preferred_element_type=jnp.float32)
    active_grad, grad_ffn_gain, grad_inner_shift = split_norm_back(
        inner_grad, inner_normed, inner_scale, ffn_gain
    )
    hidden_grad = pull_gelu(active_grad)[0].astype(jnp.bfloat16)
    grad_up_bias = jnp.sum(hidden_grad.astype(jnp.float32), 0)
    grad_up = jnp.einsum("rd,rf->df", ffn_low, hidden_grad, preferred_element_type=jnp.float32)
    ffn_grad = tensor_grad(
        jnp.einsum("rf,df->rd", hidden_grad, up_low, preferred_element_type=jnp.float32)
    )
    residual_part, grad_gain_fin, grad_bias_fin = pull_fin(ffn_grad)
    residual_grad = upstream + residual_part
    branch_low = residual_grad.astype(jnp.bfloat16)
    grad_out_bias = jnp.sum(branch_low.astype(jnp.float32), 0)
    grad_outw = jnp.einsum("re,rd->ed", sub_low, branch_low, preferred_element_type=jnp.float32)
    sub_grad = jnp.einsum("rd,ed->re", branch_low, out_low, preferred_element_type=jnp.float32)
    attn_grad, grad_head_gain, grad_sub_shift = split_norm_back(
        sub_grad, sub_normed, sub_scale, head_gain
    )
    attn_low = attn_grad.astype(jnp.bfloat16).reshape(seqs_here, local_len, local_width)

    def merge_heads(stacked):
        return stacked.transpose(1, 2, 0, 3).reshape(
            stacked.shape[1], stacked.shape[2], local_width
        )

    def backward_head(pieces):
        head_index, peak, denom = pieces
        masked = scores(head_index)
        probs = jnp.exp(masked - peak) / denom
        grad_rows = columns(attn_low, head_index)
        prob_grad = jnp.einsum(
            "sqd,skd->sqk",
            grad_rows,
            columns(values_all, head_index),
            preferred_element_type=jnp.float32,
        )
        value_grad = jnp.einsum(
            "sqk,sqd->skd",
            probs.astype(jnp.bfloat16),
            grad_rows,
            preferred_element_type=jnp.float32,
        )
        weighted = jnp.sum(probs * prob_grad, -1, keepdims=True)
        score_grad = (probs * (prob_grad - weighted)).astype(jnp.bfloat16)
        query_grad = (
            jnp.einsum(
                "sqk,skd->sqd",
                score_grad,
                columns(keys_all, head_index),
                preferred_element_type=jnp.float32,
            )
            * 0.125
        )
        key_grad = (
            jnp.einsum(
                "sqk,sqd->skd",
                score_grad,
                columns(queries, head_index),
                preferred_element_type=jnp.float32,
            )
            * 0.125
        )
        return (query_grad, key_grad, value_grad)

    query_grads, key_grads, value_grads = lax.map(
        backward_head, (jnp.arange(head_count), peaks, denoms)
    )
    key_local, value_local = (
        lax.psum_scatter(
            merge_heads(key_grads).astype(jnp.bfloat16), "ctx", scatter_dimension=1, tiled=True
        ).astype(jnp.float32),
        lax.psum_scatter(
            merge_heads(value_grads).astype(jnp.bfloat16), "ctx", scatter_dimension=1, tiled=True
        ).astype(jnp.float32),
    )
    proj_grads = jnp.stack(
        [
            merge_heads(query_grads).reshape(rows_here, local_width),
            key_local.reshape(rows_here, local_width),
            value_local.reshape(rows_here, local_width),
        ]
    ).astype(jnp.bfloat16)
    grad_qkv = jnp.einsum("rd,kre->kde", normed_low, proj_grads, preferred_element_type=jnp.float32)
    grad_query_bias = jnp.sum(proj_grads[0].astype(jnp.float32), 0)
    grad_value_bias = jnp.sum(proj_grads[2].astype(jnp.float32), 0)
    input_part = tensor_grad(
        jnp.einsum("kre,kde->rd", proj_grads, qkv_low, preferred_element_type=jnp.float32)
    )
    token_part, grad_gain_in, grad_bias_in = pull_in(input_part)
    grad_tokens = (
        (residual_grad + token_part).astype(jnp.bfloat16).reshape(seqs_here, local_len, model_width)
    )
    gain_grads = jnp.stack([grad_gain_in, grad_gain_fin])
    bias_grads = jnp.stack([grad_bias_in, grad_bias_fin, grad_out_bias, grad_fc2_bias])
    owned = (
        lax.psum_scatter(grad_qkv, ("shard", "ctx"), scatter_dimension=1, tiled=True),
        lax.psum_scatter(grad_outw, ("shard", "ctx"), scatter_dimension=1, tiled=True),
        lax.psum_scatter(grad_up, ("shard", "ctx"), scatter_dimension=0, tiled=True),
        lax.psum_scatter(grad_down, ("shard", "ctx"), scatter_dimension=1, tiled=True),
        lax.psum_scatter(gain_grads, ("shard", "ctx"), scatter_dimension=1, tiled=True),
        lax.psum_scatter(bias_grads, ("shard", "ctx"), scatter_dimension=1, tiled=True),
    )
    vectors = lax.psum(
        (
            grad_head_gain,
            jnp.stack([grad_query_bias, grad_value_bias, grad_sub_shift]),
            grad_ffn_gain,
            jnp.stack([grad_up_bias, grad_inner_shift]),
        ),
        ("shard", "ctx"),
    )
    output_low = result.astype(jnp.bfloat16).reshape(seqs_here, local_len, model_width)
    return (
        output_low,
        grad_tokens,
        owned[0],
        owned[1],
        owned[2],
        owned[3],
        owned[4],
        owned[5],
        vectors[0],
        vectors[1],
        vectors[2],
        vectors[3],
    )


def solution(mesh):
    in_specs = (
        P("shard", "ctx", None),
        P("shard", "ctx", None),
        P("shard", None),
        P(None, "shard", "tp"),
        P("tp", "shard"),
        P("shard", "tp"),
        P("tp", "shard"),
        P(None, "shard"),
        P(None, "shard"),
        P("tp"),
        P(None, "tp"),
        P("tp"),
        P(None, "tp"),
    )
    out_specs = (
        P("shard", "ctx", None),
        P("shard", "ctx", None),
        P(None, ("shard", "ctx"), "tp"),
        P("tp", ("shard", "ctx")),
        P(("shard", "ctx"), "tp"),
        P("tp", ("shard", "ctx")),
        P(None, ("shard", "ctx")),
        P(None, ("shard", "ctx")),
        P("tp"),
        P(None, "tp"),
        P("tp"),
        P(None, "tp"),
    )
    return jax.shard_map(
        per_device, mesh=mesh, in_specs=in_specs, out_specs=out_specs, check_vma=False
    )
```

profile of v0, /device:TPU:0, one launch (start us, length us, event | category | flops | bytes accessed | tf_op | source)
XLA Modules:
  0.0 1602.1 jit_solution(5641328594576289393)
XLA Ops:
  22.4 19.9 %all-gather.6.cloned.1.call-done = bf16[3,768,384]{2,1,0:T(8,128)(2,1)} async-done(((bf16[3,384,384]{2,1,0:T(8,128)(2,1)}), bf16[3,768,384]{2,1,0:T(8,128)(2,1)}) %all-gather.6.cloned.1.call-update) | async-done | bytes 1769488 | tf_op jit(solution)/shard_map/all_gather | solution.py:75
  55.1 9.5 all_gather.33
  70.9 43.4 %all-gather.8.cloned.1.call-done = bf16[2,4096,384]{1,2,0:T(8,128)(2,1)} async-done(((bf16[2,512,384]{1,2,0:T(8,128)(2,1)}), bf16[2,4096,384]{1,2,0:T(8,128)(2,1)}) %all-gather.8.cloned.1.call-update) | async-done | bytes 6291472 | tf_op jit(solution)/shard_map/all_gather | solution.py:96
  114.3 65.1 %all-gather.10.cloned.1.call-done = bf16[2,4096,384]{1,2,0:T(8,128)(2,1)} async-done(((bf16[2,512,384]{1,2,0:T(8,128)(2,1)}), bf16[2,4096,384]{1,2,0:T(8,128)(2,1)}) %all-gather.10.cloned.1.call-update) | async-done | bytes 6291472 | tf_op jit(solution)/shard_map/all_gather | solution.py:97
  179.4 141.1 %while.32 = (s32[]{:T(128)}, f32[6,2,512,64]{2,3,1,0:T(8,128)}, f32[6,2,512,1]{2,1,3,0:T(2,128)S(1)}, f32[6,2,512,1]{2,1,3,0:T(2,128)S(1)}, s32[6]{0:T(128)S(1)}...) while((s32[]{:T(128)}, f32[6,2,512,64]{2,3,1,0:T(8,128)}, ...), condition=%wide.region_5.6_spmd.clone.clone, body=%wide.region_2.5_spmd.clone.sunk.clone | while | flops 1149237248 | bytes 59262148 | solution.py:137
  187.4 6.7 fusion.136
  194.1 8.8 fusion.137
  210.9 6.7 fusion.136
  217.6 8.8 fusion.137
  227.7 6.6 fusion.135
  234.3 6.7 fusion.136
  241.0 8.8 fusion.137
  251.1 6.6 fusion.135
  257.8 6.7 fusion.136
  264.5 8.8 fusion.137
  274.6 6.6 fusion.135
  281.2 6.7 fusion.136
  288.0 8.8 fusion.137
  298.0 6.6 fusion.135
  304.7 6.7 fusion.136
  311.4 8.8 fusion.137
  344.0 43.8 %all-reduce.12.cloned.1.call-done = bf16[1024,768]{1,0:T(8,128)(2,1)} async-done(((bf16[1024,768]{1,0:T(8,128)(2,1)}), bf16[1024,768]{1,0:T(8,128)(2,1)}) %all-reduce.12.cloned.1.call-update) | async-done | bytes 1572880 | tf_op jit(solution)/shard_map/psum | solution.py:48
  392.5 32.9 %all-gather.12.cloned.1.call-done = bf16[768,1536]{1,0:T(8,128)(2,1)} async-done(((bf16[384,1536]{1,0:T(8,128)(2,1)}), bf16[768,1536]{1,0:T(8,128)(2,1)}) %all-gather.12.cloned.1.call-update) | async-done | bytes 2359312 | tf_op jit(solution)/shard_map/all_gather | solution.py:77
  425.4 9.2 fusion.79
  439.6 23.4 %all-gather.14.cloned.1.call-done = bf16[1536,768]{1,0:T(8,128)(2,1)} async-done(((bf16[1536,384]{1,0:T(8,128)(2,1)}), bf16[1536,768]{1,0:T(8,128)(2,1)}) %all-gather.14.cloned.1.call-update) | async-done | bytes 2359312 | tf_op jit(solution)/shard_map/all_gather | solution.py:78
  463.0 10.4 multiply_reduce_fusion.1
  478.8 12.0 convert_reduce_fusion
  497.2 50.6 %all-reduce.14.cloned.1.call-done = bf16[1024,768]{1,0:T(8,128)(2,1)} async-done(((bf16[1024,768]{1,0:T(8,128)(2,1)}), bf16[1024,768]{1,0:T(8,128)(2,1)}) %all-reduce.14.cloned.1.call-update) | async-done | bytes 1572880 | tf_op jit(solution)/shard_map/psum | solution.py:52
  569.4 335.4 %while.33 = (s32[]{:T(128)}, bf16[6,2,512,64]{2,3,1,0:T(8,128)(2,1)}, bf16[6,2,4096,64]{2,3,0,1:T(8,128)(2,1)}, bf16[6,2,4096,64]{2,3,0,1:T(8,128)(2,1)}, s32[6]...) while((s32[]{:T(128)}, ...), condition=%wide.region_31.32_spmd.clone.clone, body=%wide.region_29.31_spmd.clone.sunk.clone | while | flops 2735275008 | bytes 180164912 | solution.py:232
  570.7 9.5 fusion.146
  580.2 15.3 multiply_reduce_fusion.12
  595.5 11.8 multiply_convert_fusion.4
  607.3 8.3 fusion.149
  626.6 9.5 fusion.146
  636.1 15.3 multiply_reduce_fusion.12
  651.4 11.8 multiply_convert_fusion.4
  663.2 8.3 fusion.149
  682.4 9.5 fusion.146
  691.9 15.3 multiply_reduce_fusion.12
  707.3 11.8 multiply_convert_fusion.4
  719.1 8.3 fusion.149
  738.3 9.5 fusion.146
  747.8 15.3 multiply_reduce_fusion.12
  763.1 11.8 multiply_convert_fusion.4
  774.9 8.4 fusion.149
  794.2 9.5 fusion.146
  803.7 15.3 multiply_reduce_fusion.12
  819.1 11.8 multiply_convert_fusion.4
  830.9 8.3 fusion.149
  850.1 9.5 fusion.146
  859.5 15.3 multiply_reduce_fusion.12
  874.9 11.8 multiply_convert_fusion.4
  886.7 8.3 fusion.149
  914.0 60.9 %reduce-scatter.14.cloned.1.call-done = bf16[2,512,384]{1,2,0:T(8,128)(2,1)} async-done(((bf16[2,4096,384]{1,2,0:T(8,128)(2,1)}), bf16[2,512,384]{1,2,0:T(8,128)(2,1)}) %reduce-scatter.14.cloned.1.call-update) | async-done | bytes 786448 | tf_op jit(solution)/shard_map/reduce_scatter | solution.py:239
  976.4 69.0 %reduce-scatter.12.cloned.1.call-done = bf16[2,512,384]{1,2,0:T(8,128)(2,1)} async-done(((bf16[2,4096,384]{1,2,0:T(8,128)(2,1)}), bf16[2,512,384]{1,2,0:T(8,128)(2,1)}) %reduce-scatter.12.cloned.1.call-update) | async-done | bytes 786448 | tf_op jit(solution)/shard_map/reduce_scatter | solution.py:236
  1062.2 74.3 %all-reduce.18.cloned.1.call-done = (bf16[1024,768]{1,0:T(8,128)(2,1)}, bf16[1024,768]{1,0:T(8,128)(2,1)}) async-done(((bf16[1024,768]{1,0:T(8,128)(2,1)}, bf16[1024,768]{1,0:T(8,128)(2,1)}), (bf16[1024,768]{1,0:T(8,128)(2,1)}, bf16[1024,768]{1,0:T(8,128)(2,1)})) %all-reduce.18.cloned.1.call-update) | async-done | bytes 3145744 | tf_op jit(solution)/shard_map/psum | solution.py:48
  1148.0 7.8 fusion.75
  1166.9 62.3 %all-reduce.1 = (f32[384]{0:T(512)}, f32[3,384]{1,0:T(4,128)}, f32[1536]{0:T(1024)}, f32[2,1536]{1,0:T(2,128)}) all-reduce(f32[384]{0:T(512)S(1)} %copy-done.68, f32[3,384]{1,0:T(4,128)S(1)} %pad_maximum_fusion.6, f32[1536]{0:T(1024)S(1)} %copy-done.61, ...), channel_id=1, replica_groups=mesh['shard'=2,'ctx'=8,'tp'=2] {'shard','ctx'}, use_global_device_ids=true, to_apply=%region_50.51 | all-reduce | flops 6144 | bytes 49152 | tf_op jit(solution)/shard_map/psum | solution.py:270
  1229.1 29.0 %all-reduce.16.cloned.1.call-done = f32[3,768,384]{2,0,1:T(4,128)} async-done(((f32[3,768,384]{2,0,1:T(4,128)}), f32[3,768,384]{2,0,1:T(4,128)}) %all-reduce.16.cloned.1.call-update) | async-done | bytes 3538960
  1266.3 50.9 %reduce-scatter.22.cloned.1.call-done = f32[48,2]{1,0:T(8,128)} async-done(((f32[768,2]{1,0:T(8,128)}), f32[48,2]{1,0:T(8,128)}) %reduce-scatter.22.cloned.1.call-update) | async-done | bytes 400
  1318.6 56.7 %reduce-scatter.24.cloned.1.call-done = f32[48,4]{1,0:T(8,128)} async-done(((f32[768,4]{1,0:T(8,128)}), f32[48,4]{1,0:T(8,128)}) %reduce-scatter.24.cloned.1.call-update) | async-done | bytes 784
  1376.7 60.1 %reduce-scatter.16.cloned.1.call-done = f32[384,48]{0,1:T(8,128)} async-done(((f32[384,768]{0,1:T(8,128)}), f32[384,48]{0,1:T(8,128)}) %reduce-scatter.16.cloned.1.call-update) | async-done | bytes 73744 | tf_op jit(solution)/shard_map/reduce_scatter | solution.py:264
  1436.8 79.3 %reduce-scatter.18.cloned.1.call-done = f32[48,1536]{1,0:T(8,128)} async-done(((f32[768,1536]{1,0:T(8,128)}), f32[48,1536]{1,0:T(8,128)}) %reduce-scatter.18.cloned.1.call-update) | async-done | bytes 294928 | tf_op jit(solution)/shard_map/reduce_scatter | solution.py:265
  1516.2 79.0 %reduce-scatter.20.cloned.1.call-done = f32[1536,48]{0,1:T(8,128)} async-done(((f32[1536,768]{0,1:T(8,128)}), f32[1536,48]{0,1:T(8,128)}) %reduce-scatter.20.cloned.1.call-update) | async-done | bytes 294928 | tf_op jit(solution)/shard_map/reduce_scatter | solution.py:266
  (368 shorter events, 237.9 us)
Async XLA Ops:
  7.2 8.0 copy-start.63
  7.2 8.0 copy-start
  7.2 35.1 %all-gather.6.cloned.1.call-start = ((), (), s32[]{:S(2)}) async-start(), calls=%async_computation.7 | async-start | bytes 2654208 | tf_op jit(solution)/shard_map/all_gather | solution.py:75
  9.9 104.4 %all-gather.8.cloned.1.call-start = ((), (), s32[]{:S(2)}) async-start(), calls=%async_computation.8 | async-start | bytes 7077888 | tf_op jit(solution)/shard_map/all_gather | solution.py:96
  15.5 6.2 copy-start.38
  16.2 5.6 copy-start.42
  22.4 23.6 %copy-start.21 = (bf16[1024,768]{1,0:T(8,128)(2,1)}, bf16[1024,768]{1,0:T(8,128)(2,1)S(1)}, u32[]{:S(2)}) copy-start(bf16[1024,768]{1,0:T(8,128)(2,1)S(1)} %fusion.61) | copy-start | bytes 4718596
  49.4 129.9 %all-gather.10.cloned.1.call-start = ((), (), s32[]{:S(2)}) async-start(), calls=%async_computation.9 | async-start | bytes 7077888 | tf_op jit(solution)/shard_map/all_gather | solution.py:97
  54.9 333.0 %all-reduce.12.cloned.1.call-start = ((), (), s32[]{:S(2)}) async-start(), calls=%async_computation.10 | async-start | bytes 3145728 | tf_op jit(solution)/shard_map/psum | solution.py:48
  320.4 6.9 copy-start.3
  320.4 6.9 copy-start.20
  325.8 8.4 copy-start.66
  325.8 8.4 copy-start.70
  329.2 8.4 copy-start.14
  334.2 230.5 %copy-start.53 = (f32[1024,1]{0,1:T(1,128)}, f32[1024,1]{0,1:T(1,128)S(1)}, u32[]{:S(2)}) copy-start(f32[1024,1]{0,1:T(1,128)S(1)} %get-tuple-element.385) | copy-start | bytes 12292
  334.2 230.5 %copy-start.55 = (f32[1024,1]{0,1:T(1,128)}, f32[1024,1]{0,1:T(1,128)S(1)}, u32[]{:S(2)}) copy-start(f32[1024,1]{0,1:T(1,128)S(1)} %get-tuple-element.386) | copy-start | bytes 12292
  337.6 87.9 %all-gather.12.cloned.1.call-start = ((), (), s32[]{:S(2)}) async-start(), calls=%async_computation.11 | async-start | bytes 3538944 | tf_op jit(solution)/shard_map/all_gather | solution.py:77
  340.4 47.4 %copy-start.1 = (bf16[2,512,768]{2,1,0:T(8,128)(2,1)S(1)}, bf16[2,512,768]{2,1,0:T(8,128)(2,1)}, u32[]{:S(2)}) copy-start(bf16[2,512,768]{2,1,0:T(8,128)(2,1)} %param.17) | copy-start | bytes 4718596
  340.4 47.4 %copy-start.34 = (f32[768]{0:T(1024)S(1)}, f32[768]{0:T(1024)}, u32[]{:S(2)}) copy-start(f32[768]{0:T(1024)} %get-tuple-element.291) | copy-start | bytes 9220
  340.5 122.5 %all-gather.14.cloned.1.call-start = ((), (), s32[]{:S(2)}) async-start(), calls=%async_computation.12 | async-start | bytes 3538944 | tf_op jit(solution)/shard_map/all_gather | solution.py:78
  343.9 203.9 %all-reduce.14.cloned.1.call-start = ((), (), s32[]{:S(2)}) async-start(), calls=%async_computation.13 | async-start | bytes 3145728 | tf_op jit(solution)/shard_map/psum | solution.py:52
  390.0 164.2 %copy-start.36 = (f32[1024]{0:T(1024)}, f32[1024]{0:T(1024)S(1)}, u32[]{:S(2)}) copy-start(f32[1024]{0:T(1024)S(1)} %broadcast_multiply_fusion.2) | copy-start | bytes 12292
  390.0 35.4 %copy-start.28 = (f32[768]{0:T(1024)S(1)}, f32[768]{0:T(1024)}, u32[]{:S(2)}) copy-start(f32[768]{0:T(1024)} %get-tuple-element.295) | copy-start | bytes 9220
  390.0 35.4 %copy-start.32 = (f32[768]{0:T(1024)S(1)}, f32[768]{0:T(1024)}, u32[]{:S(2)}) copy-start(f32[768]{0:T(1024)} %get-tuple-element.290) | copy-start | bytes 9220
  392.5 161.7 %copy-start.30 = (f32[1024]{0:T(1024)}, f32[1024]{0:T(1024)S(1)}, u32[]{:S(2)}) copy-start(f32[1024]{0:T(1024)S(1)} %fusion.71) | copy-start | bytes 12292
  425.4 37.6 %copy-start.60 = (f32[1536]{0:T(1024)S(1)}, f32[1536]{0:T(1024)}, u32[]{:S(2)}) copy-start(f32[1536]{0:T(1024)} %param.28) | copy-start | bytes 18436
  478.8 13.6 copy-start.72
  496.2 478.7 %reduce-scatter.14.cloned.1.call-start = ((), (), s32[]{:S(2)}) async-start(), calls=%async_computation.15 | async-start | bytes 7077888 | tf_op jit(solution)/shard_map/reduce_scatter | solution.py:239
  551.3 5.5 copy-start.44
  559.6 9.8 copy-start.4
  570.7 49.5 %slice-start = ((s8[6291456]{0:T(1024)(128)(4,1)}), s8[4194304]{0:T(1024)(128)(4,1)S(1)}, s32[]{:S(2)}) async-start(s8[6291456]{0:T(1024)(128)(4,1)} %bitcast.202), calls=%async_computation.23 | async-start | bytes 8388608 | tf_op jit(solution)/shard_map/while
  580.2 40.0 %slice-start.1 = ((s8[6291456]{0:T(1024)(128)(4,1)}), s8[2097152]{0:T(1024)(128)(4,1)S(1)}, s32[]{:S(2)}) async-start(s8[6291456]{0:T(1024)(128)(4,1)} %bitcast.202), calls=%async_computation.24 | async-start | bytes 4194304 | tf_op jit(solution)/shard_map/while
  626.6 49.5 %slice-start = ((s8[6291456]{0:T(1024)(128)(4,1)}), s8[4194304]{0:T(1024)(128)(4,1)S(1)}, s32[]{:S(2)}) async-start(s8[6291456]{0:T(1024)(128)(4,1)} %bitcast.202), calls=%async_computation.23 | async-start | bytes 8388608 | tf_op jit(solution)/shard_map/while
  636.1 40.0 %slice-start.1 = ((s8[6291456]{0:T(1024)(128)(4,1)}), s8[2097152]{0:T(1024)(128)(4,1)S(1)}, s32[]{:S(2)}) async-start(s8[6291456]{0:T(1024)(128)(4,1)} %bitcast.202), calls=%async_computation.24 | async-start | bytes 4194304 | tf_op jit(solution)/shard_map/while
  682.4 49.5 %slice-start = ((s8[6291456]{0:T(1024)(128)(4,1)}), s8[4194304]{0:T(1024)(128)(4,1)S(1)}, s32[]{:S(2)}) async-start(s8[6291456]{0:T(1024)(128)(4,1)} %bitcast.202), calls=%async_computation.23 | async-start | bytes 8388608 | tf_op jit(solution)/shard_map/while
  691.9 40.0 %slice-start.1 = ((s8[6291456]{0:T(1024)(128)(4,1)}), s8[2097152]{0:T(1024)(128)(4,1)S(1)}, s32[]{:S(2)}) async-start(s8[6291456]{0:T(1024)(128)(4,1)} %bitcast.202), calls=%async_computation.24 | async-start | bytes 4194304 | tf_op jit(solution)/shard_map/while
  738.3 49.6 %slice-start = ((s8[6291456]{0:T(1024)(128)(4,1)}), s8[4194304]{0:T(1024)(128)(4,1)S(1)}, s32[]{:S(2)}) async-start(s8[6291456]{0:T(1024)(128)(4,1)} %bitcast.202), calls=%async_computation.23 | async-start | bytes 8388608 | tf_op jit(solution)/shard_map/while
  747.8 40.1 %slice-start.1 = ((s8[6291456]{0:T(1024)(128)(4,1)}), s8[2097152]{0:T(1024)(128)(4,1)S(1)}, s32[]{:S(2)}) async-start(s8[6291456]{0:T(1024)(128)(4,1)} %bitcast.202), calls=%async_computation.24 | async-start | bytes 4194304 | tf_op jit(solution)/shard_map/while
  794.2 49.5 %slice-start = ((s8[6291456]{0:T(1024)(128)(4,1)}), s8[4194304]{0:T(1024)(128)(4,1)S(1)}, s32[]{:S(2)}) async-start(s8[6291456]{0:T(1024)(128)(4,1)} %bitcast.202), calls=%async_computation.23 | async-start | bytes 8388608 | tf_op jit(solution)/shard_map/while
  803.7 40.0 %slice-start.1 = ((s8[6291456]{0:T(1024)(128)(4,1)}), s8[2097152]{0:T(1024)(128)(4,1)S(1)}, s32[]{:S(2)}) async-start(s8[6291456]{0:T(1024)(128)(4,1)} %bitcast.202), calls=%async_computation.24 | async-start | bytes 4194304 | tf_op jit(solution)/shard_map/while
  850.1 49.5 %slice-start = ((s8[6291456]{0:T(1024)(128)(4,1)}), s8[4194304]{0:T(1024)(128)(4,1)S(1)}, s32[]{:S(2)}) async-start(s8[6291456]{0:T(1024)(128)(4,1)} %bitcast.202), calls=%async_computation.23 | async-start | bytes 8388608 | tf_op jit(solution)/shard_map/while
  859.5 40.0 %slice-start.1 = ((s8[6291456]{0:T(1024)(128)(4,1)}), s8[2097152]{0:T(1024)(128)(4,1)S(1)}, s32[]{:S(2)}) async-start(s8[6291456]{0:T(1024)(128)(4,1)} %bitcast.202), calls=%async_computation.24 | async-start | bytes 4194304 | tf_op jit(solution)/shard_map/while
  904.9 140.5 %reduce-scatter.12.cloned.1.call-start = ((), (), s32[]{:S(2)}) async-start(), calls=%async_computation.14 | async-start | bytes 7077888 | tf_op jit(solution)/shard_map/reduce_scatter | solution.py:236
  905.6 230.9 %all-reduce.18.cloned.1.call-start = ((), (), s32[]{:S(2)}) async-start(), calls=%async_computation.22 | async-start | bytes 6291456 | tf_op jit(solution)/shard_map/psum | solution.py:48
  913.6 138.5 %copy-start.12 = (bf16[1,1024,384]{1,2,0:T(8,128)(2,1)}, bf16[1,1024,384]{1,2,0:T(8,128)(2,1)S(1)}, u32[]{:S(2)}) copy-start(bf16[1,1024,384]{1,2,0:T(8,128)(2,1)S(1)} %stack_reshape_reshape.4) | copy-start | bytes 2359300
  914.0 138.1 %copy-start.24 = (bf16[1,1024,384]{2,1,0:T(8,128)(2,1)}, bf16[1,1024,384]{2,1,0:T(8,128)(2,1)S(1)}, u32[]{:S(2)}) copy-start(bf16[1,1024,384]{2,1,0:T(8,128)(2,1)S(1)} %copy.58) | copy-start | bytes 2359300
  976.4 75.7 %copy-start.17 = (bf16[2,512,384]{2,1,0:T(8,128)(2,1)}, bf16[2,512,384]{2,1,0:T(8,128)(2,1)S(1)}, u32[]{:S(2)}) copy-start(bf16[2,512,384]{2,1,0:T(8,128)(2,1)S(1)} %copy.57) | copy-start | bytes 2359300
  1052.1 206.0 %all-reduce.16.cloned.1.call-start = ((), (), s32[]{:S(2)}) async-start(), calls=%async_computation.21 | async-start | bytes 9437184
  1060.5 76.1 %copy-start.2 = (bf16[2,512,768]{2,1,0:T(8,128)(2,1)S(1)}, bf16[2,512,768]{2,1,0:T(8,128)(2,1)}, u32[]{:S(2)}) copy-start(bf16[2,512,768]{2,1,0:T(8,128)(2,1)} %param.17) | copy-start | bytes 4718596
  1060.5 76.1 %copy-start.39 = (f32[1,4,2,128]{3,1,2,0:T(4,128)S(1)}, f32[1,4,2,128]{3,1,2,0:T(4,128)}, u32[]{:S(2)}) copy-start(f32[1,4,2,128]{3,1,2,0:T(4,128)} %copy-done.38) | copy-start | bytes 12292
  1060.5 76.1 %copy-start.41 = (f32[768]{0:T(1024)S(1)}, f32[768]{0:T(1024)}, u32[]{:S(2)}) copy-start(f32[768]{0:T(1024)} %copy-done.40) | copy-start | bytes 9220
  1060.5 78.7 %copy-start.49 = (f32[1,4,2,128]{3,1,2,0:T(4,128)S(1)}, f32[1,4,2,128]{3,1,2,0:T(4,128)}, u32[]{:S(2)}) copy-start(f32[1,4,2,128]{3,1,2,0:T(4,128)} %copy-done.48) | copy-start | bytes 12292
  1060.5 78.7 %copy-start.43 = (f32[1024]{0:T(1024)S(1)}, f32[1024]{0:T(1024)}, u32[]{:S(2)}) copy-start(f32[1024]{0:T(1024)} %copy-done.42) | copy-start | bytes 12292
  1060.6 256.6 %reduce-scatter.22.cloned.1.call-start = ((), (), s32[]{:S(2)}) async-start(), calls=%async_computation.19 | async-start | bytes 417792
  1142.3 233.0 %reduce-scatter.24.cloned.1.call-start = ((), (), s32[]{:S(2)}) async-start(), calls=%async_computation.20 | async-start | bytes 417792
  1143.4 293.5 %reduce-scatter.16.cloned.1.call-start = ((), (), s32[]{:S(2)}) async-start(), calls=%async_computation.16 | async-start | bytes 1253376 | tf_op jit(solution)/shard_map/reduce_scatter | solution.py:264
  1147.7 368.5 %reduce-scatter.18.cloned.1.call-start = ((), (), s32[]{:S(2)}) async-start(), calls=%async_computation.17 | async-start | bytes 5013504 | tf_op jit(solution)/shard_map/reduce_scatter | solution.py:265
  1155.9 439.2 %reduce-scatter.20.cloned.1.call-start = ((), (), s32[]{:S(2)}) async-start(), calls=%async_computation.18 | async-start | bytes 5013504 | tf_op jit(solution)/shard_map/reduce_scatter | solution.py:266
  1162.2 97.6 %copy-start.6 = (bf16[1024,768]{1,0:T(8,128)(2,1)S(1)}, bf16[1024,768]{1,0:T(8,128)(2,1)}, u32[]{:S(2)}) copy-start(bf16[1024,768]{1,0:T(8,128)(2,1)} %all-reduce.12.cloned.1.call-done) | copy-start | bytes 4718596
  1162.2 97.6 %copy-start.35 = (f32[768]{0:T(1024)S(1)}, f32[768]{0:T(1024)}, u32[]{:S(2)}) copy-start(f32[768]{0:T(1024)} %get-tuple-element.291) | copy-start | bytes 9220
  1162.2 97.6 %copy-start.37 = (f32[1024]{0:T(1024)S(1)}, f32[1024]{0:T(1024)}, u32[]{:S(2)}) copy-start(f32[1024]{0:T(1024)} %copy-done.36) | copy-start | bytes 12292
  1162.3 97.6 %copy-start.45 = (f32[1024]{0:T(1024)S(1)}, f32[1024]{0:T(1024)}, u32[]{:S(2)}) copy-start(f32[1024]{0:T(1024)} %copy-done.44) | copy-start | bytes 12292
  1162.3 97.6 %copy-start.47 = (f32[1024]{0:T(1024)S(1)}, f32[1024]{0:T(1024)}, u32[]{:S(2)}) copy-start(f32[1024]{0:T(1024)} %copy-done.46) | copy-start | bytes 12292
  1162.3 97.6 %copy-start.51 = (f32[768]{0:T(1024)S(1)}, f32[768]{0:T(1024)}, u32[]{:S(2)}) copy-start(f32[768]{0:T(1024)} %get-tuple-element.289) | copy-start | bytes 9220
  (43 other events, 122.4 us)
Sparse Core Ops, SparseCore 0:
  10.2 32.1 all-gather.5
  49.6 64.7 all-gather.7
  115.9 63.3 all-gather.9
  337.7 50.1 all-reduce.11
  389.3 36.0 all-gather.11
  426.9 36.0 all-gather.13
  496.3 51.4 all-reduce.13
  905.0 69.8 reduce-scatter.13
  977.2 68.1 reduce-scatter.11
  1052.3 84.2 all-reduce.17
  1140.6 117.4 all-reduce.15
  1261.9 55.2 reduce-scatter.21
  1320.7 54.5 reduce-scatter.23
  1379.8 56.9 reduce-scatter.15
  1441.6 74.5 reduce-scatter.17
  1520.4 74.6 reduce-scatter.19
where the time goes:
time: 1610 us; the launch traced here: 1600 us
  waiting for transfers between devices  839 us (52%)
  matrix products  400 us (25%)
  other arithmetic  172 us (11%)
  blocking collectives  102 us (6%)
  local copies, waits for them, and re-layouts  62.9 us (4%)
  between operations  16.2 us (1%)
    unnamed x19, waiting for transfers between devices  138 us
    dot_general x12, matrix products, scores(): jnp.einsum('sqd,skd->sqk', columns(queries, head_index), columns(keys_all...  132 us
    psum x2, waiting for transfers between devices, tensor_sum(): return lax.psum(partial_part.astype(jnp.bfloat16), 'tp').astype(jnp.float32)  118 us
    reduce_scatter x1, waiting for transfers between devices, per_device(): lax.psum_scatter(grad_up, ('shard', 'ctx'), scatter_dimension=0, tiled=True)  79.3 us
    reduce_scatter x1, waiting for transfers between devices, per_device(): lax.psum_scatter(grad_down, ('shard', 'ctx'), scatter_dimension=1, tiled=...  79 us
    convert_element_type x6, other arithmetic, backward_head(): score_grad = (probs * (prob_grad - weighted)).astype(jnp.bfloat16)  70.8 us
    reduce_scatter x1, waiting for transfers between devices, per_device(): lax.psum_scatter(merge_heads(key_grads).astype(jnp.bfloat16), 'ctx', scat...  69 us
    all_gather x1, waiting for transfers between devices, per_device(): lax.all_gather(own_values, 'ctx', axis=1, tiled=True)  65.1 us
  transfers between devices with their start and end apart: 16, of which 16 were waited for; matrix products, arithmetic and copies ran while one was open for 6% of the time, Pallas kernels for 0%

commit v1 on v0

v1 whole, which is shorter than its diff:
```python
import functools
import jax
import jax.numpy as jnp
from jax import lax
from jax.experimental import pallas as pl
from jax.experimental.pallas import tpu as pltpu
from jax.sharding import PartitionSpec as P
HD=64
NEG=-1e30
VL=48*1024*1024

def fwd_kernel(diag,first,last,heads,L,BQ,BK, lo_sm, qT_ref,kv_ref,lo_ref,*rest):
    n=heads*HD
    if first:
        ins=(); rest=rest
    else:
        m_in,l_in,a_in=rest[:3]; rest=rest[3:]
    if last:
        c_ref,oT_ref,lse_ref,mean_ref=rest[:4]; rest=rest[4:]
    else:
        m_out,l_out,a_out=rest[:3]; rest=rest[3:]
    m_s,l_s,acc,qm,vT=rest
    if first:
        m_s[...]=jnp.full_like(m_s,NEG); l_s[...]=jnp.zeros_like(l_s); acc[...]=jnp.zeros_like(acc)
    else:
        m_s[...]=m_in[...]; l_s[...]=l_in[...]; acc[...]=a_in[...]
    nq,nk=L//BQ,L//BK
    rowi=lax.broadcasted_iota(jnp.int32,(2*HD,L),0)
    for p in range(heads//2):
        blk=qT_ref[p*128:(p+1)*128,:]
        qm[2*p]=jnp.where(rowi<HD,blk,jnp.zeros_like(blk))
        qm[2*p+1]=jnp.where(rowi>=HD,blk,jnp.zeros_like(blk))
        vT[p*128:(p+1)*128,:]=kv_ref[:,n+p*128:n+(p+1)*128].T
    def block(qb,kb,masked):
        qs=slice(qb*BQ,(qb+1)*BQ); ks=slice(kb*BK,(kb+1)*BK)
        if masked:
            kk=lax.broadcasted_iota(jnp.int32,(BK,BQ),0)+kb*BK
            valid=kk>=lo_ref[:,qs]
            if diag and (kb+1)*BK>qb*BQ+1:
                valid=valid&(kk<=lax.broadcasted_iota(jnp.int32,(BK,BQ),1)+qb*BQ)
        for h in range(heads):
            p=h//2
            s=jnp.dot(kv_ref[ks,p*128:(p+1)*128],qm[h,:,qs],preferred_element_type=jnp.float32)
            if masked: s=jnp.where(valid,s,NEG)
            mo=m_s[h:h+1,qs]
            mn=jnp.maximum(mo,jnp.max(s,0,keepdims=True))
            e=jnp.exp(s-mn); al=jnp.exp(mo-mn)
            m_s[h:h+1,qs]=mn
            l_s[h:h+1,qs]=l_s[h:h+1,qs]*al+jnp.sum(e,0,keepdims=True)
            hs=slice(h*HD,(h+1)*HD)
            acc[hs,qs]=acc[hs,qs]*al+jnp.dot(vT[hs,ks],e.astype(jnp.bfloat16),preferred_element_type=jnp.float32)
    for qb in range(nq):
        for kb in range(nk):
            if diag and kb*BK>qb*BQ+BQ-1: continue
            vis=lo_sm[qb]<=kb*BK+BK-1
            if diag and (kb+1)*BK>qb*BQ+1:
                pl.when(vis)(functools.partial(block,qb,kb,True))
            else:
                full=lo_sm[nq+qb]<=kb*BK
                pl.when(full)(functools.partial(block,qb,kb,False))
                pl.when(jnp.logical_and(vis,jnp.logical_not(full)))(functools.partial(block,qb,kb,True))
    if last:
        tot=jnp.zeros((1,L),jnp.float32)
        for h in range(heads):
            hs=slice(h*HD,(h+1)*HD)
            o=acc[hs,:]/l_s[h:h+1,:]
            oT_ref[hs,:]=o
            tot=tot+jnp.sum(o,0,keepdims=True)
        mean=tot/n
        mean_ref[...]=mean
        lse_ref[...]=m_s[...]+jnp.log(l_s[...])
        for p in range(heads//2):
            c_ref[:,p*128:(p+1)*128]=(oT_ref[p*128:(p+1)*128,:]-mean).T.astype(jnp.bfloat16)
    else:
        m_out[...]=m_s[...]; l_out[...]=l_s[...]; a_out[...]=acc[...]

def fwd_step(w,nw,lo_sm,qT,kv,lo,state):
    n,L=qT.shape; heads=n//HD
    BQ=min(256,L); BK=min(256,L)
    first=w==0; last=w==nw
    V=pl.BlockSpec(memory_space=pltpu.VMEM)
    st=(jax.ShapeDtypeStruct((8,L),jnp.float32),jax.ShapeDtypeStruct((8,L),jnp.float32),jax.ShapeDtypeStruct((n,L),jnp.float32))
    outs=st if not last else (jax.ShapeDtypeStruct((L,n),jnp.bfloat16),st[2],st[0],jax.ShapeDtypeStruct((1,L),jnp.float32))
    args=(lo_sm,qT,kv,lo)+(() if first else tuple(state))
    return pl.pallas_call(
        functools.partial(fwd_kernel,w==0,first,last,heads,L,BQ,BK),
        out_shape=outs,
        in_specs=[pl.BlockSpec(memory_space=pltpu.SMEM)]+[V]*(len(args)-1),
        out_specs=tuple([V]*len(outs)),
        scratch_shapes=[pltpu.VMEM((8,L),jnp.float32),pltpu.VMEM((8,L),jnp.float32),pltpu.VMEM((n,L),jnp.float32),
            pltpu.VMEM((heads,128,L),jnp.bfloat16),pltpu.VMEM((n,L),jnp.bfloat16)],
        compiler_params=pltpu.CompilerParams(vmem_limit_bytes=VL),
        cost_estimate=pl.CostEstimate(flops=4*L*L*n,bytes_accessed=4*L*n*4,transcendentals=heads*L*L),
        name="attn_fwd",
    )(*args)

def bwd_kernel(NT,diag,first,last,heads,L,BQ,BK,lo_sm,qT_ref,q_ref,doT_ref,do_ref,kv_ref,lse_ref,dd_ref,lo_ref,*rest):
    n=heads*HD
    if first:
        pass
    else:
        dq_in,dkv_in=rest[:2]; rest=rest[2:]
    dq_out,dkv_out=rest[:2]; rest=rest[2:]
    qm,dm,kT,dk,dv=rest
    if first: dq_out[...]=jnp.zeros_like(dq_out)
    else: dq_out[...]=dq_in[...]
    dk[...]=jnp.zeros_like(dk); dv[...]=jnp.zeros_like(dv)
    nq,nk=L//BQ,L//BK
    rowi=lax.broadcasted_iota(jnp.int32,(2*HD,L),0)
    for p in range(heads//2):
        ps=slice(p*128,(p+1)*128)
        for ref,dst in ((qT_ref,qm),(doT_ref,dm)):
            blk=ref[ps,:]
            dst[2*p]=jnp.where(rowi<HD,blk,jnp.zeros_like(blk))
            dst[2*p+1]=jnp.where(rowi>=HD,blk,jnp.zeros_like(blk))
        kT[ps,:]=kv_ref[:,ps].T
    lane=lax.broadcasted_iota(jnp.int32,(BK,128),1)
    def block(qb,kb,masked):
        qs=slice(qb*BQ,(qb+1)*BQ); ks=slice(kb*BK,(kb+1)*BK)
        if masked:
            kk=lax.broadcasted_iota(jnp.int32,(BK,BQ),0)+kb*BK
            valid=kk>=lo_ref[:,qs]
            if diag and (kb+1)*BK>qb*BQ+1:
                valid=valid&(kk<=lax.broadcasted_iota(jnp.int32,(BK,BQ),1)+qb*BQ)
        for p in range(heads//2):
            ps=slice(p*128,(p+1)*128)
            pv=slice(n+p*128,n+(p+1)*128)
            parts=[]
            for h in (2*p,2*p+1):
                hs=slice(h*HD,(h+1)*HD)
                s=jnp.dot(kv_ref[ks,ps],qm[h,:,qs],preferred_element_type=jnp.float32)
                dp=jnp.dot(kv_ref[ks,pv],dm[h,:,qs],preferred_element_type=jnp.float32)
                if masked: s=jnp.where(valid,s,NEG)
                e=jnp.exp(s-lse_ref[h:h+1,qs])
                ds=(e*(dp-dd_ref[h:h+1,qs])).astype(jnp.bfloat16)
                eb=e.astype(jnp.bfloat16)
                if NT:
                    nt=(((1,),(1,)),((),()))
                    dv[hs,ks]+=lax.dot_general(doT_ref[hs,qs],eb,nt,preferred_element_type=jnp.float32)
                    dk[hs,ks]+=lax.dot_general(qT_ref[hs,qs],ds,nt,preferred_element_type=jnp.float32)
                else:
                    parts.append((jnp.dot(eb,do_ref[qs,ps],preferred_element_type=jnp.float32),
                              jnp.dot(ds,q_ref[qs,ps],preferred_element_type=jnp.float32)))
                dq_out[hs,qs]+=jnp.dot(kT[hs,ks],ds,preferred_element_type=jnp.float32)
            if not NT:
                dv[ks,ps]+=jnp.where(lane<HD,parts[0][0],parts[1][0])
                dk[ks,ps]+=jnp.where(lane<HD,parts[0][1],parts[1][1])
    for qb in range(nq):
        for kb in range(nk):
            if diag and kb*BK>qb*BQ+BQ-1: continue
            vis=lo_sm[qb]<=kb*BK+BK-1
            if diag and (kb+1)*BK>qb*BQ+1:
                pl.when(vis)(functools.partial(block,qb,kb,True))
            else:
                full=lo_sm[nq+qb]<=kb*BK
                pl.when(full)(functools.partial(block,qb,kb,False))
                pl.when(jnp.logical_and(vis,jnp.logical_not(full)))(functools.partial(block,qb,kb,True))
    for p in range(heads//2):
        ps=slice(p*128,(p+1)*128)
        pv=slice(n+p*128,n+(p+1)*128)
        a,b=(dk[ps,:].T,dv[ps,:].T) if NT else (dk[:,ps],dv[:,ps])
        if first:
            dkv_out[:,ps]=a.astype(jnp.bfloat16); dkv_out[:,pv]=b.astype(jnp.bfloat16)
        else:
            dkv_out[:,ps]=(a+dkv_in[:,ps].astype(jnp.float32)).astype(jnp.bfloat16)
            dkv_out[:,pv]=(b+dkv_in[:,pv].astype(jnp.float32)).astype(jnp.bfloat16)

def bwd_step(w,nw,lo_sm,qT,q,doT,do,kv,lse,dd,lo,dq,dkv,NT=False):
    n,L=qT.shape; heads=n//HD
    BQ=min(256,L); BK=min(256,L)
    first=w==nw
    V=pl.BlockSpec(memory_space=pltpu.VMEM)
    outs=(jax.ShapeDtypeStruct((n,L),jnp.float32),jax.ShapeDtypeStruct((L,2*n),jnp.bfloat16))
    args=(lo_sm,qT,q,doT,do,kv,lse,dd,lo)+(() if first else (dq,dkv))
    return pl.pallas_call(
        functools.partial(bwd_kernel,NT,w==0,first,w==0,heads,L,BQ,BK),
        out_shape=outs,
        in_specs=[pl.BlockSpec(memory_space=pltpu.SMEM)]+[V]*(len(args)-1),
        out_specs=(V,V),
        scratch_shapes=[pltpu.VMEM((heads,128,L),jnp.bfloat16),pltpu.VMEM((heads,128,L),jnp.bfloat16),pltpu.VMEM((n,L),jnp.bfloat16)]
            +[pltpu.VMEM((n,L) if NT else (L,n),jnp.float32)]*2,
        compiler_params=pltpu.CompilerParams(vmem_limit_bytes=VL),
        cost_estimate=pl.CostEstimate(flops=10*L*L*n,bytes_accessed=8*L*n*4,transcendentals=heads*L*L),
        name="attn_bwd",
    )(*args)


EPS = 1e-05
MAXDOC = 1920
BF = jnp.bfloat16
F32 = jnp.float32
NT_DIMS = (((1,), (1,)), ((), ()))
VMEM_SPEC = pl.BlockSpec(memory_space=pltpu.VMEM)
ANY_SPEC = pl.BlockSpec(memory_space=pl.ANY)
GELU_C = 0.7978845608028654
GELU_A = 0.044715


def dot(left, right):
    return jnp.dot(left, right, preferred_element_type=F32)


def dot_nt(left, right):
    return lax.dot_general(left, right, NT_DIMS, preferred_element_type=F32)


def row_mean(values):
    return jnp.mean(values, -1, keepdims=True)


def col_sum(values):
    return jnp.sum(values, 0, keepdims=True)


def qkv_kernel(x_ref, w_ref, gain_ref, shift_ref, qb_ref, vb_ref, a_ref, q_ref, qT_ref, kv_ref):
    n = qb_ref.shape[1]
    x = x_ref[...].astype(F32)
    cen = x - row_mean(x)
    a = cen * lax.rsqrt(row_mean(cen * cen) + EPS) * gain_ref[...] + shift_ref[...]
    a = a.astype(BF)
    a_ref[...] = a
    q = (dot(a, w_ref[0]) + qb_ref[...]).astype(BF).astype(F32) * 0.125
    q = q.astype(BF)
    q_ref[...] = q
    for p in range(n // 128):
        ps = slice(p * 128, (p + 1) * 128)
        qT_ref[ps, :] = q[:, ps].T
    kv_ref[:, :n] = dot(a, w_ref[1]).astype(BF)
    kv_ref[:, n:] = (dot(a, w_ref[2]) + vb_ref[...]).astype(BF)


def qkv_call(x, w, gain, shift, qb, vb):
    rows, width = x.shape
    n = qb.shape[1]
    return pl.pallas_call(
        qkv_kernel,
        out_shape=(
            jax.ShapeDtypeStruct((rows, width), BF),
            jax.ShapeDtypeStruct((rows, n), BF),
            jax.ShapeDtypeStruct((n, rows), BF),
            jax.ShapeDtypeStruct((rows, 2 * n), BF),
        ),
        in_specs=[VMEM_SPEC] * 6,
        out_specs=(VMEM_SPEC,) * 4,
        compiler_params=pltpu.CompilerParams(vmem_limit_bytes=VL),
        cost_estimate=pl.CostEstimate(
            flops=6 * rows * width * n, bytes_accessed=rows * width * 8 + 6 * width * n, transcendentals=rows
        ),
        name="qkv",
    )(x, w, gain, shift, qb, vb)


def gelu_pair(h):
    inner = GELU_C * (h + GELU_A * h * h * h)
    t = jnp.tanh(inner)
    half = 0.5 * (1.0 + t)
    slope = half + 0.5 * h * (1.0 - t * t) * (GELU_C * (1.0 + (3.0 * GELU_A) * h * h))
    return h * half, slope


def ffn_kernel(
    step,
    c0_ref, c1_ref, delta_ref, x_ref, g_ref, fw_ref, hg_ref, hb_ref, vec_ref, fvec_ref,
    out_ref, g1_ref, dat_ref, o_ref, f_ref, z_ref, dh_ref, hsum_ref, dsum_ref, fsum_ref,
    fw, u_s, gp_s, e_s, sems,
):
    ff2 = z_ref.shape[1] // 2
    n = c0_ref.shape[1]
    copies = []
    for i, (lo, hi) in enumerate(((2 * ff2, 2 * ff2 + n), (0, ff2), (ff2, 2 * ff2))):
        cp = pltpu.make_async_copy(fw_ref.at[:, :, lo:hi], fw.at[:, :, lo:hi], sems.at[i])
        cp.start()
        copies.append(cp)
    ocols = slice(2 * ff2, 2 * ff2 + n)

    n0 = c0_ref[...].astype(F32) + delta_ref[...]
    n1 = c1_ref[...].astype(F32) - delta_ref[...]
    var = (jnp.sum(n0 * n0, -1, keepdims=True) + jnp.sum(n1 * n1, -1, keepdims=True)) / (2 * n)
    rs = lax.rsqrt(var + EPS)
    nh = (n0 * rs, n1 * rs)
    os = []
    for p in range(2):
        cs = slice(p * n, (p + 1) * n)
        o = (nh[p] * hg_ref[:, cs] + hb_ref[:, cs]).astype(BF)
        o_ref[:, cs] = o
        os.append(o)
    copies[0].wait()
    y1 = x_ref[...].astype(F32) + vec_ref[2:3, :]
    for p in range(2):
        y1 = y1 + dot_nt(os[p], fw[p, :, ocols])
    cen = y1 - row_mean(y1)
    r2 = lax.rsqrt(row_mean(cen * cen) + EPS)
    yh = cen * r2
    f = (yh * vec_ref[0:1, :] + vec_ref[1:2, :]).astype(BF)
    f_ref[...] = f
    copies[1].wait()
    usum = 0.0
    chunks = [(p, j) for p in range(2) for j in range(0, ff2, step)]
    for p, j in chunks:
        cs = slice(p * ff2 + j, p * ff2 + j + step)
        h = dot(f, fw[p, :, j : j + step]) + fvec_ref[0:1, cs]
        u, slope = gelu_pair(h)
        u_s[:, cs] = u
        gp_s[:, cs] = slope
        usum = usum + jnp.sum(u, -1, keepdims=True)
    mu = usum / (2 * ff2)
    ssum = 0.0
    for p, j in chunks:
        cs = slice(p * ff2 + j, p * ff2 + j + step)
        d = u_s[:, cs] - mu
        ssum = ssum + jnp.sum(d * d, -1, keepdims=True)
    ru = lax.rsqrt(ssum / (2 * ff2) + EPS)
    copies[2].wait()
    g2 = g_ref[...]
    y2 = y1 + vec_ref[3:4, :]
    esum = 0.0
    ezsum = 0.0
    for p, j in chunks:
        cs = slice(p * ff2 + j, p * ff2 + j + step)
        w2 = fw[p, :, ff2 + j : ff2 + j + step]
        zh = (u_s[:, cs] - mu) * ru
        u_s[:, cs] = zh
        z = (zh * fvec_ref[1:2, cs] + fvec_ref[2:3, cs]).astype(BF)
        z_ref[:, cs] = z
        y2 = y2 + dot_nt(z, w2)
        dz = dot(g2, w2)
        fsum_ref[1:2, cs] = col_sum(dz * zh)
        fsum_ref[2:3, cs] = col_sum(dz)
        e = dz * fvec_ref[1:2, cs]
        e_s[:, cs] = e
        esum = esum + jnp.sum(e, -1, keepdims=True)
        ezsum = ezsum + jnp.sum(e * zh, -1, keepdims=True)
    out_ref[...] = y2.astype(BF)
    em = esum / (2 * ff2)
    ezm = ezsum / (2 * ff2)
    df = jnp.zeros_like(y1)
    for p, j in chunks:
        cs = slice(p * ff2 + j, p * ff2 + j + step)
        du = ru * (e_s[:, cs] - em - u_s[:, cs] * ezm)
        dh = (du * gp_s[:, cs]).astype(BF)
        dh_ref[:, cs] = dh
        fsum_ref[0:1, cs] = col_sum(dh.astype(F32))
        df = df + dot_nt(dh, fw[p, :, j : j + step])
    dsum_ref[0:1, :] = col_sum(df * yh)
    dsum_ref[1:2, :] = col_sum(df)
    e2 = df * vec_ref[0:1, :]
    g = g2.astype(F32)
    dy1 = g + r2 * (e2 - row_mean(e2) - yh * row_mean(e2 * yh))
    g1 = dy1.astype(BF)
    g1_ref[...] = g1
    dsum_ref[2:3, :] = col_sum(g1.astype(F32))
    dsum_ref[3:4, :] = col_sum(g)
    es = []
    for p in range(2):
        cs = slice(p * n, (p + 1) * n)
        dsub = dot(g1, fw[p, :, ocols])
        hsum_ref[0:1, cs] = col_sum(dsub * nh[p])
        hsum_ref[1:2, cs] = col_sum(dsub)
        es.append(dsub * hg_ref[:, cs])
    em = sum(jnp.sum(e, -1, keepdims=True) for e in es) / (2 * n)
    ezm = sum(jnp.sum(e * h, -1, keepdims=True) for e, h in zip(es, nh)) / (2 * n)
    for p in range(2):
        cs = slice(p * n, (p + 1) * n)
        dat_ref[:, cs] = (rs * (es[p] - em - nh[p] * ezm)).astype(BF)


def ffn_call(c0, c1, delta, x, g, fw, hg, hb, vec, fvec):
    rows, n = c0.shape
    width = x.shape[1]
    ff = fvec.shape[1]
    step = 512
    sds = jax.ShapeDtypeStruct
    return pl.pallas_call(
        functools.partial(ffn_kernel, step),
        out_shape=(
            sds((rows, width), BF),
            sds((rows, width), BF),
            sds((rows, 2 * n), BF),
            sds((rows, 2 * n), BF),
            sds((rows, width), BF),
            sds((rows, ff), BF),
            sds((rows, ff), BF),
            sds((2, 2 * n), F32),
            sds((4, width), F32),
            sds((3, ff), F32),
        ),
        in_specs=[VMEM_SPEC] * 5 + [ANY_SPEC] + [VMEM_SPEC] * 4,
        out_specs=(VMEM_SPEC,) * 10,
        scratch_shapes=[
            pltpu.VMEM(fw.shape, BF),
            pltpu.VMEM((rows, ff), F32),
            pltpu.VMEM((rows, ff), F32),
            pltpu.VMEM((rows, ff), F32),
            pltpu.SemaphoreType.DMA((3,)),
        ],
        compiler_params=pltpu.CompilerParams(vmem_limit_bytes=VL),
        cost_estimate=pl.CostEstimate(
            flops=2 * rows * fw.size * 2, bytes_accessed=2 * fw.size, transcendentals=rows * ff
        ),
        name="ffn",
    )(c0, c1, delta, x, g, fw, hg, hb, vec, fvec)


def tail_kernel(own_ref, peer_ref, x_ref, g1_ref, gain_ref, out_ref, sum_ref):
    da = own_ref[...].astype(F32) + peer_ref[...].astype(F32)
    x = x_ref[...].astype(F32)
    cen = x - row_mean(x)
    r = lax.rsqrt(row_mean(cen * cen) + EPS)
    xh = cen * r
    sum_ref[0:1, :] = col_sum(da * xh)
    sum_ref[1:2, :] = col_sum(da)
    e = da * gain_ref[...]
    dx = r * (e - row_mean(e) - xh * row_mean(e * xh))
    out_ref[...] = (g1_ref[...].astype(F32) + dx).astype(BF)


def tail_call(own, peer, x, g1, gain):
    rows, width = x.shape
    return pl.pallas_call(
        tail_kernel,
        out_shape=(jax.ShapeDtypeStruct((rows, width), BF), jax.ShapeDtypeStruct((2, width), F32)),
        in_specs=[VMEM_SPEC] * 5,
        out_specs=(VMEM_SPEC, VMEM_SPEC),
        compiler_params=pltpu.CompilerParams(vmem_limit_bytes=VL),
        cost_estimate=pl.CostEstimate(
            flops=20 * rows * width, bytes_accessed=10 * rows * width, transcendentals=rows
        ),
        name="tail",
    )(own, peer, x, g1, gain)


def swap(value, axis):
    return lax.ppermute(value, axis, [(0, 1), (1, 0)])


def hop(value, bit):
    size = lax.axis_size("ctx")
    return lax.ppermute(value, "ctx", [(i, i ^ bit) for i in range(size)])


def shift(value, by):
    size = lax.axis_size("ctx")
    return lax.ppermute(value, "ctx", [(i, i + by) for i in range(size) if 0 <= i + by < size])


def ordered(own, peer, index, axis):
    first = jnp.where(index == 0, own, peer)
    second = jnp.where(index == 0, peer, own)
    return jnp.concatenate([first, second], axis)


def put(whole, piece, *start):
    return lax.dynamic_update_slice(whole, piece, start)


def gather_qkv(w, fast, s, c):
    if not fast:
        return lax.all_gather(w, "shard", axis=1, tiled=True)
    k, rows, cols = w.shape
    half = rows // 2
    mine = lax.dynamic_slice_in_dim(w, c * half, half, 1)
    far = swap(mine, "shard")
    rest = hop(far, 1)
    full = jnp.zeros((k, 2 * rows, cols), w.dtype)
    full = put(full, w, 0, s * rows, 0)
    full = put(full, far, 0, (1 - s) * rows + c * half, 0)
    return put(full, rest, 0, (1 - s) * rows + (1 - c) * half, 0)


def gather_ffn(w, fast, s, c, t):
    if not fast:
        w = lax.all_gather(w, "shard", axis=0, tiled=True)
        return lax.all_gather(w, "tp", axis=0)
    rows, cols = w.shape
    half = rows // 2
    mine = lax.dynamic_slice_in_dim(w, c * half, half, 0)
    near = swap(mine, "tp")
    far = swap(mine, "shard")
    both = swap(far, "tp")
    full = jnp.zeros((2, 2 * rows, cols), w.dtype)
    full = put(full, w[None], t, s * rows, 0)
    for piece, ti, si in ((far, t, 1 - s), (near, 1 - t, s), (both, 1 - t, 1 - s)):
        full = put(full, piece[None], ti, si * rows + c * half, 0)
        full = put(full, hop(piece, 1)[None], ti, si * rows + (1 - c) * half, 0)
    return full


def take(value, index, axis):
    return lax.dynamic_index_in_dim(value, index, axis, keepdims=False)


def scatter_rows(grad, fast, s, z, c, t=None):
    width, cols = grad.shape
    if not fast:
        if t is not None:
            grad = lax.psum_scatter(grad.reshape(width, 2, cols // 2), "tp", scatter_dimension=1, tiled=False)
        return lax.psum_scatter(grad.astype(F32), ("shard", "ctx"), scatter_dimension=0, tiled=True)
    nz = lax.axis_size("ctx") // 2
    part = grad.astype(BF).reshape(2, nz, 2, width // (4 * nz), cols)

    def fold(value, index, axis, send):
        got = send(take(value, 1 - index, axis))
        return (take(value, index, axis).astype(F32) + got.astype(F32)).astype(BF)

    part = fold(part, c, 2, lambda v: hop(v, 1))
    if t is not None:
        part = part.reshape(part.shape[:-1] + (2, cols // 2))
        part = fold(part, t, part.ndim - 2, lambda v: swap(v, "tp"))
    part = fold(part, s, 0, lambda v: swap(v, "shard"))
    bit = nz // 2
    while bit:
        part = part.reshape((2, bit) + part.shape[-2:])
        part = fold(part, (z // bit) % 2, 0, lambda v, b=2 * bit: hop(v, b))
        bit //= 2
    return part.reshape(part.shape[-2:]).astype(F32)


def per_device(
    tokens,
    cotangent,
    segment_ids,
    w_qkv,
    w_out,
    w_fc1,
    w_fc2,
    norm_gain,
    norm_bias,
    head_gain,
    head_bias,
    ffn_gain,
    ffn_bias,
):
    seqs, length, width = tokens.shape
    n = w_qkv.shape[2]
    heads = n // HD
    ff2 = w_fc1.shape[1]
    half = length // 2
    s, r, t = lax.axis_index("shard"), lax.axis_index("ctx"), lax.axis_index("tp")
    c, z = r % 2, r // 2
    fast = lax.axis_size("shard") == 2
    nw = min(-(-(MAXDOC - 1) // length), lax.axis_size("ctx") - 1)

    wqkv = gather_qkv(w_qkv.astype(BF), fast, s, c)
    small = jnp.concatenate([norm_gain, norm_bias]).astype(BF)
    if fast:
        small = ordered(small, swap(small, "shard"), s, 1)
    else:
        small = lax.all_gather(small, "shard", axis=1, tiled=True)
    small = small.astype(F32)
    gains, biases = small[:2], small[2:]
    vectors = jnp.concatenate([ffn_bias[0], ffn_gain, ffn_bias[1], head_gain, head_bias[2]])
    far = swap(vectors, "tp")
    v0, v1 = jnp.where(t == 0, vectors, far), jnp.where(t == 0, far, vectors)
    fvec = jnp.concatenate([v0[: 3 * ff2].reshape(3, ff2), v1[: 3 * ff2].reshape(3, ff2)], 1)
    hvec = jnp.concatenate([v0[3 * ff2 :].reshape(2, n), v1[3 * ff2 :].reshape(2, n)], 1)
    hg, hb = hvec[:1], hvec[1:]
    pack = jnp.concatenate([w_fc1.astype(BF), w_fc2.astype(BF).T, w_out.astype(BF).T], 1)
    fw = gather_ffn(pack, fast, s, c, t)
    vec = jnp.stack([gains[1], biases[1], biases[2], biases[3]])

    below = jnp.sum(segment_ids[:, None, :] < jnp.arange(1, 4, dtype=jnp.int32)[None, :, None], -1, dtype=jnp.int32)
    seg_q = lax.dynamic_slice_in_dim(segment_ids, r * length, length, 1)
    start = jnp.zeros_like(seg_q)
    for v in range(1, 4):
        start = jnp.where(seg_q == v, below[:, v - 1 : v], start)
    block = min(256, length)

    def bounds(b, w):
        lo = start[b] + (w - r) * length
        return jnp.concatenate([lo[::block], lo[block - 1 :: block]]), lo[None]

    acts, qs, qTs, rings, states = [], [], [], [], []
    for b in range(seqs):
        a, q, qT, kv = qkv_call(tokens[b], wqkv, gains[:1], biases[:1], head_bias[:1], head_bias[1:2])
        acts.append(a)
        qs.append(q)
        qTs.append(qT)
        rings.append([kv])
        states.append(None)
    for w in range(nw):
        for b in range(seqs):
            rings[b].append(shift(rings[b][w], 1))
    for w in range(nw + 1):
        for b in range(seqs):
            sm, lo = bounds(b, w)
            states[b] = fwd_step(w, nw, sm, qTs[b], rings[b][w], lo, states[b])

    def own_rows(value, index):
        return lax.dynamic_slice_in_dim(value, index * half, half, 0)

    outs, g1s, dos, mids = [], [], [], []
    for b in range(seqs):
        cen, oT, lse, mean = states[b]
        own, peer = own_rows(cen, t), swap(own_rows(cen, 1 - t), "tp")
        mrow = mean.reshape(length, 1)
        mown, mpeer = own_rows(mrow, t), swap(own_rows(mean[0], 1 - t), "tp").reshape(half, 1)
        first = t == 0
        c0, c1 = jnp.where(first, own, peer), jnp.where(first, peer, own)
        delta = jnp.where(first, mown - mpeer, mpeer - mown) * 0.5
        x, g = own_rows(tokens[b], t), own_rows(cotangent[b], t)
        mid = ffn_call(c0, c1, delta, x, g, fw, hg, hb, vec, fvec)
        out, g1, dat = mid[:3]
        mids.append(mid[3:] + (g, g1))
        mine = lax.dynamic_slice_in_dim(dat, t * n, n, 1)
        theirs = lax.dynamic_slice_in_dim(dat, (1 - t) * n, n, 1)
        dos.append(ordered(mine, swap(theirs, "tp"), t, 0))
        outs.append(ordered(out, swap(out, "tp"), t, 0))
        g1s.append(ordered(g1, swap(g1, "tp"), t, 0))

    prep, dqs, dkvs = [], [None] * seqs, [None] * seqs
    for b in range(seqs):
        cen, oT, lse, mean = states[b]
        doT = dos[b].T
        dd = jnp.sum(doT.reshape(heads, HD, length).astype(F32) * oT.reshape(heads, HD, length), 1)
        dd = jnp.concatenate([dd, jnp.zeros((8 - heads, length), F32)])
        prep.append((doT, dd))
    for w in range(nw, -1, -1):
        for b in range(seqs):
            sm, lo = bounds(b, w)
            doT, dd = prep[b]
            dqs[b], dkvs[b] = bwd_step(
                w, nw, sm, qTs[b], qs[b], doT, dos[b], rings[b][w], states[b][2], dd, lo, dqs[b], dkvs[b]
            )
            if w:
                dkvs[b] = shift(dkvs[b], -1)

    def rows_of(i):
        return jnp.concatenate([mids[b][i] for b in range(seqs)])

    def outer(left, right):
        return lax.dot_general(left, right, (((0,), (0,)), ((), ())), preferred_element_type=F32).astype(BF)

    o_all, f_all, z_all, dh_all, g_all, g1_all = (rows_of(i) for i in (0, 1, 2, 3, 7, 8))
    grad_down = scatter_rows(outer(g_all, z_all), fast, s, z, c, t).T
    grad_up = scatter_rows(outer(f_all, dh_all), fast, s, z, c, t)
    grad_out = scatter_rows(outer(g1_all, o_all), fast, s, z, c, t).T
    hsum, dsum, fsum = (sum(mids[b][i] for b in range(seqs)) for i in (4, 5, 6))
    mid_sums = lax.psum(
        jnp.concatenate([hsum.reshape(-1), dsum.reshape(-1), fsum.reshape(-1)]), ("shard", "ctx", "tp")
    )
    hsum = mid_sums[: hsum.size].reshape(hsum.shape)
    fsum = mid_sums[hsum.size + dsum.size :].reshape(fsum.shape)
    dsum = mid_sums[hsum.size : hsum.size + dsum.size].reshape(dsum.shape)

    grad_tokens, in_sums, projs = [], 0.0, []
    for b in range(seqs):
        dq = (dqs[b].T * 0.125).astype(BF)
        proj = jnp.concatenate([dq, dkvs[b]], 1)
        projs.append(proj)
        da = sum(dot_nt(proj[:, i * n : (i + 1) * n], wqkv[i]) for i in range(3)).astype(BF)
        gt, sums = tail_call(da, swap(da, "tp"), tokens[b], g1s[b], gains[:1])
        grad_tokens.append(gt)
        in_sums = in_sums + sums
    proj = jnp.concatenate(projs)
    grad_qkv = scatter_rows(outer(jnp.concatenate(acts), proj), fast, s, z, c)
    grad_qkv = grad_qkv.reshape(-1, 3, n).transpose(1, 0, 2)
    bias_sums = jnp.sum(proj.astype(F32), 0)
    tail_sums = lax.psum(jnp.concatenate([in_sums.reshape(-1), bias_sums]), ("shard", "ctx"))
    in_sums = tail_sums[: 2 * width].reshape(2, width)
    bias_sums = tail_sums[2 * width :]

    piece = width // (lax.axis_size("shard") * lax.axis_size("ctx"))
    mine = (s * lax.axis_size("ctx") + r) * piece
    grad_gain = lax.dynamic_slice_in_dim(jnp.stack([in_sums[0], dsum[0]]), mine, piece, 1)
    grad_bias = lax.dynamic_slice_in_dim(jnp.stack([in_sums[1], dsum[1], dsum[2], dsum[3]]), mine, piece, 1)
    hsum = lax.dynamic_slice_in_dim(hsum, t * n, n, 1)
    fsum = lax.dynamic_slice_in_dim(fsum, t * ff2, ff2, 1)
    return (
        jnp.stack(outs),
        jnp.stack(grad_tokens),
        grad_qkv,
        grad_out,
        grad_up,
        grad_down,
        grad_gain,
        grad_bias,
        hsum[0],
        jnp.stack([bias_sums[:n], bias_sums[2 * n :], hsum[1]]),
        fsum[1],
        jnp.stack([fsum[0], fsum[2]]),
    )


def solution(mesh):
    in_specs = (
        P("shard", "ctx", None),
        P("shard", "ctx", None),
        P("shard", None),
        P(None, "shard", "tp"),
        P("tp", "shard"),
        P("shard", "tp"),
        P("tp", "shard"),
        P(None, "shard"),
        P(None, "shard"),
        P("tp"),
        P(None, "tp"),
        P("tp"),
        P(None, "tp"),
    )
    out_specs = (
        P("shard", "ctx", None),
        P("shard", "ctx", None),
        P(None, ("shard", "ctx"), "tp"),
        P("tp", ("shard", "ctx")),
        P(("shard", "ctx"), "tp"),
        P("tp", ("shard", "ctx")),
        P(None, ("shard", "ctx")),
        P(None, ("shard", "ctx")),
        P("tp"),
        P(None, "tp"),
        P("tp"),
        P(None, "tp"),
    )
    return jax.shard_map(
        per_device, mesh=mesh, in_specs=in_specs, out_specs=out_specs, check_vma=False
    )
```

time: 1610 us -> 610 us (0.38)
  waiting for transfers between devices: 839 us -> 61.5 us
  matrix products: 400 us -> 15.3 us
  starting transfers between devices: 0.91 us -> 121 us
  Pallas kernels: 0 us -> 112 us
  other arithmetic: 172 us -> 74.4 us
  local copies, waits for them, and re-layouts: 62.9 us -> 111 us
    dot_general x54 -> x10, matrix products: 400 us -> 15.3 us  [the longest x4 10.6 us: outer(): lax.dot_general(left, right, (((0,), (0,)), ((), ())), preferred_element_...]
    reduce_scatter x5 -> x0, waiting for transfers between devices: 348 us -> none  [the longest x1 79.3 us: per_device(): lax.psum_scatter(grad_up, ('shard', 'ctx'), scatter_dimension=0, tiled=True)]
    all_gather x5 -> x0, waiting for transfers between devices: 185 us -> none  [the longest x1 65.1 us: per_device(): lax.all_gather(own_values, 'ctx', axis=1, tiled=True)]
    psum x3 -> x0, waiting for transfers between devices: 169 us -> none  [the longest x2 118 us: tensor_sum(): return lax.psum(partial_part.astype(jnp.bfloat16), 'tp').astype(jnp.float32)]
    unnamed x19 -> x0, waiting for transfers between devices: 138 us -> none
    ppermute x0 -> x57, starting transfers between devices: none -> 121 us  [the longest x16 55.9 us: shift(): lax.ppermute(value, 'ctx', [(i, i + by) for i in range(size) if 0 <= i +...]
    pallas_call x0 -> x26, Pallas kernels: none -> 112 us  [the longest x10 40.6 us: fwd_step(): pl.pallas_call(functools.partial(fwd_kernel, w == 0, first, last, heads,...]
    reduce_sum x20 -> x4, other arithmetic: 76.8 us -> 1.94 us  [the longest x2 1.29 us: per_device(): jnp.sum(doT.reshape(heads, HD, length).astype(F32) * oT.reshape(heads, HD...]
  transfers between devices with their start and end apart: 16 -> 57, of which waited for: 16 -> 10; matrix products, arithmetic and copies ran while one was open for 6% -> 25% of each run, Pallas kernels for 0% -> 17%
where the time goes in v1:
time: 610 us; the launch traced here: 599 us
  starting transfers between devices  121 us (20%)
  Pallas kernels  112 us (18%)
  local copies, waits for them, and re-layouts  111 us (18%)
  blocking collectives  99.6 us (16%)
  other arithmetic  74.4 us (12%)
  waiting for transfers between devices  61.5 us (10%)
  matrix products  15.3 us (3%)
    psum x1, blocking collectives, per_device(): lax.psum(jnp.concatenate([in_sums.reshape(-1), bias_sums]), ('shard', 'ct...  58.6 us
    ppermute x16, starting transfers between devices, shift(): lax.ppermute(value, 'ctx', [(i, i + by) for i in range(size) if 0 <= i +...  55.9 us
    unnamed x370, local copies, waits for them, and re-layouts  45.2 us
    psum x1, blocking collectives, per_device(): lax.psum(jnp.concatenate([hsum.reshape(-1), dsum.reshape(-1), fsum.reshap...  40.9 us
    pallas_call x10, Pallas kernels, fwd_step(): pl.pallas_call(functools.partial(fwd_kernel, w == 0, first, last, heads,...  40.6 us
    pallas_call x10, Pallas kernels, bwd_step(): pl.pallas_call(functools.partial(bwd_kernel, NT, w == 0, first, w == 0, h...  37.7 us
    ppermute x25, waiting for transfers between devices, swap(): return lax.ppermute(value, axis, [(0, 1), (1, 0)])  36.9 us
    ppermute x16, starting transfers between devices, hop(): return lax.ppermute(value, 'ctx', [(i, i ^ bit) for i in range(size)])  33.4 us
  transfers between devices with their start and end apart: 57, of which 10 were waited for; matrix products, arithmetic and copies ran while one was open for 25% of the time, Pallas kernels for 17%

profile of v1, /device:TPU:0, one launch (start us, length us, event | category | flops | bytes accessed | tf_op | source)
XLA Modules:
  0.0 599.4 jit_solution(9202678592043954029)
XLA Ops:
  6.6 2.9 collective-permute-start.9
  19.1 3.2 fusion.69
  31.6 3.7 copy-done.140
  35.6 12.9 %collective-permute-done.2 = bf16[6,384]{1,0:T(8,128)(2,1)S(1)} collective-permute-done((bf16[6,384]{1,0:T(8,128)(2,1)S(1)}, bf16[6,384]{1,0:T(8,128)(2,1)S(1)}, u32[]{:S(2)}, u32[]{:S(2)}) %collective-permute-start.2) | collective-permute-done | bytes 4640 | tf_op jit(solution)/shard_map/ppermute | solution.py:433
  52.0 2.7 qkv.2
  55.6 3.0 collective-permute-start.3
  58.5 2.6 qkv.3
  62.9 3.7 collective-permute-start.17
  68.4 6.9 %attn_fwd.10 = (f32[8,512]{1,0:T(8,128)S(1)}, f32[8,512]{1,0:T(8,128)S(1)}, f32[384,512]{1,0:T(8,128)S(1)}) custom-call(s32[4]{0:T(128)S(1)} %pad_add_fusion.4.lo_sm, bf16[384,512]{1,0:T(8,128)(2,1)S(1)} %get-tuple-element.96.qT_ref, bf16[512,768]{1,0:T(8,128)(2,1)} %get-tuple-element.97.kv_ref, s32[1,512]{1,0:T(1,128)S(1)} %get-tuple-element.277.lo_ref), custom_call_target="tpu_custom_call" | custom-call | flops 402653184 | bytes 3145728 | tf_op jit(solution)/shard_map/attn_fwd/pallas_call | solution.py:85
  75.3 6.6 %attn_fwd.15 = (f32[8,512]{1,0:T(8,128)S(1)}, f32[8,512]{1,0:T(8,128)S(1)}, f32[384,512]{1,0:T(8,128)S(1)}) custom-call(s32[4]{0:T(128)S(1)} %pad_add_fusion.9.lo_sm, bf16[384,512]{1,0:T(8,128)(2,1)S(1)} %get-tuple-element.113.qT_ref, bf16[512,768]{1,0:T(8,128)(2,1)} %get-tuple-element.114.kv_ref, s32[1,512]{1,0:T(1,128)S(1)} %get-tuple-element.286.lo_ref), custom_call_target="tpu_custom_call" | custom-call | flops 402653184 | bytes 3145728 | tf_op jit(solution)/shard_map/attn_fwd/pallas_call | solution.py:85
  82.2 2.3 collective-permute-start.4
  84.5 2.4 collective-permute-start.18
  86.9 2.5 bitcast_dynamic-update-slice_fusion.6
  92.7 10.9 %collective-permute-start.5 = (bf16[512,768]{1,0:T(8,128)(2,1)S(1)}, bf16[512,768]{1,0:T(8,128)(2,1)S(1)}, u32[]{:S(2)}, u32[]{:S(2)}) collective-permute-start(bf16[512,768]{1,0:T(8,128)(2,1)S(1)} %collective-permute-done.4.kv_ref), channel_id=1, source_target_pairs={{0,2},{2,4},{4,6},{6,8},{8,10},{10,12},{12,14},{1,3},{3,5},{5,7},{... | collective-permute-start | bytes 2359304 | tf_op jit(solution)/shard_map/ppermute | solution.py:443
  103.6 8.1 %collective-permute-start.19 = (bf16[512,768]{1,0:T(8,128)(2,1)S(1)}, bf16[512,768]{1,0:T(8,128)(2,1)S(1)}, u32[]{:S(2)}, u32[]{:S(2)}) collective-permute-start(bf16[512,768]{1,0:T(8,128)(2,1)S(1)} %collective-permute-done.18.kv_ref), channel_id=1, source_target_pairs={{0,2},{2,4},{4,6},{6,8},{8,10},{10,12},{12,14},{1,3},{3,5},{5,7},{... | collective-permute-start | bytes 2359304 | tf_op jit(solution)/shard_map/ppermute | solution.py:443
  112.7 8.4 %attn_fwd.17 = (f32[8,512]{1,0:T(8,128)S(1)}, f32[8,512]{1,0:T(8,128)S(1)}, f32[384,512]{1,0:T(8,128)S(1)}) custom-call(s32[4]{0:T(128)S(1)} %get-tuple-element.297.lo_sm, bf16[384,512]{1,0:T(8,128)(2,1)S(1)} %get-tuple-element.113.qT_ref, bf16[512,768]{1,0:T(8,128)(2,1)S(1)} %collective-permute-done.18.kv_ref, s32[1,512]{1,0:T(1,128)S(1)} %get-tuple-element.282.lo_ref, ...), custom_call_target="tpu_custom_call" | custom-call | flops 402653184 | bytes 3145728 | tf_op jit(solution)/shard_map/attn_fwd/pallas_call | solution.py:85
  123.0 2.5 bitcast_dynamic-update-slice_fusion.4
  129.7 8.3 %collective-permute-start.20 = (bf16[512,768]{1,0:T(8,128)(2,1)S(1)}, bf16[512,768]{1,0:T(8,128)(2,1)S(1)}, u32[]{:S(2)}, u32[]{:S(2)}) collective-permute-start(bf16[512,768]{1,0:T(8,128)(2,1)S(1)} %collective-permute-done.19.kv_ref), channel_id=1, source_target_pairs={{0,2},{2,4},{4,6},{6,8},{8,10},{10,12},{12,14},{1,3},{3,5},{5,7},{... | collective-permute-start | bytes 2359304 | tf_op jit(solution)/shard_map/ppermute | solution.py:443
  141.4 7.5 %attn_fwd.14 = (bf16[512,384]{1,0:T(8,128)(2,1)S(1)}, f32[384,512]{1,0:T(8,128)S(1)}, f32[8,512]{1,0:T(8,128)S(1)}, f32[1,512]{1,0:T(1,128)S(1)}) custom-call(s32[4]{0:T(128)S(1)} %pad_add_fusion.lo_sm, bf16[384,512]{1,0:T(8,128)(2,1)S(1)} %get-tuple-element.96.qT_ref, bf16[512,768]{1,0:T(8,128)(2,1)S(1)} %collective-permute-done.6.kv_ref, ...), custom_call_target="tpu_custom_call" | custom-call | flops 402653184 | bytes 3145728 | tf_op jit(solution)/shard_map/attn_fwd/pallas_call | solution.py:85
  152.5 4.9 attn_fwd.19
  162.2 2.4 copy.101
  169.3 13.1 %ffn.2 = (bf16[256,768]{1,0:T(8,128)(2,1)}, bf16[256,768]{1,0:T(8,128)(2,1)S(1)}, bf16[256,768]{1,0:T(8,128)(2,1)S(1)}, bf16[256,768]{1,0:T(8,128)(2,1)S(1)}, bf...) custom-call(bf16[256,384]{1,0:T(8,128)(2,1)S(1)} %get-tuple-element., ...), custom_call_target="tpu_custom_call" | custom-call | flops 5435817984 | bytes 10616832 | tf_op jit(solution)/shard_map/ffn/pallas_call | solution.py:373
  187.6 12.0 %ffn.3 = (bf16[256,768]{1,0:T(8,128)(2,1)S(1)}, bf16[256,768]{1,0:T(8,128)(2,1)S(1)}, bf16[256,768]{1,0:T(8,128)(2,1)S(1)}, bf16[256,768]{1,0:T(8,128)(2,1)S(1)}...) custom-call(bf16[256,384]{1,0:T(8,128)(2,1)S(1)} %get-tuple-element., ...), custom_call_target="tpu_custom_call" | custom-call | flops 5435817984 | bytes 10616832 | tf_op jit(solution)/shard_map/ffn/pallas_call | solution.py:373
  206.7 40.9 %psum.15 = f32[13824]{0:T(1024)S(1)} all-reduce(f32[13824]{0:T(1024)S(1)} %pad_maximum_fusion.7), channel_id=1, replica_groups=mesh['shard'=2,'ctx'=8,'tp'=2] {'shard','ctx','tp'}, use_global_device_ids=true, to_apply=%region_5.6 | all-reduce | flops 13824 | bytes 110592 | tf_op jit(solution)/shard_map/psum | solution.py:638
  247.8 2.3 collective-permute-start.30
  250.8 2.0 collective-permute-start.37
  253.6 4.7 convolution_convert_fusion
  262.9 2.9 convolution_convert_fusion.1
  284.5 2.2 attn_bwd.10
  287.6 2.3 copy.102
  305.9 2.5 reshape.251
  308.5 2.4 constant_dynamic-slice_fusion.13
  316.8 3.8 collective-permute-done.43
  320.7 2.2 collective-permute-start.44
  323.9 2.0 attn_bwd.11
  327.3 7.7 %collective-permute-start.45 = (bf16[2,48,384]{2,1,0:T(8,128)(2,1)S(1)}, bf16[2,48,384]{2,1,0:T(8,128)(2,1)S(1)}, u32[]{:S(2)}, u32[]{:S(2)}) collective-permute-start(bf16[2,48,384]{2,1,0:T(8,128)(2,1)S(1)} %dynamic-slice_bitcast_fusion.15), channel_id=1, source_target_pairs={{0,8},{2,10},{4,12},{6,14},{8,0},{10,2},{12,4},{14,6},{1,9},{3,11}... | collective-permute-start | bytes 221192 | tf_op jit(solution)/shard_map/ppermute | solution.py:438
  337.9 9.9 %collective-permute-done.45 = bf16[2,48,384]{2,1,0:T(8,128)(2,1)S(1)} collective-permute-done((bf16[2,48,384]{2,1,0:T(8,128)(2,1)S(1)}, bf16[2,48,384]{2,1,0:T(8,128)(2,1)S(1)}, u32[]{:S(2)}, u32[]{:S(2)}) %collective-permute-start.45) | collective-permute-done | bytes 73760 | tf_op jit(solution)/shard_map/ppermute | solution.py:438
  348.9 3.0 collective-permute-done.46
  352.6 2.5 attn_bwd.12
  357.3 9.0 %attn_bwd.17 = (f32[384,512]{1,0:T(8,128)S(1)}, bf16[512,768]{1,0:T(8,128)(2,1)}) custom-call(s32[4]{0:T(128)S(1)} %copy-done.101, bf16[384,512]{1,0:T(8,128)(2,1)S(1)} %copy-done.7, bf16[512,384]{1,0:T(8,128)(2,1)S(1)} %copy-done.2, bf16[384,512]{1,0:T(8,128)(2,1)S(1)} %copy.107.doT_ref, bf16[512,384]{1,0:T(8,128)(2,1)S(1)} %get-tuple-element.250.do_ref, ...), custom_call_target="tpu_custom_call" | custom-call | flops 1006632960 | bytes 6291456 | tf_op jit(solution)/shard_map/attn_bwd/pallas_call | solution.py:175
  368.5 4.7 fusion
  373.2 6.5 %reshape.257 = bf16[2,4,48,2,1536]{4,3,2,1,0:T(2,128)(2,1)} reshape(bf16[2,4,48,3072]{3,2,1,0:T(8,128)(2,1)} %fusion) | data formatting | bytes 4718592 | tf_op jit(solution)/shard_map/reshape | solution.py:507
  379.7 8.8 %constant_dynamic-slice_fusion.9 = (bf16[2,4,48,1,1536]{4,3,2,1,0:T(2,128)(2,1)S(1)}, f32[2,4,48,1,1536]{4,3,2,1,0:T(1,128)}) fusion(bf16[2,4,48,2,1536]{4,3,2,1,0:T(2,128)(2,1)} %reshape.257, s32[]{:T(128)S(6)} %select_n.320, s32[]{:T(128)S(6)} %select_n.319), kind=kLoop, calls=%fused_computation.157 | loop fusion | flops 589824 | bytes 5898248 | tf_op jit(solution)/shard_map/jit(dynamic_index_in_dim)/dynamic_slice | solution.py:489
  390.6 3.0 attn_bwd.13
  394.5 6.3 %collective-permute-start.28 = (bf16[512,768]{1,0:T(8,128)(2,1)}, bf16[512,768]{1,0:T(8,128)(2,1)}, u32[]{:S(2)}, u32[]{:S(2)}) collective-permute-start(bf16[512,768]{1,0:T(8,128)(2,1)} %get-tuple-element.141), channel_id=1, source_target_pairs={{2,0},{4,2},{6,4},{8,6},{10,8},{12,10},{14,12},{3,1},{5,3},{7,5},{... | collective-permute-start | bytes 2359304 | tf_op jit(solution)/shard_map/ppermute | solution.py:443
  400.7 4.8 fusion.1
  405.6 6.5 %reshape.254 = bf16[2,4,48,2,1536]{4,3,2,1,0:T(2,128)(2,1)} reshape(bf16[2,4,48,3072]{3,2,1,0:T(8,128)(2,1)} %fusion.1) | data formatting | bytes 4718592 | tf_op jit(solution)/shard_map/reshape | solution.py:507
  412.1 8.7 %constant_dynamic-slice_fusion.11 = (bf16[2,4,48,1,1536]{4,3,2,1,0:T(2,128)(2,1)S(1)}, f32[2,4,48,1,1536]{4,3,2,1,0:T(1,128)}) fusion(bf16[2,4,48,2,1536]{4,3,2,1,0:T(2,128)(2,1)} %reshape.254, s32[]{:T(128)S(6)} %select_n.320, s32[]{:T(128)S(6)} %select_n.319), kind=kLoop, calls=%fused_computation.159 | loop fusion | flops 589824 | bytes 5898248 | tf_op jit(solution)/shard_map/jit(dynamic_index_in_dim)/dynamic_slice | solution.py:489
  423.4 3.1 attn_bwd.18
  428.8 6.6 %attn_bwd.14 = (f32[384,512]{1,0:T(8,128)S(1)}, bf16[512,768]{1,0:T(8,128)(2,1)S(1)}) custom-call(s32[4]{0:T(128)S(1)} %copy-done.111, bf16[384,512]{1,0:T(8,128)(2,1)S(1)} %copy-done.18, bf16[512,384]{1,0:T(8,128)(2,1)S(1)} %copy-done.13, bf16[384,512]{1,0:T(8,128)(2,1)S(1)} %copy.99.doT_ref, bf16[512,384]{1,0:T(8,128)(2,1)S(1)} %get-tuple-element.248.do_ref, ...), custom_call_target="tpu_custom_call" | custom-call | flops 1006632960 | bytes 6291456 | tf_op jit(solution)/shard_map/attn_bwd/pallas_call | solution.py:175
  443.0 6.6 %attn_bwd.19 = (f32[384,512]{1,0:T(8,128)S(1)}, bf16[512,768]{1,0:T(8,128)(2,1)S(1)}) custom-call(s32[4]{0:T(128)S(1)} %copy-done.109, bf16[384,512]{1,0:T(8,128)(2,1)S(1)} %copy-done.9, bf16[512,384]{1,0:T(8,128)(2,1)S(1)} %copy-done.4, bf16[384,512]{1,0:T(8,128)(2,1)S(1)} %copy.107.doT_ref, bf16[512,384]{1,0:T(8,128)(2,1)S(1)} %get-tuple-element.250.do_ref, ...), custom_call_target="tpu_custom_call" | custom-call | flops 1006632960 | bytes 6291456 | tf_op jit(solution)/shard_map/attn_bwd/pallas_call | solution.py:175
  457.3 2.2 convolution_convert_fusion.2
  460.6 9.0 %collective-permute-start.38 = (bf16[2,4,48,1152]{3,2,1,0:T(8,128)(2,1)}, bf16[2,4,48,1152]{3,2,1,0:T(8,128)(2,1)}, u32[]{:S(2)}, u32[]{:S(2)}) collective-permute-start(bf16[2,4,48,1152]{3,2,1,0:T(8,128)(2,1)} %dynamic-slice_bitcast_fusion.2), channel_id=1, source_target_pairs={{0,2},{2,0},{4,6},{6,4},{8,10},{10,8},{12,14},{14,12},{1,3},{3,1},... | collective-permute-start | bytes 2654216 | tf_op jit(solution)/shard_map/ppermute | solution.py:438
  471.9 3.2 collective-permute-start.54
  477.0 11.9 %collective-permute-done.54 = bf16[4,48,1536]{2,1,0:T(8,128)(2,1)S(1)} collective-permute-done((bf16[4,48,1536]{2,1,0:T(8,128)(2,1)S(1)}, bf16[4,48,1536]{2,1,0:T(8,128)(2,1)S(1)}, u32[]{:S(2)}, u32[]{:S(2)}) %collective-permute-start.54) | collective-permute-done | bytes 589856 | tf_op jit(solution)/shard_map/ppermute | solution.py:433
  489.8 6.0 %collective-permute-start.55 = (bf16[2,48,1536]{2,1,0:T(8,128)(2,1)}, bf16[2,48,1536]{2,1,0:T(8,128)(2,1)}, u32[]{:S(2)}, u32[]{:S(2)}) collective-permute-start(bf16[2,48,1536]{2,1,0:T(8,128)(2,1)} %dynamic-slice_bitcast_fusion.11), channel_id=1, source_target_pairs={{0,8},{2,10},{4,12},{6,14},{8,0},{10,2},{12,4},{14,6},{1,9},{3,11}... | collective-permute-start | bytes 884744 | tf_op jit(solution)/shard_map/ppermute | solution.py:438
  495.8 5.7 collective-permute-done.49
  502.4 6.0 %collective-permute-start.50 = (bf16[2,48,1536]{2,1,0:T(8,128)(2,1)}, bf16[2,48,1536]{2,1,0:T(8,128)(2,1)}, u32[]{:S(2)}, u32[]{:S(2)}) collective-permute-start(bf16[2,48,1536]{2,1,0:T(8,128)(2,1)} %dynamic-slice_bitcast_fusion.12), channel_id=1, source_target_pairs={{0,8},{2,10},{4,12},{6,14},{8,0},{10,2},{12,4},{14,6},{1,9},{3,11}... | collective-permute-start | bytes 884744 | tf_op jit(solution)/shard_map/ppermute | solution.py:438
  508.4 2.5 tail.2
  512.3 58.6 %psum.14 = f32[2688]{0:T(1024)S(1)} all-reduce(f32[2688]{0:T(1024)S(1)} %pad_maximum_fusion.9), channel_id=1, replica_groups=mesh['shard'=2,'ctx'=8,'tp'=2] {'shard','ctx'}, use_global_device_ids=true, to_apply=%region_4.5 | all-reduce | flops 2688 | bytes 21504 | tf_op jit(solution)/shard_map/psum | solution.py:658
  579.7 2.1 collective-permute-start.51
  581.7 2.6 collective-permute-done.39
  585.3 7.8 %collective-permute-done.40 = bf16[2,48,1152]{2,1,0:T(8,128)(2,1)S(1)} collective-permute-done((bf16[2,48,1152]{2,1,0:T(8,128)(2,1)S(1)}, bf16[2,48,1152]{2,1,0:T(8,128)(2,1)S(1)}, u32[]{:S(2)}, u32[]{:S(2)}) %collective-permute-start.40) | collective-permute-done | bytes 221216 | tf_op jit(solution)/shard_map/ppermute | solution.py:438
  595.2 2.9 collective-permute-done.41
  (652 shorter events, 173.8 us)
Async XLA Ops:
  6.6 60.1 %collective-permute-start.9 = (bf16[192,3456]{1,0:T(8,128)(2,1)}, bf16[192,3456]{1,0:T(8,128)(2,1)}, u32[]{:S(2)}, u32[]{:S(2)}) collective-permute-start(bf16[192,3456]{1,0:T(8,128)(2,1)} %constant_dynamic-slice_fusion.20), channel_id=1, source_target_pairs={{0,16},{16,0},{1,17},{17,1},{2,18},{18,2},{3,19},{19,3},{4,20},{20... | collective-permute-start | bytes 3981320 | tf_op jit(solution)/shard_map/ppermute | solution.py:433
  9.5 72.4 %collective-permute-start.11 = (bf16[192,3456]{1,0:T(8,128)(2,1)}, bf16[192,3456]{1,0:T(8,128)(2,1)}, u32[]{:S(2)}, u32[]{:S(2)}) collective-permute-start(bf16[192,3456]{1,0:T(8,128)(2,1)} %constant_dynamic-slice_fusion.20), channel_id=1, source_target_pairs={{0,1},{1,0},{2,3},{3,2},{4,5},{5,4},{6,7},{7,6},{8,9},{9,8},{10,11... | collective-permute-start | bytes 3981320 | tf_op jit(solution)/shard_map/ppermute | solution.py:433
  13.9 34.7 %collective-permute-start = (bf16[3,192,384]{2,1,0:T(8,128)(2,1)}, bf16[3,192,384]{2,1,0:T(8,128)(2,1)}, u32[]{:S(2)}, u32[]{:S(2)}) collective-permute-start(bf16[3,192,384]{2,1,0:T(8,128)(2,1)} %constant_dynamic-slice_fusion.24), channel_id=1, source_target_pairs={{0,16},{16,0},{1,17},{17,1},{2,18},{18,2},{3,19},{19,3},{4,20},{20... | collective-permute-start | bytes 1327112 | tf_op jit(solution)/shard_map/ppermute | solution.py:433
  14.5 34.1 %collective-permute-start.2 = (bf16[6,384]{1,0:T(8,128)(2,1)S(1)}, bf16[6,384]{1,0:T(8,128)(2,1)S(1)}, u32[]{:S(2)}, u32[]{:S(2)}) collective-permute-start(bf16[6,384]{1,0:T(8,128)(2,1)S(1)} %pad_maximum_fusion.12), channel_id=1, source_target_pairs={{0,16},{16,0},{1,17},{17,1},{2,18},{18,2},{3,19},{19,3},{4,20},{20... | collective-permute-start | bytes 13832 | tf_op jit(solution)/shard_map/ppermute | solution.py:433
  16.2 32.5 %collective-permute-start.15 = (f32[5376]{0:T(1024)S(1)}, f32[5376]{0:T(1024)S(1)}, u32[]{:S(2)}, u32[]{:S(2)}) collective-permute-start(f32[5376]{0:T(1024)S(1)} %constant_dynamic-update-slice_fusion.9), channel_id=1, source_target_pairs={{0,1},{1,0},{2,3},{3,2},{4,5},{5,4},{6,7},{7,6},{8,9},{9,8},{10,11... | collective-permute-start | bytes 64520 | tf_op jit(solution)/shard_map/ppermute | solution.py:433
  17.2 120.8 %copy-start.90 = (s32[1,512]{1,0:T(1,128)}, s32[1,512]{1,0:T(1,128)S(1)}, u32[]{:S(2)}) copy-start(s32[1,512]{1,0:T(1,128)S(1)} %get-tuple-element.278.lo_ref) | copy-start | bytes 6148
  17.2 122.1 %copy-start.88 = (s32[1,512]{1,0:T(1,128)}, s32[1,512]{1,0:T(1,128)S(1)}, u32[]{:S(2)}) copy-start(s32[1,512]{1,0:T(1,128)S(1)} %get-tuple-element.281.lo_ref) | copy-start | bytes 6148
  17.2 124.2 %copy-start.98 = (s32[1,512]{1,0:T(1,128)}, s32[1,512]{1,0:T(1,128)S(1)}, u32[]{:S(2)}) copy-start(s32[1,512]{1,0:T(1,128)S(1)} %get-tuple-element.285.lo_ref) | copy-start | bytes 6148
  17.2 135.3 %copy-start.96 = (s32[1,512]{1,0:T(1,128)}, s32[1,512]{1,0:T(1,128)S(1)}, u32[]{:S(2)}) copy-start(s32[1,512]{1,0:T(1,128)S(1)} %get-tuple-element.284.lo_ref) | copy-start | bytes 6148
  29.1 112.3 %copy-start.122 = (s32[4]{0:T(128)}, s32[4]{0:T(128)S(1)}, u32[]{:S(2)}) copy-start(s32[4]{0:T(128)S(1)} %pad_add_fusion.lo_sm) | copy-start | bytes 52
  35.4 117.1 %copy-start.124 = (s32[4]{0:T(128)}, s32[4]{0:T(128)S(1)}, u32[]{:S(2)}) copy-start(s32[4]{0:T(128)S(1)} %pad_add_fusion.5.lo_sm) | copy-start | bytes 52
  48.6 2.1 collective-permute-start.1
  55.6 228.9 %copy-start.10 = (bf16[512,384]{1,0:T(8,128)(2,1)}, bf16[512,384]{1,0:T(8,128)(2,1)S(1)}, u32[]{:S(2)}) copy-start(bf16[512,384]{1,0:T(8,128)(2,1)S(1)} %get-tuple-element.130.q_ref) | copy-start | bytes 1179652
  55.6 26.6 %collective-permute-start.3 = (bf16[512,768]{1,0:T(8,128)(2,1)}, bf16[512,768]{1,0:T(8,128)(2,1)}, u32[]{:S(2)}, u32[]{:S(2)}) collective-permute-start(bf16[512,768]{1,0:T(8,128)(2,1)} %get-tuple-element.97.kv_ref), channel_id=1, source_target_pairs={{0,2},{2,4},{4,6},{6,8},{8,10},{10,12},{12,14},{1,3},{3,5},{5,7},{... | collective-permute-start | bytes 2359304 | tf_op jit(solution)/shard_map/ppermute | solution.py:443
  62.9 21.6 %collective-permute-start.17 = (bf16[512,768]{1,0:T(8,128)(2,1)}, bf16[512,768]{1,0:T(8,128)(2,1)}, u32[]{:S(2)}, u32[]{:S(2)}) collective-permute-start(bf16[512,768]{1,0:T(8,128)(2,1)} %get-tuple-element.114.kv_ref), channel_id=1, source_target_pairs={{0,2},{2,4},{4,6},{6,8},{8,10},{10,12},{12,14},{1,3},{3,5},{5,7},{... | collective-permute-start | bytes 2359304 | tf_op jit(solution)/shard_map/ppermute | solution.py:443
  66.7 55.0 %collective-permute-start.10 = (bf16[192,3456]{1,0:T(8,128)(2,1)}, bf16[192,3456]{1,0:T(8,128)(2,1)S(1)}, u32[]{:S(2)}, u32[]{:S(2)}) collective-permute-start(bf16[192,3456]{1,0:T(8,128)(2,1)} %collective-permute-done.9), channel_id=1, source_target_pairs={{0,2},{2,0},{4,6},{6,4},{8,10},{10,8},{12,14},{14,12},{1,3},{3,1},... | collective-permute-start | bytes 3981320 | tf_op jit(solution)/shard_map/ppermute | solution.py:438
  66.8 54.3 %collective-permute-start.13 = (bf16[192,3456]{1,0:T(8,128)(2,1)}, bf16[192,3456]{1,0:T(8,128)(2,1)S(1)}, u32[]{:S(2)}, u32[]{:S(2)}) collective-permute-start(bf16[192,3456]{1,0:T(8,128)(2,1)} %collective-permute-done.9), channel_id=1, source_target_pairs={{0,1},{1,0},{2,3},{3,2},{4,5},{5,4},{6,7},{7,6},{8,9},{9,8},{10,11... | collective-permute-start | bytes 3981320 | tf_op jit(solution)/shard_map/ppermute | solution.py:433
  81.9 43.5 %collective-permute-start.12 = (bf16[192,3456]{1,0:T(8,128)(2,1)}, bf16[192,3456]{1,0:T(8,128)(2,1)S(1)}, u32[]{:S(2)}, u32[]{:S(2)}) collective-permute-start(bf16[192,3456]{1,0:T(8,128)(2,1)} %collective-permute-done.11), channel_id=1, source_target_pairs={{0,2},{2,0},{4,6},{6,4},{8,10},{10,8},{12,14},{14,12},{1,3},{3,1},... | collective-permute-start | bytes 3981320 | tf_op jit(solution)/shard_map/ppermute | solution.py:438
  82.2 10.5 %collective-permute-start.4 = (bf16[512,768]{1,0:T(8,128)(2,1)}, bf16[512,768]{1,0:T(8,128)(2,1)S(1)}, u32[]{:S(2)}, u32[]{:S(2)}) collective-permute-start(bf16[512,768]{1,0:T(8,128)(2,1)} %collective-permute-done.3.kv_ref), channel_id=1, source_target_pairs={{0,2},{2,4},{4,6},{6,8},{8,10},{10,12},{12,14},{1,3},{3,5},{5,7},{... | collective-permute-start | bytes 2359304 | tf_op jit(solution)/shard_map/ppermute | solution.py:443
  84.5 19.1 %collective-permute-start.18 = (bf16[512,768]{1,0:T(8,128)(2,1)}, bf16[512,768]{1,0:T(8,128)(2,1)S(1)}, u32[]{:S(2)}, u32[]{:S(2)}) collective-permute-start(bf16[512,768]{1,0:T(8,128)(2,1)} %collective-permute-done.17.kv_ref), channel_id=1, source_target_pairs={{0,2},{2,4},{4,6},{6,8},{8,10},{10,12},{12,14},{1,3},{3,5},{5,7},{... | collective-permute-start | bytes 2359304 | tf_op jit(solution)/shard_map/ppermute | solution.py:443
  92.7 35.2 %collective-permute-start.5 = (bf16[512,768]{1,0:T(8,128)(2,1)S(1)}, bf16[512,768]{1,0:T(8,128)(2,1)S(1)}, u32[]{:S(2)}, u32[]{:S(2)}) collective-permute-start(bf16[512,768]{1,0:T(8,128)(2,1)S(1)} %collective-permute-done.4.kv_ref), channel_id=1, source_target_pairs={{0,2},{2,4},{4,6},{6,8},{8,10},{10,12},{12,14},{1,3},{3,5},{5,7},{... | collective-permute-start | bytes 2359304 | tf_op jit(solution)/shard_map/ppermute | solution.py:443
  103.6 26.1 %collective-permute-start.19 = (bf16[512,768]{1,0:T(8,128)(2,1)S(1)}, bf16[512,768]{1,0:T(8,128)(2,1)S(1)}, u32[]{:S(2)}, u32[]{:S(2)}) collective-permute-start(bf16[512,768]{1,0:T(8,128)(2,1)S(1)} %collective-permute-done.18.kv_ref), channel_id=1, source_target_pairs={{0,2},{2,4},{4,6},{6,8},{8,10},{10,12},{12,14},{1,3},{3,5},{5,7},{... | collective-permute-start | bytes 2359304 | tf_op jit(solution)/shard_map/ppermute | solution.py:443
  121.1 19.1 %collective-permute-start.14 = (bf16[192,3456]{1,0:T(8,128)(2,1)S(1)}, bf16[192,3456]{1,0:T(8,128)(2,1)S(1)}, u32[]{:S(2)}, u32[]{:S(2)}) collective-permute-start(bf16[192,3456]{1,0:T(8,128)(2,1)S(1)} %collective-permute-done.13), channel_id=1, source_target_pairs={{0,2},{2,0},{4,6},{6,4},{8,10},{10,8},{12,14},{14,12},{1,3},{3,1},... | collective-permute-start | bytes 3981320 | tf_op jit(solution)/shard_map/ppermute | solution.py:438
  127.9 13.5 %collective-permute-start.6 = (bf16[512,768]{1,0:T(8,128)(2,1)S(1)}, bf16[512,768]{1,0:T(8,128)(2,1)S(1)}, u32[]{:S(2)}, u32[]{:S(2)}) collective-permute-start(bf16[512,768]{1,0:T(8,128)(2,1)S(1)} %collective-permute-done.5.kv_ref), channel_id=1, source_target_pairs={{0,2},{2,4},{4,6},{6,8},{8,10},{10,12},{12,14},{1,3},{3,5},{5,7},{... | collective-permute-start | bytes 2359304 | tf_op jit(solution)/shard_map/ppermute | solution.py:443
  129.7 22.8 %collective-permute-start.20 = (bf16[512,768]{1,0:T(8,128)(2,1)S(1)}, bf16[512,768]{1,0:T(8,128)(2,1)S(1)}, u32[]{:S(2)}, u32[]{:S(2)}) collective-permute-start(bf16[512,768]{1,0:T(8,128)(2,1)S(1)} %collective-permute-done.19.kv_ref), channel_id=1, source_target_pairs={{0,2},{2,4},{4,6},{6,8},{8,10},{10,12},{12,14},{1,3},{3,5},{5,7},{... | collective-permute-start | bytes 2359304 | tf_op jit(solution)/shard_map/ppermute | solution.py:443
  149.7 14.8 %collective-permute-start.8 = (f32[256]{0:T(256)S(1)}, f32[256]{0:T(256)S(1)}, u32[]{:S(2)}, u32[]{:S(2)}) collective-permute-start(f32[256]{0:T(256)S(1)} %bitcast.259), channel_id=1, source_target_pairs={{0,1},{1,0},{2,3},{3,2},{4,5},{5,4},{6,7},{7,6},{8,9},{9,8},{10,11... | collective-permute-start | bytes 3080 | tf_op jit(solution)/shard_map/ppermute | solution.py:433
  150.7 14.8 %collective-permute-start.7 = (bf16[256,384]{1,0:T(8,128)(2,1)}, bf16[256,384]{1,0:T(8,128)(2,1)}, u32[]{:S(2)}, u32[]{:S(2)}) collective-permute-start(bf16[256,384]{1,0:T(8,128)(2,1)} %constant_dynamic-slice_fusion.23), channel_id=1, source_target_pairs={{0,1},{1,0},{2,3},{3,2},{4,5},{5,4},{6,7},{7,6},{8,9},{9,8},{10,11... | collective-permute-start | bytes 589832 | tf_op jit(solution)/shard_map/ppermute | solution.py:433
  158.3 7.1 %collective-permute-start.22 = (f32[256]{0:T(256)S(1)}, f32[256]{0:T(256)S(1)}, u32[]{:S(2)}, u32[]{:S(2)}) collective-permute-start(f32[256]{0:T(256)S(1)} %bitcast.260), channel_id=1, source_target_pairs={{0,1},{1,0},{2,3},{3,2},{4,5},{5,4},{6,7},{7,6},{8,9},{9,8},{10,11... | collective-permute-start | bytes 3080 | tf_op jit(solution)/shard_map/ppermute | solution.py:433
  159.7 25.3 %collective-permute-start.21 = (bf16[256,384]{1,0:T(8,128)(2,1)}, bf16[256,384]{1,0:T(8,128)(2,1)}, u32[]{:S(2)}, u32[]{:S(2)}) collective-permute-start(bf16[256,384]{1,0:T(8,128)(2,1)} %constant_dynamic-slice_fusion.19), channel_id=1, source_target_pairs={{0,1},{1,0},{2,3},{3,2},{4,5},{5,4},{6,7},{7,6},{8,9},{9,8},{10,11... | collective-permute-start | bytes 589832 | tf_op jit(solution)/shard_map/ppermute | solution.py:433
  247.8 54.0 %collective-permute-start.30 = (bf16[256,768]{1,0:T(8,128)(2,1)}, bf16[256,768]{1,0:T(8,128)(2,1)}, u32[]{:S(2)}, u32[]{:S(2)}) collective-permute-start(bf16[256,768]{1,0:T(8,128)(2,1)} %copy-done.66), channel_id=1, source_target_pairs={{0,1},{1,0},{2,3},{3,2},{4,5},{5,4},{6,7},{7,6},{8,9},{9,8},{10,11... | collective-permute-start | bytes 1179656 | tf_op jit(solution)/shard_map/ppermute | solution.py:433
  250.8 21.5 %collective-permute-start.24 = (bf16[256,384]{1,0:T(8,128)(2,1)}, bf16[256,384]{1,0:T(8,128)(2,1)}, u32[]{:S(2)}, u32[]{:S(2)}) collective-permute-start(bf16[256,384]{1,0:T(8,128)(2,1)} %constant_dynamic-slice_fusion.16), channel_id=1, source_target_pairs={{0,1},{1,0},{2,3},{3,2},{4,5},{5,4},{6,7},{7,6},{8,9},{9,8},{10,11... | collective-permute-start | bytes 589832 | tf_op jit(solution)/shard_map/ppermute | solution.py:433
  250.8 63.4 %collective-permute-start.37 = (bf16[256,768]{1,0:T(8,128)(2,1)}, bf16[256,768]{1,0:T(8,128)(2,1)}, u32[]{:S(2)}, u32[]{:S(2)}) collective-permute-start(bf16[256,768]{1,0:T(8,128)(2,1)} %copy-done.63), channel_id=1, source_target_pairs={{0,1},{1,0},{2,3},{3,2},{4,5},{5,4},{6,7},{7,6},{8,9},{9,8},{10,11... | collective-permute-start | bytes 1179656 | tf_op jit(solution)/shard_map/ppermute | solution.py:433
  253.5 28.0 %collective-permute-start.31 = (bf16[256,384]{1,0:T(8,128)(2,1)}, bf16[256,384]{1,0:T(8,128)(2,1)}, u32[]{:S(2)}, u32[]{:S(2)}) collective-permute-start(bf16[256,384]{1,0:T(8,128)(2,1)} %constant_dynamic-slice_fusion.15), channel_id=1, source_target_pairs={{0,1},{1,0},{2,3},{3,2},{4,5},{5,4},{6,7},{7,6},{8,9},{9,8},{10,11... | collective-permute-start | bytes 589832 | tf_op jit(solution)/shard_map/ppermute | solution.py:433
  261.8 106.7 %collective-permute-start.52 = (bf16[2,4,48,3072]{3,2,1,0:T(8,128)(2,1)}, bf16[2,4,48,3072]{3,2,1,0:T(8,128)(2,1)}, u32[]{:S(2)}, u32[]{:S(2)}) collective-permute-start(bf16[2,4,48,3072]{3,2,1,0:T(8,128)(2,1)} %dynamic-slice_bitcast_fusion), channel_id=1, source_target_pairs={{0,2},{2,0},{4,6},{6,4},{8,10},{10,8},{12,14},{14,12},{1,3},{3,1},... | collective-permute-start | bytes 7077896 | tf_op jit(solution)/shard_map/ppermute | solution.py:438
  272.3 24.6 %collective-permute-start.16 = (bf16[256,768]{1,0:T(8,128)(2,1)}, bf16[256,768]{1,0:T(8,128)(2,1)}, u32[]{:S(2)}, u32[]{:S(2)}) collective-permute-start(bf16[256,768]{1,0:T(8,128)(2,1)} %get-tuple-element.112), channel_id=1, source_target_pairs={{0,1},{1,0},{2,3},{3,2},{4,5},{5,4},{6,7},{7,6},{8,9},{9,8},{10,11... | collective-permute-start | bytes 1179656 | tf_op jit(solution)/shard_map/ppermute | solution.py:433
  281.5 17.1 %collective-permute-start.23 = (bf16[256,768]{1,0:T(8,128)(2,1)}, bf16[256,768]{1,0:T(8,128)(2,1)}, u32[]{:S(2)}, u32[]{:S(2)}) collective-permute-start(bf16[256,768]{1,0:T(8,128)(2,1)} %copy-done.69), channel_id=1, source_target_pairs={{0,1},{1,0},{2,3},{3,2},{4,5},{5,4},{6,7},{7,6},{8,9},{9,8},{10,11... | collective-permute-start | bytes 1179656 | tf_op jit(solution)/shard_map/ppermute | solution.py:433
  296.9 103.8 %collective-permute-start.47 = (bf16[2,4,48,3072]{3,2,1,0:T(8,128)(2,1)}, bf16[2,4,48,3072]{3,2,1,0:T(8,128)(2,1)}, u32[]{:S(2)}, u32[]{:S(2)}) collective-permute-start(bf16[2,4,48,3072]{3,2,1,0:T(8,128)(2,1)} %dynamic-slice_bitcast_fusion.1), channel_id=1, source_target_pairs={{0,2},{2,0},{4,6},{6,4},{8,10},{10,8},{12,14},{14,12},{1,3},{3,1},... | collective-permute-start | bytes 7077896 | tf_op jit(solution)/shard_map/ppermute | solution.py:438
  298.7 6.3 %collective-permute-start.42 = (bf16[2,4,48,768]{3,2,1,0:T(8,128)(2,1)S(1)}, bf16[2,4,48,768]{3,2,1,0:T(8,128)(2,1)S(1)}, u32[]{:S(2)}, u32[]{:S(2)}) collective-permute-start(bf16[2,4,48,768]{3,2,1,0:T(8,128)(2,1)S(1)} %copy-done.169), channel_id=1, source_target_pairs={{0,2},{2,0},{4,6},{6,4},{8,10},{10,8},{12,14},{14,12},{1,3},{3,1},... | collective-permute-start | bytes 1769480 | tf_op jit(solution)/shard_map/ppermute | solution.py:438
  301.7 22.1 %collective-permute-start.25 = (bf16[512,768]{1,0:T(8,128)(2,1)}, bf16[512,768]{1,0:T(8,128)(2,1)}, u32[]{:S(2)}, u32[]{:S(2)}) collective-permute-start(bf16[512,768]{1,0:T(8,128)(2,1)} %get-tuple-element.135), channel_id=1, source_target_pairs={{2,0},{4,2},{6,4},{8,6},{10,8},{12,10},{14,12},{3,1},{5,3},{7,5},{... | collective-permute-start | bytes 2359304 | tf_op jit(solution)/shard_map/ppermute | solution.py:443
  311.0 9.6 %collective-permute-start.43 = (bf16[2,4,48,384]{3,2,1,0:T(8,128)(2,1)S(1)}, bf16[2,4,48,384]{3,2,1,0:T(8,128)(2,1)S(1)}, u32[]{:S(2)}, u32[]{:S(2)}) collective-permute-start(bf16[2,4,48,384]{3,2,1,0:T(8,128)(2,1)S(1)} %bitcast.254), channel_id=1, source_target_pairs={{0,1},{1,0},{2,3},{3,2},{4,5},{5,4},{6,7},{7,6},{8,9},{9,8},{10,11... | collective-permute-start | bytes 884744 | tf_op jit(solution)/shard_map/ppermute | solution.py:433
  314.3 20.8 %collective-permute-start.32 = (bf16[512,768]{1,0:T(8,128)(2,1)S(1)}, bf16[512,768]{1,0:T(8,128)(2,1)S(1)}, u32[]{:S(2)}, u32[]{:S(2)}) collective-permute-start(bf16[512,768]{1,0:T(8,128)(2,1)S(1)} %copy-done.121), channel_id=1, source_target_pairs={{2,0},{4,2},{6,4},{8,6},{10,8},{12,10},{14,12},{3,1},{5,3},{7,5},{... | collective-permute-start | bytes 2359304 | tf_op jit(solution)/shard_map/ppermute | solution.py:443
  320.7 6.5 %collective-permute-start.44 = (bf16[4,48,384]{2,1,0:T(8,128)(2,1)S(1)}, bf16[4,48,384]{2,1,0:T(8,128)(2,1)S(1)}, u32[]{:S(2)}, u32[]{:S(2)}) collective-permute-start(bf16[4,48,384]{2,1,0:T(8,128)(2,1)S(1)} %dynamic-slice_bitcast_fusion.14), channel_id=1, source_target_pairs={{0,16},{16,0},{1,17},{17,1},{2,18},{18,2},{3,19},{19,3},{4,20},{20... | collective-permute-start | bytes 442376 | tf_op jit(solution)/shard_map/ppermute | solution.py:433
  325.9 26.6 %collective-permute-start.26 = (bf16[512,768]{1,0:T(8,128)(2,1)S(1)}, bf16[512,768]{1,0:T(8,128)(2,1)S(1)}, u32[]{:S(2)}, u32[]{:S(2)}) collective-permute-start(bf16[512,768]{1,0:T(8,128)(2,1)S(1)} %get-tuple-element.137), channel_id=1, source_target_pairs={{2,0},{4,2},{6,4},{8,6},{10,8},{12,10},{14,12},{3,1},{5,3},{7,5},{... | collective-permute-start | bytes 2359304 | tf_op jit(solution)/shard_map/ppermute | solution.py:443
  327.3 20.5 %collective-permute-start.45 = (bf16[2,48,384]{2,1,0:T(8,128)(2,1)S(1)}, bf16[2,48,384]{2,1,0:T(8,128)(2,1)S(1)}, u32[]{:S(2)}, u32[]{:S(2)}) collective-permute-start(bf16[2,48,384]{2,1,0:T(8,128)(2,1)S(1)} %dynamic-slice_bitcast_fusion.15), channel_id=1, source_target_pairs={{0,8},{2,10},{4,12},{6,14},{8,0},{10,2},{12,4},{14,6},{1,9},{3,11}... | collective-permute-start | bytes 221192 | tf_op jit(solution)/shard_map/ppermute | solution.py:438
  336.5 20.8 %collective-permute-start.33 = (bf16[512,768]{1,0:T(8,128)(2,1)S(1)}, bf16[512,768]{1,0:T(8,128)(2,1)S(1)}, u32[]{:S(2)}, u32[]{:S(2)}) collective-permute-start(bf16[512,768]{1,0:T(8,128)(2,1)S(1)} %get-tuple-element.153), channel_id=1, source_target_pairs={{2,0},{4,2},{6,4},{8,6},{10,8},{12,10},{14,12},{3,1},{5,3},{7,5},{... | collective-permute-start | bytes 2359304 | tf_op jit(solution)/shard_map/ppermute | solution.py:443
  347.8 4.1 collective-permute-start.46
  356.0 34.5 %collective-permute-start.27 = (bf16[512,768]{1,0:T(8,128)(2,1)}, bf16[512,768]{1,0:T(8,128)(2,1)}, u32[]{:S(2)}, u32[]{:S(2)}) collective-permute-start(bf16[512,768]{1,0:T(8,128)(2,1)} %get-tuple-element.139), channel_id=1, source_target_pairs={{2,0},{4,2},{6,4},{8,6},{10,8},{12,10},{14,12},{3,1},{5,3},{7,5},{... | collective-permute-start | bytes 2359304 | tf_op jit(solution)/shard_map/ppermute | solution.py:443
  367.2 56.1 %collective-permute-start.34 = (bf16[512,768]{1,0:T(8,128)(2,1)}, bf16[512,768]{1,0:T(8,128)(2,1)}, u32[]{:S(2)}, u32[]{:S(2)}) collective-permute-start(bf16[512,768]{1,0:T(8,128)(2,1)} %get-tuple-element.155), channel_id=1, source_target_pairs={{2,0},{4,2},{6,4},{8,6},{10,8},{12,10},{14,12},{3,1},{5,3},{7,5},{... | collective-permute-start | bytes 2359304 | tf_op jit(solution)/shard_map/ppermute | solution.py:443
  389.8 80.2 %collective-permute-start.53 = (bf16[2,4,48,1536]{3,2,1,0:T(8,128)(2,1)}, bf16[2,4,48,1536]{3,2,1,0:T(8,128)(2,1)}, u32[]{:S(2)}, u32[]{:S(2)}) collective-permute-start(bf16[2,4,48,1536]{3,2,1,0:T(8,128)(2,1)} %bitcast.206), channel_id=1, source_target_pairs={{0,1},{1,0},{2,3},{3,2},{4,5},{5,4},{6,7},{7,6},{8,9},{9,8},{10,11... | collective-permute-start | bytes 3538952 | tf_op jit(solution)/shard_map/ppermute | solution.py:433
  394.5 34.2 %collective-permute-start.28 = (bf16[512,768]{1,0:T(8,128)(2,1)}, bf16[512,768]{1,0:T(8,128)(2,1)}, u32[]{:S(2)}, u32[]{:S(2)}) collective-permute-start(bf16[512,768]{1,0:T(8,128)(2,1)} %get-tuple-element.141), channel_id=1, source_target_pairs={{2,0},{4,2},{6,4},{8,6},{10,8},{12,10},{14,12},{3,1},{5,3},{7,5},{... | collective-permute-start | bytes 2359304 | tf_op jit(solution)/shard_map/ppermute | solution.py:443
  422.0 53.1 %collective-permute-start.48 = (bf16[2,4,48,1536]{3,2,1,0:T(8,128)(2,1)}, bf16[2,4,48,1536]{3,2,1,0:T(8,128)(2,1)}, u32[]{:S(2)}, u32[]{:S(2)}) collective-permute-start(bf16[2,4,48,1536]{3,2,1,0:T(8,128)(2,1)} %bitcast.207), channel_id=1, source_target_pairs={{0,1},{1,0},{2,3},{3,2},{4,5},{5,4},{6,7},{7,6},{8,9},{9,8},{10,11... | collective-permute-start | bytes 3538952 | tf_op jit(solution)/shard_map/ppermute | solution.py:433
  427.4 15.5 %collective-permute-start.35 = (bf16[512,768]{1,0:T(8,128)(2,1)}, bf16[512,768]{1,0:T(8,128)(2,1)}, u32[]{:S(2)}, u32[]{:S(2)}) collective-permute-start(bf16[512,768]{1,0:T(8,128)(2,1)} %get-tuple-element.157), channel_id=1, source_target_pairs={{2,0},{4,2},{6,4},{8,6},{10,8},{12,10},{14,12},{3,1},{5,3},{7,5},{... | collective-permute-start | bytes 2359304 | tf_op jit(solution)/shard_map/ppermute | solution.py:443
  441.3 67.2 %collective-permute-start.29 = (bf16[512,768]{1,0:T(8,128)(2,1)S(1)}, bf16[512,768]{1,0:T(8,128)(2,1)}, u32[]{:S(2)}, u32[]{:S(2)}) collective-permute-start(bf16[512,768]{1,0:T(8,128)(2,1)S(1)} %add_convert_fusion.1.own_ref), channel_id=1, source_target_pairs={{0,1},{1,0},{2,3},{3,2},{4,5},{5,4},{6,7},{7,6},{8,9},{9,8},{10,11... | collective-permute-start | bytes 2359304 | tf_op jit(solution)/shard_map/ppermute | solution.py:433
  455.9 55.0 %collective-permute-start.36 = (bf16[512,768]{1,0:T(8,128)(2,1)S(1)}, bf16[512,768]{1,0:T(8,128)(2,1)S(1)}, u32[]{:S(2)}, u32[]{:S(2)}) collective-permute-start(bf16[512,768]{1,0:T(8,128)(2,1)S(1)} %add_convert_fusion.own_ref), channel_id=1, source_target_pairs={{0,1},{1,0},{2,3},{3,2},{4,5},{5,4},{6,7},{7,6},{8,9},{9,8},{10,11... | collective-permute-start | bytes 2359304 | tf_op jit(solution)/shard_map/ppermute | solution.py:433
  460.6 113.6 %collective-permute-start.38 = (bf16[2,4,48,1152]{3,2,1,0:T(8,128)(2,1)}, bf16[2,4,48,1152]{3,2,1,0:T(8,128)(2,1)}, u32[]{:S(2)}, u32[]{:S(2)}) collective-permute-start(bf16[2,4,48,1152]{3,2,1,0:T(8,128)(2,1)} %dynamic-slice_bitcast_fusion.2), channel_id=1, source_target_pairs={{0,2},{2,0},{4,6},{6,4},{8,10},{10,8},{12,14},{14,12},{1,3},{3,1},... | collective-permute-start | bytes 2654216 | tf_op jit(solution)/shard_map/ppermute | solution.py:438
  471.9 17.0 %collective-permute-start.54 = (bf16[4,48,1536]{2,1,0:T(8,128)(2,1)S(1)}, bf16[4,48,1536]{2,1,0:T(8,128)(2,1)S(1)}, u32[]{:S(2)}, u32[]{:S(2)}) collective-permute-start(bf16[4,48,1536]{2,1,0:T(8,128)(2,1)S(1)} %dynamic-slice_bitcast_fusion.3), channel_id=1, source_target_pairs={{0,16},{16,0},{1,17},{17,1},{2,18},{18,2},{3,19},{19,3},{4,20},{20... | collective-permute-start | bytes 1769480 | tf_op jit(solution)/shard_map/ppermute | solution.py:433
  476.8 24.7 %collective-permute-start.49 = (bf16[4,48,1536]{2,1,0:T(8,128)(2,1)S(1)}, bf16[4,48,1536]{2,1,0:T(8,128)(2,1)S(1)}, u32[]{:S(2)}, u32[]{:S(2)}) collective-permute-start(bf16[4,48,1536]{2,1,0:T(8,128)(2,1)S(1)} %dynamic-slice_bitcast_fusion.4), channel_id=1, source_target_pairs={{0,16},{16,0},{1,17},{17,1},{2,18},{18,2},{3,19},{19,3},{4,20},{20... | collective-permute-start | bytes 1769480 | tf_op jit(solution)/shard_map/ppermute | solution.py:433
  489.8 87.7 %collective-permute-start.55 = (bf16[2,48,1536]{2,1,0:T(8,128)(2,1)}, bf16[2,48,1536]{2,1,0:T(8,128)(2,1)}, u32[]{:S(2)}, u32[]{:S(2)}) collective-permute-start(bf16[2,48,1536]{2,1,0:T(8,128)(2,1)} %dynamic-slice_bitcast_fusion.11), channel_id=1, source_target_pairs={{0,8},{2,10},{4,12},{6,14},{8,0},{10,2},{12,4},{14,6},{1,9},{3,11}... | collective-permute-start | bytes 884744 | tf_op jit(solution)/shard_map/ppermute | solution.py:438
  502.4 76.2 %collective-permute-start.50 = (bf16[2,48,1536]{2,1,0:T(8,128)(2,1)}, bf16[2,48,1536]{2,1,0:T(8,128)(2,1)}, u32[]{:S(2)}, u32[]{:S(2)}) collective-permute-start(bf16[2,48,1536]{2,1,0:T(8,128)(2,1)} %dynamic-slice_bitcast_fusion.12), channel_id=1, source_target_pairs={{0,8},{2,10},{4,12},{6,14},{8,0},{10,2},{12,4},{14,6},{1,9},{3,11}... | collective-permute-start | bytes 884744 | tf_op jit(solution)/shard_map/ppermute | solution.py:438
  576.0 8.4 %collective-permute-start.39 = (bf16[4,48,1152]{2,1,0:T(8,128)(2,1)S(1)}, bf16[4,48,1152]{2,1,0:T(8,128)(2,1)S(1)}, u32[]{:S(2)}, u32[]{:S(2)}) collective-permute-start(bf16[4,48,1152]{2,1,0:T(8,128)(2,1)S(1)} %dynamic-slice_bitcast_fusion.6), channel_id=1, source_target_pairs={{0,16},{16,0},{1,17},{17,1},{2,18},{18,2},{3,19},{19,3},{4,20},{20... | collective-permute-start | bytes 1327112 | tf_op jit(solution)/shard_map/ppermute | solution.py:433
  578.5 6.1 %collective-permute-start.56 = (bf16[1,48,1536]{2,1,0:T(8,128)(2,1)S(1)}, bf16[1,48,1536]{2,1,0:T(8,128)(2,1)S(1)}, u32[]{:S(2)}, u32[]{:S(2)}) collective-permute-start(bf16[1,48,1536]{2,1,0:T(8,128)(2,1)S(1)} %constant_dynamic-slice_fusion.8), channel_id=1, source_target_pairs={{0,4},{2,6},{4,0},{6,2},{8,12},{10,14},{12,8},{14,10},{1,5},{3,7},... | collective-permute-start | bytes 442376 | tf_op jit(solution)/shard_map/ppermute | solution.py:438
  579.7 14.8 %collective-permute-start.51 = (bf16[1,48,1536]{2,1,0:T(8,128)(2,1)S(1)}, bf16[1,48,1536]{2,1,0:T(8,128)(2,1)S(1)}, u32[]{:S(2)}, u32[]{:S(2)}) collective-permute-start(bf16[1,48,1536]{2,1,0:T(8,128)(2,1)S(1)} %constant_dynamic-slice_fusion.10), channel_id=1, source_target_pairs={{0,4},{2,6},{4,0},{6,2},{8,12},{10,14},{12,8},{14,10},{1,5},{3,7},... | collective-permute-start | bytes 442376 | tf_op jit(solution)/shard_map/ppermute | solution.py:438
  584.5 8.6 %collective-permute-start.40 = (bf16[2,48,1152]{2,1,0:T(8,128)(2,1)S(1)}, bf16[2,48,1152]{2,1,0:T(8,128)(2,1)S(1)}, u32[]{:S(2)}, u32[]{:S(2)}) collective-permute-start(bf16[2,48,1152]{2,1,0:T(8,128)(2,1)S(1)} %dynamic-slice_bitcast_fusion.13), channel_id=1, source_target_pairs={{0,8},{2,10},{4,12},{6,14},{8,0},{10,2},{12,4},{14,6},{1,9},{3,11}... | collective-permute-start | bytes 663560 | tf_op jit(solution)/shard_map/ppermute | solution.py:438
  593.2 4.9 collective-permute-start.41
  (172 other events, 2141.9 us)

commit v2 on v1

--- a/solution.py
+++ b/solution.py
@@ -515,6 +515,19 @@
     return part.reshape(part.shape[-2:]).astype(F32)
 
 
+def total(value, fast, over_tp):
+    if not fast:
+        return lax.psum(value, ("shard", "ctx", "tp") if over_tp else ("shard", "ctx"))
+    if over_tp:
+        value = value + swap(value, "tp")
+    value = value + swap(value, "shard")
+    bit = 1
+    while bit < lax.axis_size("ctx"):
+        value = value + hop(value, bit)
+        bit *= 2
+    return value
+
+
 def per_device(
     tokens,
     cotangent,
@@ -635,9 +648,7 @@
     grad_up = scatter_rows(outer(f_all, dh_all), fast, s, z, c, t)
     grad_out = scatter_rows(outer(g1_all, o_all), fast, s, z, c, t).T
     hsum, dsum, fsum = (sum(mids[b][i] for b in range(seqs)) for i in (4, 5, 6))
-    mid_sums = lax.psum(
-        jnp.concatenate([hsum.reshape(-1), dsum.reshape(-1), fsum.reshape(-1)]), ("shard", "ctx", "tp")
-    )
+    mid_sums = total(jnp.concatenate([hsum.reshape(-1), dsum.reshape(-1), fsum.reshape(-1)]), fast, True)
     hsum = mid_sums[: hsum.size].reshape(hsum.shape)
     fsum = mid_sums[hsum.size + dsum.size :].reshape(fsum.shape)
     dsum = mid_sums[hsum.size : hsum.size + dsum.size].reshape(dsum.shape)
@@ -655,7 +666,7 @@
     grad_qkv = scatter_rows(outer(jnp.concatenate(acts), proj), fast, s, z, c)
     grad_qkv = grad_qkv.reshape(-1, 3, n).transpose(1, 0, 2)
     bias_sums = jnp.sum(proj.astype(F32), 0)
-    tail_sums = lax.psum(jnp.concatenate([in_sums.reshape(-1), bias_sums]), ("shard", "ctx"))
+    tail_sums = total(jnp.concatenate([in_sums.reshape(-1), bias_sums]), fast, False)
     in_sums = tail_sums[: 2 * width].reshape(2, width)
     bias_sums = tail_sums[2 * width :]
 

time: 610 us -> 553 us (0.907)
  blocking collectives: 99.6 us -> 0 us
  starting transfers between devices: 121 us -> 149 us
  waiting for transfers between devices: 61.5 us -> 82.7 us
    psum x2 -> x0, blocking collectives: 99.6 us -> none  [the longest x1 58.6 us: per_device(): lax.psum(jnp.concatenate([in_sums.reshape(-1), bias_sums]), ('shard', 'ct...]
    ppermute x16 -> x22, starting transfers between devices: 33.4 us -> 58.3 us  [hop(): return lax.ppermute(value, 'ctx', [(i, i ^ bit) for i in range(size)])]
    ppermute x16 -> x22, waiting for transfers between devices: 24.5 us -> 39.8 us  [hop(): return lax.ppermute(value, 'ctx', [(i, i ^ bit) for i in range(size)])]
    pallas_call x10, Pallas kernels: 37.7 us -> 30.1 us  [bwd_step(): pl.pallas_call(functools.partial(bwd_kernel, NT, w == 0, first, w == 0, h...]
    ppermute x25 -> x28, waiting for transfers between devices: 36.9 us -> 42.9 us  [swap(): return lax.ppermute(value, axis, [(0, 1), (1, 0)])]
    ppermute x25 -> x28, starting transfers between devices: 31.9 us -> 34.4 us  [swap(): return lax.ppermute(value, axis, [(0, 1), (1, 0)])]
    unnamed x370 -> x386, local copies, waits for them, and re-layouts: 45.2 us -> 46.5 us
  transfers between devices with their start and end apart: 57 -> 66, of which waited for: 10 -> 14; matrix products, arithmetic and copies ran while one was open for 25% -> 28% of each run, Pallas kernels for 17% -> 17%
where the time goes in v2:
time: 553 us; the launch traced here: 545 us
  starting transfers between devices  149 us (27%)
  local copies, waits for them, and re-layouts  116 us (21%)
  Pallas kernels  106 us (19%)
  waiting for transfers between devices  82.7 us (15%)
  other arithmetic  70.5 us (13%)
  matrix products  16.9 us (3%)
    ppermute x22, starting transfers between devices, hop(): return lax.ppermute(value, 'ctx', [(i, i ^ bit) for i in range(size)])  58.3 us
    ppermute x16, starting transfers between devices, shift(): lax.ppermute(value, 'ctx', [(i, i + by) for i in range(size) if 0 <= i +...  56.4 us
    unnamed x386, local copies, waits for them, and re-layouts  46.5 us
    ppermute x28, waiting for transfers between devices, swap(): return lax.ppermute(value, axis, [(0, 1), (1, 0)])  42.9 us
    pallas_call x10, Pallas kernels, fwd_step(): pl.pallas_call(functools.partial(fwd_kernel, w == 0, first, last, heads,...  40.9 us
    ppermute x22, waiting for transfers between devices, hop(): return lax.ppermute(value, 'ctx', [(i, i ^ bit) for i in range(size)])  39.8 us
    ppermute x28, starting transfers between devices, swap(): return lax.ppermute(value, axis, [(0, 1), (1, 0)])  34.4 us
    pallas_call x10, Pallas kernels, bwd_step(): pl.pallas_call(functools.partial(bwd_kernel, NT, w == 0, first, w == 0, h...  30.1 us
  transfers between devices with their start and end apart: 66, of which 14 were waited for; matrix products, arithmetic and copies ran while one was open for 28% of the time, Pallas kernels for 17%

profile of v2, /device:TPU:0, one launch (start us, length us, event | category | flops | bytes accessed | tf_op | source)
XLA Modules:
  0.0 545.1 jit_solution(12218652503574363269)
XLA Ops:
  2.6 2.2 convert_element_type.306
  7.1 2.9 collective-permute-start.9
  19.5 3.1 fusion.69
  32.4 3.7 copy-done.141
  36.3 12.7 %collective-permute-done.2 = bf16[6,384]{1,0:T(8,128)(2,1)S(1)} collective-permute-done((bf16[6,384]{1,0:T(8,128)(2,1)S(1)}, bf16[6,384]{1,0:T(8,128)(2,1)S(1)}, u32[]{:S(2)}, u32[]{:S(2)}) %collective-permute-start.2) | collective-permute-done | bytes 4640 | tf_op jit(solution)/shard_map/ppermute | solution.py:433
  52.3 2.6 qkv.2
  56.6 2.9 collective-permute-start.3
  59.6 2.6 qkv.3
  63.9 2.9 collective-permute-start.17
  70.7 6.8 %attn_fwd.10 = (f32[8,512]{1,0:T(8,128)S(1)}, f32[8,512]{1,0:T(8,128)S(1)}, f32[384,512]{1,0:T(8,128)S(1)}) custom-call(s32[4]{0:T(128)S(1)} %pad_add_fusion.4.lo_sm, bf16[384,512]{1,0:T(8,128)(2,1)S(1)} %get-tuple-element.96.qT_ref, bf16[512,768]{1,0:T(8,128)(2,1)} %get-tuple-element.97.kv_ref, s32[1,512]{1,0:T(1,128)S(1)} %get-tuple-element.277.lo_ref), custom_call_target="tpu_custom_call" | custom-call | flops 402653184 | bytes 3145728 | tf_op jit(solution)/shard_map/attn_fwd/pallas_call | solution.py:85
  77.5 6.6 %attn_fwd.15 = (f32[8,512]{1,0:T(8,128)S(1)}, f32[8,512]{1,0:T(8,128)S(1)}, f32[384,512]{1,0:T(8,128)S(1)}) custom-call(s32[4]{0:T(128)S(1)} %pad_add_fusion.9.lo_sm, bf16[384,512]{1,0:T(8,128)(2,1)S(1)} %get-tuple-element.113.qT_ref, bf16[512,768]{1,0:T(8,128)(2,1)} %get-tuple-element.114.kv_ref, s32[1,512]{1,0:T(1,128)S(1)} %get-tuple-element.286.lo_ref), custom_call_target="tpu_custom_call" | custom-call | flops 402653184 | bytes 3145728 | tf_op jit(solution)/shard_map/attn_fwd/pallas_call | solution.py:85
  84.4 2.3 collective-permute-start.4
  86.8 3.1 collective-permute-start.18
  89.9 2.5 bitcast_dynamic-update-slice_fusion.6
  95.0 9.2 %collective-permute-start.5 = (bf16[512,768]{1,0:T(8,128)(2,1)S(1)}, bf16[512,768]{1,0:T(8,128)(2,1)S(1)}, u32[]{:S(2)}, u32[]{:S(2)}) collective-permute-start(bf16[512,768]{1,0:T(8,128)(2,1)S(1)} %collective-permute-done.4.kv_ref), channel_id=1, source_target_pairs={{0,2},{2,4},{4,6},{6,8},{8,10},{10,12},{12,14},{1,3},{3,5},{5,7},{... | collective-permute-start | bytes 2359304 | tf_op jit(solution)/shard_map/ppermute | solution.py:443
  104.2 9.8 %collective-permute-start.19 = (bf16[512,768]{1,0:T(8,128)(2,1)S(1)}, bf16[512,768]{1,0:T(8,128)(2,1)S(1)}, u32[]{:S(2)}, u32[]{:S(2)}) collective-permute-start(bf16[512,768]{1,0:T(8,128)(2,1)S(1)} %collective-permute-done.18.kv_ref), channel_id=1, source_target_pairs={{0,2},{2,4},{4,6},{6,8},{8,10},{10,12},{12,14},{1,3},{3,5},{5,7},{... | collective-permute-start | bytes 2359304 | tf_op jit(solution)/shard_map/ppermute | solution.py:443
  115.2 8.3 %attn_fwd.17 = (f32[8,512]{1,0:T(8,128)S(1)}, f32[8,512]{1,0:T(8,128)S(1)}, f32[384,512]{1,0:T(8,128)S(1)}) custom-call(s32[4]{0:T(128)S(1)} %get-tuple-element.297.lo_sm, bf16[384,512]{1,0:T(8,128)(2,1)S(1)} %get-tuple-element.113.qT_ref, bf16[512,768]{1,0:T(8,128)(2,1)S(1)} %collective-permute-done.18.kv_ref, s32[1,512]{1,0:T(1,128)S(1)} %get-tuple-element.282.lo_ref, ...), custom_call_target="tpu_custom_call" | custom-call | flops 402653184 | bytes 3145728 | tf_op jit(solution)/shard_map/attn_fwd/pallas_call | solution.py:85
  125.3 2.5 bitcast_dynamic-update-slice_fusion.4
  132.1 8.1 %collective-permute-start.20 = (bf16[512,768]{1,0:T(8,128)(2,1)S(1)}, bf16[512,768]{1,0:T(8,128)(2,1)S(1)}, u32[]{:S(2)}, u32[]{:S(2)}) collective-permute-start(bf16[512,768]{1,0:T(8,128)(2,1)S(1)} %collective-permute-done.19.kv_ref), channel_id=1, source_target_pairs={{0,2},{2,4},{4,6},{6,8},{8,10},{10,12},{12,14},{1,3},{3,5},{5,7},{... | collective-permute-start | bytes 2359304 | tf_op jit(solution)/shard_map/ppermute | solution.py:443
  143.6 7.5 %attn_fwd.14 = (bf16[512,384]{1,0:T(8,128)(2,1)S(1)}, f32[384,512]{1,0:T(8,128)S(1)}, f32[8,512]{1,0:T(8,128)S(1)}, f32[1,512]{1,0:T(1,128)S(1)}) custom-call(s32[4]{0:T(128)S(1)} %pad_add_fusion.lo_sm, bf16[384,512]{1,0:T(8,128)(2,1)S(1)} %get-tuple-element.96.qT_ref, bf16[512,768]{1,0:T(8,128)(2,1)S(1)} %collective-permute-done.6.kv_ref, ...), custom_call_target="tpu_custom_call" | custom-call | flops 402653184 | bytes 3145728 | tf_op jit(solution)/shard_map/attn_fwd/pallas_call | solution.py:85
  153.9 5.9 %attn_fwd.19 = (bf16[512,384]{1,0:T(8,128)(2,1)S(1)}, f32[384,512]{1,0:T(8,128)S(1)}, f32[8,512]{1,0:T(8,128)S(1)}, f32[1,512]{1,0:T(1,128)S(1)}) custom-call(s32[4]{0:T(128)S(1)} %pad_add_fusion.5.lo_sm, bf16[384,512]{1,0:T(8,128)(2,1)S(1)} %get-tuple-element.113.qT_ref, bf16[512,768]{1,0:T(8,128)(2,1)S(1)} %collective-permute-done.20.kv_ref, ...), custom_call_target="tpu_custom_call" | custom-call | flops 402653184 | bytes 3145728 | tf_op jit(solution)/shard_map/attn_fwd/pallas_call | solution.py:85
  169.9 13.1 %ffn.2 = (bf16[256,768]{1,0:T(8,128)(2,1)}, bf16[256,768]{1,0:T(8,128)(2,1)S(1)}, bf16[256,768]{1,0:T(8,128)(2,1)S(1)}, bf16[256,768]{1,0:T(8,128)(2,1)S(1)}, bf...) custom-call(bf16[256,384]{1,0:T(8,128)(2,1)S(1)} %get-tuple-element., ...), custom_call_target="tpu_custom_call" | custom-call | flops 5435817984 | bytes 10616832 | tf_op jit(solution)/shard_map/ffn/pallas_call | solution.py:373
  187.6 13.0 %ffn.3 = (bf16[256,768]{1,0:T(8,128)(2,1)}, bf16[256,768]{1,0:T(8,128)(2,1)S(1)}, bf16[256,768]{1,0:T(8,128)(2,1)S(1)}, bf16[256,768]{1,0:T(8,128)(2,1)S(1)}, bf...) custom-call(bf16[256,384]{1,0:T(8,128)(2,1)S(1)} %get-tuple-element., ...), custom_call_target="tpu_custom_call" | custom-call | flops 5435817984 | bytes 10616832 | tf_op jit(solution)/shard_map/ffn/pallas_call | solution.py:373
  215.1 4.5 convolution_convert_fusion
  224.2 3.3 convolution_convert_fusion.1
  231.3 3.3 collective-permute-done.62
  246.6 2.3 copy.102
  254.5 2.1 attn_bwd.10
  258.4 11.5 %collective-permute-start.65 = (f32[13824]{0:T(1024)S(1)}, f32[13824]{0:T(1024)S(1)}, u32[]{:S(2)}, u32[]{:S(2)}) collective-permute-start(f32[13824]{0:T(1024)S(1)} %add.498), channel_id=1, source_target_pairs={{0,8},{2,10},{4,12},{6,14},{8,0},{10,2},{12,4},{14,6},{1,9},{3,11}... | collective-permute-start | bytes 165896 | tf_op jit(solution)/shard_map/ppermute | solution.py:438
  288.4 2.5 reshape.251
  290.9 2.4 constant_dynamic-slice_fusion.13
  298.1 5.1 collective-permute-done.43
  304.5 2.2 attn_bwd.11
  309.3 10.5 %collective-permute-start.45 = (bf16[2,48,384]{2,1,0:T(8,128)(2,1)S(1)}, bf16[2,48,384]{2,1,0:T(8,128)(2,1)S(1)}, u32[]{:S(2)}, u32[]{:S(2)}) collective-permute-start(bf16[2,48,384]{2,1,0:T(8,128)(2,1)S(1)} %dynamic-slice_bitcast_fusion.15), channel_id=1, source_target_pairs={{0,8},{2,10},{4,12},{6,14},{8,0},{10,2},{12,4},{14,6},{1,9},{3,11}... | collective-permute-start | bytes 221192 | tf_op jit(solution)/shard_map/ppermute | solution.py:438
  322.6 9.5 %collective-permute-done.45 = bf16[2,48,384]{2,1,0:T(8,128)(2,1)S(1)} collective-permute-done((bf16[2,48,384]{2,1,0:T(8,128)(2,1)S(1)}, bf16[2,48,384]{2,1,0:T(8,128)(2,1)S(1)}, u32[]{:S(2)}, u32[]{:S(2)}) %collective-permute-start.45) | collective-permute-done | bytes 73760 | tf_op jit(solution)/shard_map/ppermute | solution.py:438
  333.2 3.3 collective-permute-done.46
  337.2 2.2 attn_bwd.12
  344.5 2.1 collective-permute-start.34
  346.5 4.8 fusion
  351.3 6.5 %reshape.257 = bf16[2,4,48,2,1536]{4,3,2,1,0:T(2,128)(2,1)} reshape(bf16[2,4,48,3072]{3,2,1,0:T(8,128)(2,1)} %fusion) | data formatting | bytes 4718592 | tf_op jit(solution)/shard_map/reshape | solution.py:507
  357.8 8.1 %constant_dynamic-slice_fusion.9 = (bf16[2,4,48,1,1536]{4,3,2,1,0:T(2,128)(2,1)S(1)}, f32[2,4,48,1,1536]{4,3,2,1,0:T(1,128)}) fusion(bf16[2,4,48,2,1536]{4,3,2,1,0:T(2,128)(2,1)} %reshape.257, s32[]{:T(128)S(6)} %select_n.320, s32[]{:T(128)S(6)} %select_n.319), kind=kLoop, calls=%fused_computation.156 | loop fusion | flops 589824 | bytes 5898248 | tf_op jit(solution)/shard_map/jit(dynamic_index_in_dim)/dynamic_slice | solution.py:489
  367.9 3.0 attn_bwd.13
  371.8 6.0 %collective-permute-start.28 = (bf16[512,768]{1,0:T(8,128)(2,1)}, bf16[512,768]{1,0:T(8,128)(2,1)}, u32[]{:S(2)}, u32[]{:S(2)}) collective-permute-start(bf16[512,768]{1,0:T(8,128)(2,1)} %get-tuple-element.141), channel_id=1, source_target_pairs={{2,0},{4,2},{6,4},{8,6},{10,8},{12,10},{14,12},{3,1},{5,3},{7,5},{... | collective-permute-start | bytes 2359304 | tf_op jit(solution)/shard_map/ppermute | solution.py:443
  377.9 4.9 fusion.1
  382.8 6.5 %reshape.254 = bf16[2,4,48,2,1536]{4,3,2,1,0:T(2,128)(2,1)} reshape(bf16[2,4,48,3072]{3,2,1,0:T(8,128)(2,1)} %fusion.1) | data formatting | bytes 4718592 | tf_op jit(solution)/shard_map/reshape | solution.py:507
  389.3 8.1 %constant_dynamic-slice_fusion.11 = (bf16[2,4,48,1,1536]{4,3,2,1,0:T(2,128)(2,1)S(1)}, f32[2,4,48,1,1536]{4,3,2,1,0:T(1,128)}) fusion(bf16[2,4,48,2,1536]{4,3,2,1,0:T(2,128)(2,1)} %reshape.254, s32[]{:T(128)S(6)} %select_n.320, s32[]{:T(128)S(6)} %select_n.319), kind=kLoop, calls=%fused_computation.158 | loop fusion | flops 589824 | bytes 5898248 | tf_op jit(solution)/shard_map/jit(dynamic_index_in_dim)/dynamic_slice | solution.py:489
  400.0 3.1 attn_bwd.18
  405.4 6.5 %attn_bwd.14 = (f32[384,512]{1,0:T(8,128)S(1)}, bf16[512,768]{1,0:T(8,128)(2,1)S(1)}) custom-call(s32[4]{0:T(128)S(1)} %copy-done.112, bf16[384,512]{1,0:T(8,128)(2,1)S(1)} %copy-done.19, bf16[512,384]{1,0:T(8,128)(2,1)S(1)} %copy-done.14, bf16[384,512]{1,0:T(8,128)(2,1)S(1)} %copy.99.doT_ref, bf16[512,384]{1,0:T(8,128)(2,1)S(1)} %get-tuple-element.248.do_ref, ...), custom_call_target="tpu_custom_call" | custom-call | flops 1006632960 | bytes 6291456 | tf_op jit(solution)/shard_map/attn_bwd/pallas_call | solution.py:175
  419.5 6.6 %attn_bwd.19 = (f32[384,512]{1,0:T(8,128)S(1)}, bf16[512,768]{1,0:T(8,128)(2,1)S(1)}) custom-call(s32[4]{0:T(128)S(1)} %copy-done.110, bf16[384,512]{1,0:T(8,128)(2,1)S(1)} %copy-done.9, bf16[512,384]{1,0:T(8,128)(2,1)S(1)} %copy-done.4, bf16[384,512]{1,0:T(8,128)(2,1)S(1)} %copy.107.doT_ref, bf16[512,384]{1,0:T(8,128)(2,1)S(1)} %get-tuple-element.250.do_ref, ...), custom_call_target="tpu_custom_call" | custom-call | flops 1006632960 | bytes 6291456 | tf_op jit(solution)/shard_map/attn_bwd/pallas_call | solution.py:175
  428.7 2.3 copy.108
  435.0 2.2 convolution_convert_fusion.2
  438.3 12.2 %collective-permute-start.38 = (bf16[2,4,48,1152]{3,2,1,0:T(8,128)(2,1)}, bf16[2,4,48,1152]{3,2,1,0:T(8,128)(2,1)}, u32[]{:S(2)}, u32[]{:S(2)}) collective-permute-start(bf16[2,4,48,1152]{3,2,1,0:T(8,128)(2,1)} %dynamic-slice_bitcast_fusion.2), channel_id=1, source_target_pairs={{0,2},{2,0},{4,6},{6,4},{8,10},{10,8},{12,14},{14,12},{1,3},{3,1},... | collective-permute-start | bytes 2654216 | tf_op jit(solution)/shard_map/ppermute | solution.py:438
  452.7 5.0 collective-permute-start.54
  460.4 11.1 %collective-permute-done.54 = bf16[4,48,1536]{2,1,0:T(8,128)(2,1)S(1)} collective-permute-done((bf16[4,48,1536]{2,1,0:T(8,128)(2,1)S(1)}, bf16[4,48,1536]{2,1,0:T(8,128)(2,1)S(1)}, u32[]{:S(2)}, u32[]{:S(2)}) %collective-permute-start.54) | collective-permute-done | bytes 589856 | tf_op jit(solution)/shard_map/ppermute | solution.py:433
  471.7 2.6 tail.2
  475.7 2.3 collective-permute-start.57
  478.1 7.2 %collective-permute-start.55 = (bf16[2,48,1536]{2,1,0:T(8,128)(2,1)S(1)}, bf16[2,48,1536]{2,1,0:T(8,128)(2,1)S(1)}, u32[]{:S(2)}, u32[]{:S(2)}) collective-permute-start(bf16[2,48,1536]{2,1,0:T(8,128)(2,1)S(1)} %dynamic-slice_bitcast_fusion.11), channel_id=1, source_target_pairs={{0,8},{2,10},{4,12},{6,14},{8,0},{10,2},{12,4},{14,6},{1,9},{3,11}... | collective-permute-start | bytes 884744 | tf_op jit(solution)/shard_map/ppermute | solution.py:438
  486.6 4.2 collective-permute-start.59
  490.9 6.6 %collective-permute-start.50 = (bf16[2,48,1536]{2,1,0:T(8,128)(2,1)S(1)}, bf16[2,48,1536]{2,1,0:T(8,128)(2,1)S(1)}, u32[]{:S(2)}, u32[]{:S(2)}) collective-permute-start(bf16[2,48,1536]{2,1,0:T(8,128)(2,1)S(1)} %dynamic-slice_bitcast_fusion.12), channel_id=1, source_target_pairs={{0,8},{2,10},{4,12},{6,14},{8,0},{10,2},{12,4},{14,6},{1,9},{3,11}... | collective-permute-start | bytes 884744 | tf_op jit(solution)/shard_map/ppermute | solution.py:438
  500.3 10.8 %collective-permute-done.60 = f32[2688]{0:T(1024)S(1)} collective-permute-done((f32[2688]{0:T(1024)S(1)}, f32[2688]{0:T(1024)S(1)}, u32[]{:S(2)}, u32[]{:S(2)}) %collective-permute-start.60) | collective-permute-done | bytes 10784 | tf_op jit(solution)/shard_map/ppermute | solution.py:438
  514.5 2.3 collective-permute-start.39
  519.2 7.9 %collective-permute-done.39 = bf16[4,48,1152]{2,1,0:T(8,128)(2,1)S(1)} collective-permute-done((bf16[4,48,1152]{2,1,0:T(8,128)(2,1)S(1)}, bf16[4,48,1152]{2,1,0:T(8,128)(2,1)S(1)}, u32[]{:S(2)}, u32[]{:S(2)}) %collective-permute-start.39) | collective-permute-done | bytes 442400 | tf_op jit(solution)/shard_map/ppermute | solution.py:433
  528.2 10.8 %collective-permute-done.40 = bf16[2,48,1152]{2,1,0:T(8,128)(2,1)S(1)} collective-permute-done((bf16[2,48,1152]{2,1,0:T(8,128)(2,1)S(1)}, bf16[2,48,1152]{2,1,0:T(8,128)(2,1)S(1)}, u32[]{:S(2)}, u32[]{:S(2)}) %collective-permute-start.40) | collective-permute-done | bytes 221216 | tf_op jit(solution)/shard_map/ppermute | solution.py:438
  539.9 4.2 collective-permute-done.41
  (694 shorter events, 184.2 us)
Async XLA Ops:
  7.1 61.1 %collective-permute-start.9 = (bf16[192,3456]{1,0:T(8,128)(2,1)}, bf16[192,3456]{1,0:T(8,128)(2,1)}, u32[]{:S(2)}, u32[]{:S(2)}) collective-permute-start(bf16[192,3456]{1,0:T(8,128)(2,1)} %constant_dynamic-slice_fusion.20), channel_id=1, source_target_pairs={{0,16},{16,0},{1,17},{17,1},{2,18},{18,2},{3,19},{19,3},{4,20},{20... | collective-permute-start | bytes 3981320 | tf_op jit(solution)/shard_map/ppermute | solution.py:433
  10.0 74.2 %collective-permute-start.11 = (bf16[192,3456]{1,0:T(8,128)(2,1)}, bf16[192,3456]{1,0:T(8,128)(2,1)}, u32[]{:S(2)}, u32[]{:S(2)}) collective-permute-start(bf16[192,3456]{1,0:T(8,128)(2,1)} %constant_dynamic-slice_fusion.20), channel_id=1, source_target_pairs={{0,1},{1,0},{2,3},{3,2},{4,5},{5,4},{6,7},{7,6},{8,9},{9,8},{10,11... | collective-permute-start | bytes 3981320 | tf_op jit(solution)/shard_map/ppermute | solution.py:433
  14.3 34.7 %collective-permute-start = (bf16[3,192,384]{2,1,0:T(8,128)(2,1)}, bf16[3,192,384]{2,1,0:T(8,128)(2,1)}, u32[]{:S(2)}, u32[]{:S(2)}) collective-permute-start(bf16[3,192,384]{2,1,0:T(8,128)(2,1)} %constant_dynamic-slice_fusion.24), channel_id=1, source_target_pairs={{0,16},{16,0},{1,17},{17,1},{2,18},{18,2},{3,19},{19,3},{4,20},{20... | collective-permute-start | bytes 1327112 | tf_op jit(solution)/shard_map/ppermute | solution.py:433
  14.9 34.1 %collective-permute-start.2 = (bf16[6,384]{1,0:T(8,128)(2,1)S(1)}, bf16[6,384]{1,0:T(8,128)(2,1)S(1)}, u32[]{:S(2)}, u32[]{:S(2)}) collective-permute-start(bf16[6,384]{1,0:T(8,128)(2,1)S(1)} %pad_maximum_fusion.11), channel_id=1, source_target_pairs={{0,16},{16,0},{1,17},{17,1},{2,18},{18,2},{3,19},{19,3},{4,20},{20... | collective-permute-start | bytes 13832 | tf_op jit(solution)/shard_map/ppermute | solution.py:433
  16.6 32.5 %collective-permute-start.15 = (f32[5376]{0:T(1024)S(1)}, f32[5376]{0:T(1024)S(1)}, u32[]{:S(2)}, u32[]{:S(2)}) collective-permute-start(f32[5376]{0:T(1024)S(1)} %constant_dynamic-update-slice_fusion.13), channel_id=1, source_target_pairs={{0,1},{1,0},{2,3},{3,2},{4,5},{5,4},{6,7},{7,6},{8,9},{9,8},{10,11... | collective-permute-start | bytes 64520 | tf_op jit(solution)/shard_map/ppermute | solution.py:433
  49.1 2.1 collective-permute-start.1
  56.6 27.7 %collective-permute-start.3 = (bf16[512,768]{1,0:T(8,128)(2,1)}, bf16[512,768]{1,0:T(8,128)(2,1)}, u32[]{:S(2)}, u32[]{:S(2)}) collective-permute-start(bf16[512,768]{1,0:T(8,128)(2,1)} %get-tuple-element.97.kv_ref), channel_id=1, source_target_pairs={{0,2},{2,4},{4,6},{6,8},{8,10},{10,12},{12,14},{1,3},{3,5},{5,7},{... | collective-permute-start | bytes 2359304 | tf_op jit(solution)/shard_map/ppermute | solution.py:443
  63.9 22.9 %collective-permute-start.17 = (bf16[512,768]{1,0:T(8,128)(2,1)}, bf16[512,768]{1,0:T(8,128)(2,1)S(1)}, u32[]{:S(2)}, u32[]{:S(2)}) collective-permute-start(bf16[512,768]{1,0:T(8,128)(2,1)} %get-tuple-element.114.kv_ref), channel_id=1, source_target_pairs={{0,2},{2,4},{4,6},{6,8},{8,10},{10,12},{12,14},{1,3},{3,5},{5,7},{... | collective-permute-start | bytes 2359304 | tf_op jit(solution)/shard_map/ppermute | solution.py:443
  68.2 55.9 %collective-permute-start.10 = (bf16[192,3456]{1,0:T(8,128)(2,1)}, bf16[192,3456]{1,0:T(8,128)(2,1)S(1)}, u32[]{:S(2)}, u32[]{:S(2)}) collective-permute-start(bf16[192,3456]{1,0:T(8,128)(2,1)} %collective-permute-done.9), channel_id=1, source_target_pairs={{0,2},{2,0},{4,6},{6,4},{8,10},{10,8},{12,14},{14,12},{1,3},{3,1},... | collective-permute-start | bytes 3981320 | tf_op jit(solution)/shard_map/ppermute | solution.py:438
  68.4 55.2 %collective-permute-start.13 = (bf16[192,3456]{1,0:T(8,128)(2,1)}, bf16[192,3456]{1,0:T(8,128)(2,1)S(1)}, u32[]{:S(2)}, u32[]{:S(2)}) collective-permute-start(bf16[192,3456]{1,0:T(8,128)(2,1)} %collective-permute-done.9), channel_id=1, source_target_pairs={{0,1},{1,0},{2,3},{3,2},{4,5},{5,4},{6,7},{7,6},{8,9},{9,8},{10,11... | collective-permute-start | bytes 3981320 | tf_op jit(solution)/shard_map/ppermute | solution.py:433
  84.2 43.6 %collective-permute-start.12 = (bf16[192,3456]{1,0:T(8,128)(2,1)}, bf16[192,3456]{1,0:T(8,128)(2,1)S(1)}, u32[]{:S(2)}, u32[]{:S(2)}) collective-permute-start(bf16[192,3456]{1,0:T(8,128)(2,1)} %collective-permute-done.11), channel_id=1, source_target_pairs={{0,2},{2,0},{4,6},{6,4},{8,10},{10,8},{12,14},{14,12},{1,3},{3,1},... | collective-permute-start | bytes 3981320 | tf_op jit(solution)/shard_map/ppermute | solution.py:438
  84.4 10.6 %collective-permute-start.4 = (bf16[512,768]{1,0:T(8,128)(2,1)}, bf16[512,768]{1,0:T(8,128)(2,1)S(1)}, u32[]{:S(2)}, u32[]{:S(2)}) collective-permute-start(bf16[512,768]{1,0:T(8,128)(2,1)} %collective-permute-done.3.kv_ref), channel_id=1, source_target_pairs={{0,2},{2,4},{4,6},{6,8},{8,10},{10,12},{12,14},{1,3},{3,5},{5,7},{... | collective-permute-start | bytes 2359304 | tf_op jit(solution)/shard_map/ppermute | solution.py:443
  86.8 17.4 %collective-permute-start.18 = (bf16[512,768]{1,0:T(8,128)(2,1)S(1)}, bf16[512,768]{1,0:T(8,128)(2,1)S(1)}, u32[]{:S(2)}, u32[]{:S(2)}) collective-permute-start(bf16[512,768]{1,0:T(8,128)(2,1)S(1)} %collective-permute-done.17.kv_ref), channel_id=1, source_target_pairs={{0,2},{2,4},{4,6},{6,8},{8,10},{10,12},{12,14},{1,3},{3,5},{5,7},{... | collective-permute-start | bytes 2359304 | tf_op jit(solution)/shard_map/ppermute | solution.py:443
  95.0 35.2 %collective-permute-start.5 = (bf16[512,768]{1,0:T(8,128)(2,1)S(1)}, bf16[512,768]{1,0:T(8,128)(2,1)S(1)}, u32[]{:S(2)}, u32[]{:S(2)}) collective-permute-start(bf16[512,768]{1,0:T(8,128)(2,1)S(1)} %collective-permute-done.4.kv_ref), channel_id=1, source_target_pairs={{0,2},{2,4},{4,6},{6,8},{8,10},{10,12},{12,14},{1,3},{3,5},{5,7},{... | collective-permute-start | bytes 2359304 | tf_op jit(solution)/shard_map/ppermute | solution.py:443
  104.2 28.0 %collective-permute-start.19 = (bf16[512,768]{1,0:T(8,128)(2,1)S(1)}, bf16[512,768]{1,0:T(8,128)(2,1)S(1)}, u32[]{:S(2)}, u32[]{:S(2)}) collective-permute-start(bf16[512,768]{1,0:T(8,128)(2,1)S(1)} %collective-permute-done.18.kv_ref), channel_id=1, source_target_pairs={{0,2},{2,4},{4,6},{6,8},{8,10},{10,12},{12,14},{1,3},{3,5},{5,7},{... | collective-permute-start | bytes 2359304 | tf_op jit(solution)/shard_map/ppermute | solution.py:443
  123.6 18.8 %collective-permute-start.14 = (bf16[192,3456]{1,0:T(8,128)(2,1)S(1)}, bf16[192,3456]{1,0:T(8,128)(2,1)S(1)}, u32[]{:S(2)}, u32[]{:S(2)}) collective-permute-start(bf16[192,3456]{1,0:T(8,128)(2,1)S(1)} %collective-permute-done.13), channel_id=1, source_target_pairs={{0,2},{2,0},{4,6},{6,4},{8,10},{10,8},{12,14},{14,12},{1,3},{3,1},... | collective-permute-start | bytes 3981320 | tf_op jit(solution)/shard_map/ppermute | solution.py:438
  130.2 13.4 %collective-permute-start.6 = (bf16[512,768]{1,0:T(8,128)(2,1)S(1)}, bf16[512,768]{1,0:T(8,128)(2,1)S(1)}, u32[]{:S(2)}, u32[]{:S(2)}) collective-permute-start(bf16[512,768]{1,0:T(8,128)(2,1)S(1)} %collective-permute-done.5.kv_ref), channel_id=1, source_target_pairs={{0,2},{2,4},{4,6},{6,8},{8,10},{10,12},{12,14},{1,3},{3,5},{5,7},{... | collective-permute-start | bytes 2359304 | tf_op jit(solution)/shard_map/ppermute | solution.py:443
  132.1 21.8 %collective-permute-start.20 = (bf16[512,768]{1,0:T(8,128)(2,1)S(1)}, bf16[512,768]{1,0:T(8,128)(2,1)S(1)}, u32[]{:S(2)}, u32[]{:S(2)}) collective-permute-start(bf16[512,768]{1,0:T(8,128)(2,1)S(1)} %collective-permute-done.19.kv_ref), channel_id=1, source_target_pairs={{0,2},{2,4},{4,6},{6,8},{8,10},{10,12},{12,14},{1,3},{3,5},{5,7},{... | collective-permute-start | bytes 2359304 | tf_op jit(solution)/shard_map/ppermute | solution.py:443
  151.1 14.7 %collective-permute-start.8 = (f32[256]{0:T(256)S(1)}, f32[256]{0:T(256)S(1)}, u32[]{:S(2)}, u32[]{:S(2)}) collective-permute-start(f32[256]{0:T(256)S(1)} %bitcast.259), channel_id=1, source_target_pairs={{0,1},{1,0},{2,3},{3,2},{4,5},{5,4},{6,7},{7,6},{8,9},{9,8},{10,11... | collective-permute-start | bytes 3080 | tf_op jit(solution)/shard_map/ppermute | solution.py:433
  152.4 13.7 %collective-permute-start.7 = (bf16[256,384]{1,0:T(8,128)(2,1)}, bf16[256,384]{1,0:T(8,128)(2,1)}, u32[]{:S(2)}, u32[]{:S(2)}) collective-permute-start(bf16[256,384]{1,0:T(8,128)(2,1)} %constant_dynamic-slice_fusion.23), channel_id=1, source_target_pairs={{0,1},{1,0},{2,3},{3,2},{4,5},{5,4},{6,7},{7,6},{8,9},{9,8},{10,11... | collective-permute-start | bytes 589832 | tf_op jit(solution)/shard_map/ppermute | solution.py:433
  160.7 5.2 collective-permute-start.22
  162.1 22.8 %collective-permute-start.21 = (bf16[256,384]{1,0:T(8,128)(2,1)}, bf16[256,384]{1,0:T(8,128)(2,1)}, u32[]{:S(2)}, u32[]{:S(2)}) collective-permute-start(bf16[256,384]{1,0:T(8,128)(2,1)} %constant_dynamic-slice_fusion.19), channel_id=1, source_target_pairs={{0,1},{1,0},{2,3},{3,2},{4,5},{5,4},{6,7},{7,6},{8,9},{9,8},{10,11... | collective-permute-start | bytes 589832 | tf_op jit(solution)/shard_map/ppermute | solution.py:433
  209.5 20.9 %collective-permute-start.61 = (f32[13824]{0:T(1024)}, f32[13824]{0:T(1024)S(1)}, u32[]{:S(2)}, u32[]{:S(2)}) collective-permute-start(f32[13824]{0:T(1024)} %constant_dynamic-update-slice_fusion.12), channel_id=1, source_target_pairs={{0,1},{1,0},{2,3},{3,2},{4,5},{5,4},{6,7},{7,6},{8,9},{9,8},{10,11... | collective-permute-start | bytes 165896 | tf_op jit(solution)/shard_map/ppermute | solution.py:433
  210.2 74.0 %collective-permute-start.30 = (bf16[256,768]{1,0:T(8,128)(2,1)}, bf16[256,768]{1,0:T(8,128)(2,1)}, u32[]{:S(2)}, u32[]{:S(2)}) collective-permute-start(bf16[256,768]{1,0:T(8,128)(2,1)} %copy-done.71), channel_id=1, source_target_pairs={{0,1},{1,0},{2,3},{3,2},{4,5},{5,4},{6,7},{7,6},{8,9},{9,8},{10,11... | collective-permute-start | bytes 1179656 | tf_op jit(solution)/shard_map/ppermute | solution.py:433
  211.5 24.6 %collective-permute-start.24 = (bf16[256,384]{1,0:T(8,128)(2,1)S(1)}, bf16[256,384]{1,0:T(8,128)(2,1)S(1)}, u32[]{:S(2)}, u32[]{:S(2)}) collective-permute-start(bf16[256,384]{1,0:T(8,128)(2,1)S(1)} %constant_dynamic-slice_fusion.16), channel_id=1, source_target_pairs={{0,1},{1,0},{2,3},{3,2},{4,5},{5,4},{6,7},{7,6},{8,9},{9,8},{10,11... | collective-permute-start | bytes 589832 | tf_op jit(solution)/shard_map/ppermute | solution.py:433
  212.3 83.2 %collective-permute-start.37 = (bf16[256,768]{1,0:T(8,128)(2,1)}, bf16[256,768]{1,0:T(8,128)(2,1)}, u32[]{:S(2)}, u32[]{:S(2)}) collective-permute-start(bf16[256,768]{1,0:T(8,128)(2,1)} %copy-done.68), channel_id=1, source_target_pairs={{0,1},{1,0},{2,3},{3,2},{4,5},{5,4},{6,7},{7,6},{8,9},{9,8},{10,11... | collective-permute-start | bytes 1179656 | tf_op jit(solution)/shard_map/ppermute | solution.py:433
  214.3 28.5 %collective-permute-start.31 = (bf16[256,384]{1,0:T(8,128)(2,1)}, bf16[256,384]{1,0:T(8,128)(2,1)}, u32[]{:S(2)}, u32[]{:S(2)}) collective-permute-start(bf16[256,384]{1,0:T(8,128)(2,1)} %constant_dynamic-slice_fusion.15), channel_id=1, source_target_pairs={{0,1},{1,0},{2,3},{3,2},{4,5},{5,4},{6,7},{7,6},{8,9},{9,8},{10,11... | collective-permute-start | bytes 589832 | tf_op jit(solution)/shard_map/ppermute | solution.py:433
  230.4 4.2 collective-permute-start.62
  235.9 110.6 %collective-permute-start.52 = (bf16[2,4,48,3072]{3,2,1,0:T(8,128)(2,1)}, bf16[2,4,48,3072]{3,2,1,0:T(8,128)(2,1)}, u32[]{:S(2)}, u32[]{:S(2)}) collective-permute-start(bf16[2,4,48,3072]{3,2,1,0:T(8,128)(2,1)} %dynamic-slice_bitcast_fusion), channel_id=1, source_target_pairs={{0,2},{2,0},{4,6},{6,4},{8,10},{10,8},{12,14},{14,12},{1,3},{3,1},... | collective-permute-start | bytes 7077896 | tf_op jit(solution)/shard_map/ppermute | solution.py:438
  236.1 42.2 %collective-permute-start.16 = (bf16[256,768]{1,0:T(8,128)(2,1)}, bf16[256,768]{1,0:T(8,128)(2,1)}, u32[]{:S(2)}, u32[]{:S(2)}) collective-permute-start(bf16[256,768]{1,0:T(8,128)(2,1)} %get-tuple-element.112), channel_id=1, source_target_pairs={{0,1},{1,0},{2,3},{3,2},{4,5},{5,4},{6,7},{7,6},{8,9},{9,8},{10,11... | collective-permute-start | bytes 1179656 | tf_op jit(solution)/shard_map/ppermute | solution.py:433
  242.9 14.7 %collective-permute-start.64 = (f32[13824]{0:T(1024)S(1)}, f32[13824]{0:T(1024)}, u32[]{:S(2)}, u32[]{:S(2)}) collective-permute-start(f32[13824]{0:T(1024)S(1)} %add.497), channel_id=1, source_target_pairs={{0,4},{2,6},{4,0},{6,2},{8,12},{10,14},{12,8},{14,10},{1,5},{3,7},... | collective-permute-start | bytes 165896 | tf_op jit(solution)/shard_map/ppermute | solution.py:438
  258.4 14.6 %collective-permute-start.65 = (f32[13824]{0:T(1024)S(1)}, f32[13824]{0:T(1024)S(1)}, u32[]{:S(2)}, u32[]{:S(2)}) collective-permute-start(f32[13824]{0:T(1024)S(1)} %add.498), channel_id=1, source_target_pairs={{0,8},{2,10},{4,12},{6,14},{8,0},{10,2},{12,4},{14,6},{1,9},{3,11}... | collective-permute-start | bytes 165896 | tf_op jit(solution)/shard_map/ppermute | solution.py:438
  272.9 8.2 %collective-permute-start.23 = (bf16[256,768]{1,0:T(8,128)(2,1)}, bf16[256,768]{1,0:T(8,128)(2,1)}, u32[]{:S(2)}, u32[]{:S(2)}) collective-permute-start(bf16[256,768]{1,0:T(8,128)(2,1)} %get-tuple-element.129), channel_id=1, source_target_pairs={{0,1},{1,0},{2,3},{3,2},{4,5},{5,4},{6,7},{7,6},{8,9},{9,8},{10,11... | collective-permute-start | bytes 1179656 | tf_op jit(solution)/shard_map/ppermute | solution.py:433
  278.3 99.6 %collective-permute-start.47 = (bf16[2,4,48,3072]{3,2,1,0:T(8,128)(2,1)}, bf16[2,4,48,3072]{3,2,1,0:T(8,128)(2,1)}, u32[]{:S(2)}, u32[]{:S(2)}) collective-permute-start(bf16[2,4,48,3072]{3,2,1,0:T(8,128)(2,1)} %dynamic-slice_bitcast_fusion.1), channel_id=1, source_target_pairs={{0,2},{2,0},{4,6},{6,4},{8,10},{10,8},{12,14},{14,12},{1,3},{3,1},... | collective-permute-start | bytes 7077896 | tf_op jit(solution)/shard_map/ppermute | solution.py:438
  281.1 6.4 %collective-permute-start.42 = (bf16[2,4,48,768]{3,2,1,0:T(8,128)(2,1)}, bf16[2,4,48,768]{3,2,1,0:T(8,128)(2,1)S(1)}, u32[]{:S(2)}, u32[]{:S(2)}) collective-permute-start(bf16[2,4,48,768]{3,2,1,0:T(8,128)(2,1)} %dynamic-slice_bitcast_fusion.5), channel_id=1, source_target_pairs={{0,2},{2,0},{4,6},{6,4},{8,10},{10,8},{12,14},{14,12},{1,3},{3,1},... | collective-permute-start | bytes 1769480 | tf_op jit(solution)/shard_map/ppermute | solution.py:438
  284.2 20.2 %collective-permute-start.25 = (bf16[512,768]{1,0:T(8,128)(2,1)}, bf16[512,768]{1,0:T(8,128)(2,1)}, u32[]{:S(2)}, u32[]{:S(2)}) collective-permute-start(bf16[512,768]{1,0:T(8,128)(2,1)} %get-tuple-element.135), channel_id=1, source_target_pairs={{2,0},{4,2},{6,4},{8,6},{10,8},{12,10},{14,12},{3,1},{5,3},{7,5},{... | collective-permute-start | bytes 2359304 | tf_op jit(solution)/shard_map/ppermute | solution.py:443
  293.5 9.8 %collective-permute-start.43 = (bf16[2,4,48,384]{3,2,1,0:T(8,128)(2,1)S(1)}, bf16[2,4,48,384]{3,2,1,0:T(8,128)(2,1)S(1)}, u32[]{:S(2)}, u32[]{:S(2)}) collective-permute-start(bf16[2,4,48,384]{3,2,1,0:T(8,128)(2,1)S(1)} %bitcast.254), channel_id=1, source_target_pairs={{0,1},{1,0},{2,3},{3,2},{4,5},{5,4},{6,7},{7,6},{8,9},{9,8},{10,11... | collective-permute-start | bytes 884744 | tf_op jit(solution)/shard_map/ppermute | solution.py:433
  295.6 24.3 %collective-permute-start.32 = (bf16[512,768]{1,0:T(8,128)(2,1)S(1)}, bf16[512,768]{1,0:T(8,128)(2,1)S(1)}, u32[]{:S(2)}, u32[]{:S(2)}) collective-permute-start(bf16[512,768]{1,0:T(8,128)(2,1)S(1)} %copy-done.122), channel_id=1, source_target_pairs={{2,0},{4,2},{6,4},{8,6},{10,8},{12,10},{14,12},{3,1},{5,3},{7,5},{... | collective-permute-start | bytes 2359304 | tf_op jit(solution)/shard_map/ppermute | solution.py:443
  303.3 5.9 %collective-permute-start.44 = (bf16[4,48,384]{2,1,0:T(8,128)(2,1)S(1)}, bf16[4,48,384]{2,1,0:T(8,128)(2,1)S(1)}, u32[]{:S(2)}, u32[]{:S(2)}) collective-permute-start(bf16[4,48,384]{2,1,0:T(8,128)(2,1)S(1)} %dynamic-slice_bitcast_fusion.14), channel_id=1, source_target_pairs={{0,16},{16,0},{1,17},{17,1},{2,18},{18,2},{3,19},{19,3},{4,20},{20... | collective-permute-start | bytes 442376 | tf_op jit(solution)/shard_map/ppermute | solution.py:433
  306.7 30.4 %collective-permute-start.26 = (bf16[512,768]{1,0:T(8,128)(2,1)S(1)}, bf16[512,768]{1,0:T(8,128)(2,1)S(1)}, u32[]{:S(2)}, u32[]{:S(2)}) collective-permute-start(bf16[512,768]{1,0:T(8,128)(2,1)S(1)} %get-tuple-element.137), channel_id=1, source_target_pairs={{2,0},{4,2},{6,4},{8,6},{10,8},{12,10},{14,12},{3,1},{5,3},{7,5},{... | collective-permute-start | bytes 2359304 | tf_op jit(solution)/shard_map/ppermute | solution.py:443
  309.3 22.8 %collective-permute-start.45 = (bf16[2,48,384]{2,1,0:T(8,128)(2,1)S(1)}, bf16[2,48,384]{2,1,0:T(8,128)(2,1)S(1)}, u32[]{:S(2)}, u32[]{:S(2)}) collective-permute-start(bf16[2,48,384]{2,1,0:T(8,128)(2,1)S(1)} %dynamic-slice_bitcast_fusion.15), channel_id=1, source_target_pairs={{0,8},{2,10},{4,12},{6,14},{8,0},{10,2},{12,4},{14,6},{1,9},{3,11}... | collective-permute-start | bytes 221192 | tf_op jit(solution)/shard_map/ppermute | solution.py:438
  321.2 20.4 %collective-permute-start.33 = (bf16[512,768]{1,0:T(8,128)(2,1)S(1)}, bf16[512,768]{1,0:T(8,128)(2,1)S(1)}, u32[]{:S(2)}, u32[]{:S(2)}) collective-permute-start(bf16[512,768]{1,0:T(8,128)(2,1)S(1)} %get-tuple-element.153), channel_id=1, source_target_pairs={{2,0},{4,2},{6,4},{8,6},{10,8},{12,10},{14,12},{3,1},{5,3},{7,5},{... | collective-permute-start | bytes 2359304 | tf_op jit(solution)/shard_map/ppermute | solution.py:443
  332.2 4.3 collective-permute-start.46
  340.3 27.6 %collective-permute-start.27 = (bf16[512,768]{1,0:T(8,128)(2,1)}, bf16[512,768]{1,0:T(8,128)(2,1)}, u32[]{:S(2)}, u32[]{:S(2)}) collective-permute-start(bf16[512,768]{1,0:T(8,128)(2,1)} %get-tuple-element.139), channel_id=1, source_target_pairs={{2,0},{4,2},{6,4},{8,6},{10,8},{12,10},{14,12},{3,1},{5,3},{7,5},{... | collective-permute-start | bytes 2359304 | tf_op jit(solution)/shard_map/ppermute | solution.py:443
  344.5 55.5 %collective-permute-start.34 = (bf16[512,768]{1,0:T(8,128)(2,1)}, bf16[512,768]{1,0:T(8,128)(2,1)}, u32[]{:S(2)}, u32[]{:S(2)}) collective-permute-start(bf16[512,768]{1,0:T(8,128)(2,1)} %get-tuple-element.155), channel_id=1, source_target_pairs={{2,0},{4,2},{6,4},{8,6},{10,8},{12,10},{14,12},{3,1},{5,3},{7,5},{... | collective-permute-start | bytes 2359304 | tf_op jit(solution)/shard_map/ppermute | solution.py:443
  367.2 83.7 %collective-permute-start.53 = (bf16[2,4,48,1536]{3,2,1,0:T(8,128)(2,1)}, bf16[2,4,48,1536]{3,2,1,0:T(8,128)(2,1)}, u32[]{:S(2)}, u32[]{:S(2)}) collective-permute-start(bf16[2,4,48,1536]{3,2,1,0:T(8,128)(2,1)} %bitcast.206), channel_id=1, source_target_pairs={{0,1},{1,0},{2,3},{3,2},{4,5},{5,4},{6,7},{7,6},{8,9},{9,8},{10,11... | collective-permute-start | bytes 3538952 | tf_op jit(solution)/shard_map/ppermute | solution.py:433
  371.8 33.5 %collective-permute-start.28 = (bf16[512,768]{1,0:T(8,128)(2,1)}, bf16[512,768]{1,0:T(8,128)(2,1)}, u32[]{:S(2)}, u32[]{:S(2)}) collective-permute-start(bf16[512,768]{1,0:T(8,128)(2,1)} %get-tuple-element.141), channel_id=1, source_target_pairs={{2,0},{4,2},{6,4},{8,6},{10,8},{12,10},{14,12},{3,1},{5,3},{7,5},{... | collective-permute-start | bytes 2359304 | tf_op jit(solution)/shard_map/ppermute | solution.py:443
  398.6 59.1 %collective-permute-start.48 = (bf16[2,4,48,1536]{3,2,1,0:T(8,128)(2,1)}, bf16[2,4,48,1536]{3,2,1,0:T(8,128)(2,1)}, u32[]{:S(2)}, u32[]{:S(2)}) collective-permute-start(bf16[2,4,48,1536]{3,2,1,0:T(8,128)(2,1)} %bitcast.207), channel_id=1, source_target_pairs={{0,1},{1,0},{2,3},{3,2},{4,5},{5,4},{6,7},{7,6},{8,9},{9,8},{10,11... | collective-permute-start | bytes 3538952 | tf_op jit(solution)/shard_map/ppermute | solution.py:433
  404.1 15.4 %collective-permute-start.35 = (bf16[512,768]{1,0:T(8,128)(2,1)}, bf16[512,768]{1,0:T(8,128)(2,1)}, u32[]{:S(2)}, u32[]{:S(2)}) collective-permute-start(bf16[512,768]{1,0:T(8,128)(2,1)} %get-tuple-element.157), channel_id=1, source_target_pairs={{2,0},{4,2},{6,4},{8,6},{10,8},{12,10},{14,12},{3,1},{5,3},{7,5},{... | collective-permute-start | bytes 2359304 | tf_op jit(solution)/shard_map/ppermute | solution.py:443
  417.9 53.8 %collective-permute-start.29 = (bf16[512,768]{1,0:T(8,128)(2,1)S(1)}, bf16[512,768]{1,0:T(8,128)(2,1)}, u32[]{:S(2)}, u32[]{:S(2)}) collective-permute-start(bf16[512,768]{1,0:T(8,128)(2,1)S(1)} %add_convert_fusion.1.own_ref), channel_id=1, source_target_pairs={{0,1},{1,0},{2,3},{3,2},{4,5},{5,4},{6,7},{7,6},{8,9},{9,8},{10,11... | collective-permute-start | bytes 2359304 | tf_op jit(solution)/shard_map/ppermute | solution.py:433
  433.5 40.8 %collective-permute-start.36 = (bf16[512,768]{1,0:T(8,128)(2,1)S(1)}, bf16[512,768]{1,0:T(8,128)(2,1)S(1)}, u32[]{:S(2)}, u32[]{:S(2)}) collective-permute-start(bf16[512,768]{1,0:T(8,128)(2,1)S(1)} %add_convert_fusion.own_ref), channel_id=1, source_target_pairs={{0,1},{1,0},{2,3},{3,2},{4,5},{5,4},{6,7},{7,6},{8,9},{9,8},{10,11... | collective-permute-start | bytes 2359304 | tf_op jit(solution)/shard_map/ppermute | solution.py:433
  438.3 74.8 %collective-permute-start.38 = (bf16[2,4,48,1152]{3,2,1,0:T(8,128)(2,1)}, bf16[2,4,48,1152]{3,2,1,0:T(8,128)(2,1)}, u32[]{:S(2)}, u32[]{:S(2)}) collective-permute-start(bf16[2,4,48,1152]{3,2,1,0:T(8,128)(2,1)} %dynamic-slice_bitcast_fusion.2), channel_id=1, source_target_pairs={{0,2},{2,0},{4,6},{6,4},{8,10},{10,8},{12,14},{14,12},{1,3},{3,1},... | collective-permute-start | bytes 2654216 | tf_op jit(solution)/shard_map/ppermute | solution.py:438
  452.7 18.8 %collective-permute-start.54 = (bf16[4,48,1536]{2,1,0:T(8,128)(2,1)S(1)}, bf16[4,48,1536]{2,1,0:T(8,128)(2,1)S(1)}, u32[]{:S(2)}, u32[]{:S(2)}) collective-permute-start(bf16[4,48,1536]{2,1,0:T(8,128)(2,1)S(1)} %dynamic-slice_bitcast_fusion.3), channel_id=1, source_target_pairs={{0,16},{16,0},{1,17},{17,1},{2,18},{18,2},{3,19},{19,3},{4,20},{20... | collective-permute-start | bytes 1769480 | tf_op jit(solution)/shard_map/ppermute | solution.py:433
  460.3 25.0 %collective-permute-start.49 = (bf16[4,48,1536]{2,1,0:T(8,128)(2,1)}, bf16[4,48,1536]{2,1,0:T(8,128)(2,1)}, u32[]{:S(2)}, u32[]{:S(2)}) collective-permute-start(bf16[4,48,1536]{2,1,0:T(8,128)(2,1)} %dynamic-slice_bitcast_fusion.4), channel_id=1, source_target_pairs={{0,16},{16,0},{1,17},{17,1},{2,18},{18,2},{3,19},{19,3},{4,20},{20... | collective-permute-start | bytes 1769480 | tf_op jit(solution)/shard_map/ppermute | solution.py:433
  475.7 9.5 %collective-permute-start.57 = (f32[2688]{0:T(1024)S(1)}, f32[2688]{0:T(1024)S(1)}, u32[]{:S(2)}, u32[]{:S(2)}) collective-permute-start(f32[2688]{0:T(1024)S(1)} %pad_maximum_fusion.8), channel_id=1, source_target_pairs={{0,16},{16,0},{1,17},{17,1},{2,18},{18,2},{3,19},{19,3},{4,20},{20... | collective-permute-start | bytes 32264 | tf_op jit(solution)/shard_map/ppermute | solution.py:433
  478.1 38.8 %collective-permute-start.55 = (bf16[2,48,1536]{2,1,0:T(8,128)(2,1)S(1)}, bf16[2,48,1536]{2,1,0:T(8,128)(2,1)S(1)}, u32[]{:S(2)}, u32[]{:S(2)}) collective-permute-start(bf16[2,48,1536]{2,1,0:T(8,128)(2,1)S(1)} %dynamic-slice_bitcast_fusion.11), channel_id=1, source_target_pairs={{0,8},{2,10},{4,12},{6,14},{8,0},{10,2},{12,4},{14,6},{1,9},{3,11}... | collective-permute-start | bytes 884744 | tf_op jit(solution)/shard_map/ppermute | solution.py:438
  486.6 10.9 %collective-permute-start.59 = (f32[2688]{0:T(1024)S(1)}, f32[2688]{0:T(1024)S(1)}, u32[]{:S(2)}, u32[]{:S(2)}) collective-permute-start(f32[2688]{0:T(1024)S(1)} %add.489), channel_id=1, source_target_pairs={{0,4},{2,6},{4,0},{6,2},{8,12},{10,14},{12,8},{14,10},{1,5},{3,7},... | collective-permute-start | bytes 32264 | tf_op jit(solution)/shard_map/ppermute | solution.py:438
  490.9 26.2 %collective-permute-start.50 = (bf16[2,48,1536]{2,1,0:T(8,128)(2,1)S(1)}, bf16[2,48,1536]{2,1,0:T(8,128)(2,1)S(1)}, u32[]{:S(2)}, u32[]{:S(2)}) collective-permute-start(bf16[2,48,1536]{2,1,0:T(8,128)(2,1)S(1)} %dynamic-slice_bitcast_fusion.12), channel_id=1, source_target_pairs={{0,8},{2,10},{4,12},{6,14},{8,0},{10,2},{12,4},{14,6},{1,9},{3,11}... | collective-permute-start | bytes 884744 | tf_op jit(solution)/shard_map/ppermute | solution.py:438
  497.5 13.7 %collective-permute-start.60 = (f32[2688]{0:T(1024)S(1)}, f32[2688]{0:T(1024)S(1)}, u32[]{:S(2)}, u32[]{:S(2)}) collective-permute-start(f32[2688]{0:T(1024)S(1)} %add.490), channel_id=1, source_target_pairs={{0,8},{2,10},{4,12},{6,14},{8,0},{10,2},{12,4},{14,6},{1,9},{3,11}... | collective-permute-start | bytes 32264 | tf_op jit(solution)/shard_map/ppermute | solution.py:438
  514.5 12.6 %collective-permute-start.39 = (bf16[4,48,1152]{2,1,0:T(8,128)(2,1)S(1)}, bf16[4,48,1152]{2,1,0:T(8,128)(2,1)S(1)}, u32[]{:S(2)}, u32[]{:S(2)}) collective-permute-start(bf16[4,48,1152]{2,1,0:T(8,128)(2,1)S(1)} %dynamic-slice_bitcast_fusion.6), channel_id=1, source_target_pairs={{0,16},{16,0},{1,17},{17,1},{2,18},{18,2},{3,19},{19,3},{4,20},{20... | collective-permute-start | bytes 1327112 | tf_op jit(solution)/shard_map/ppermute | solution.py:433
  517.0 10.4 %collective-permute-start.56 = (bf16[1,48,1536]{2,1,0:T(8,128)(2,1)S(1)}, bf16[1,48,1536]{2,1,0:T(8,128)(2,1)S(1)}, u32[]{:S(2)}, u32[]{:S(2)}) collective-permute-start(bf16[1,48,1536]{2,1,0:T(8,128)(2,1)S(1)} %constant_dynamic-slice_fusion.8), channel_id=1, source_target_pairs={{0,4},{2,6},{4,0},{6,2},{8,12},{10,14},{12,8},{14,10},{1,5},{3,7},... | collective-permute-start | bytes 442376 | tf_op jit(solution)/shard_map/ppermute | solution.py:438
  517.2 21.9 %collective-permute-start.51 = (bf16[1,48,1536]{2,1,0:T(8,128)(2,1)S(1)}, bf16[1,48,1536]{2,1,0:T(8,128)(2,1)S(1)}, u32[]{:S(2)}, u32[]{:S(2)}) collective-permute-start(bf16[1,48,1536]{2,1,0:T(8,128)(2,1)S(1)} %constant_dynamic-slice_fusion.10), channel_id=1, source_target_pairs={{0,4},{2,6},{4,0},{6,2},{8,12},{10,14},{12,8},{14,10},{1,5},{3,7},... | collective-permute-start | bytes 442376 | tf_op jit(solution)/shard_map/ppermute | solution.py:438
  527.3 11.6 %collective-permute-start.40 = (bf16[2,48,1152]{2,1,0:T(8,128)(2,1)S(1)}, bf16[2,48,1152]{2,1,0:T(8,128)(2,1)S(1)}, u32[]{:S(2)}, u32[]{:S(2)}) collective-permute-start(bf16[2,48,1152]{2,1,0:T(8,128)(2,1)S(1)} %dynamic-slice_bitcast_fusion.13), channel_id=1, source_target_pairs={{0,8},{2,10},{4,12},{6,14},{8,0},{10,2},{12,4},{14,6},{1,9},{3,11}... | collective-permute-start | bytes 663560 | tf_op jit(solution)/shard_map/ppermute | solution.py:438
  539.0 5.0 collective-permute-start.41
  (188 other events, 3117.5 us)
